TPU v7x, 32 devices: a whole 2x2x4 slice. The times are simulated.
32 devices in a mesh: dp: 4 (over y, x), fsdp: 8 (over z, core).
Axes of the slice: x: 2, y: 2, z: 4, core: 2. Of those that a mesh axis runs over, the one named last changes fastest.
Arguments:
- tokens_in: bfloat16 [32, 256, 1024], P(('dp', 'fsdp')), may hold values from -6 to 6
- cotangent: bfloat16 [32, 256, 1024], P(('dp', 'fsdp')), may hold values from -6 to 6
- lengths: int32 [32], P(('dp', 'fsdp')), may hold values from 128 to 256
- qkv_master: float32 [1024, 3072], P('fsdp'), may hold values from -0.5625 to 0.5625
- out_master: float32 [1024, 1024], P('fsdp'), may hold values from -2.25 to 2.25
- up_master: float32 [1024, 4096], P('fsdp'), may hold values from -0.5625 to 0.5625
- down_master: float32 [4096, 1024], P('fsdp'), may hold values from -0.28125 to 0.28125
- small_master: float32 [13312], P('fsdp'), may hold values from -0.8 to 1.4
- qkv_first: float32 [1024, 3072], P('fsdp'), may hold values from -814.58701 to 814.58701
- out_first: float32 [1024, 1024], P('fsdp'), may hold values from -407.29351 to 407.29351
- up_first: float32 [1024, 4096], P('fsdp'), may hold values from -814.58701 to 814.58701
- down_first: float32 [4096, 1024], P('fsdp'), may hold values from -814.58701 to 814.58701
- small_first: float32 [13312], P('fsdp'), may hold values from -1629.17402 to 1629.17402
- qkv_second: float32 [1024, 3072], P('fsdp'), may hold values from 2048 to 8192
- out_second: float32 [1024, 1024], P('fsdp'), may hold values from 512 to 2048
- up_second: float32 [1024, 4096], P('fsdp'), may hold values from 2048 to 8192
- down_second: float32 [4096, 1024], P('fsdp'), may hold values from 2048 to 8192
- small_second: float32 [13312], P('fsdp'), may hold values from 8192 to 32768
Outputs:
- output: bfloat16 [32, 256, 1024], P(('dp', 'fsdp'))
- input_grad: bfloat16 [32, 256, 1024], P(('dp', 'fsdp'))
- qkv_new: float32 [1024, 3072], P('fsdp')
- out_new: float32 [1024, 1024], P('fsdp')
- up_new: float32 [1024, 4096], P('fsdp')
- down_new: float32 [4096, 1024], P('fsdp')
- small_new: float32 [13312], P('fsdp')
- qkv_first_new: float32 [1024, 3072], P('fsdp')
- out_first_new: float32 [1024, 1024], P('fsdp')
- up_first_new: float32 [1024, 4096], P('fsdp')
- down_first_new: float32 [4096, 1024], P('fsdp')
- small_first_new: float32 [13312], P('fsdp')
- qkv_second_new: float32 [1024, 3072], P('fsdp')
- out_second_new: float32 [1024, 1024], P('fsdp')
- up_second_new: float32 [1024, 4096], P('fsdp')
- down_second_new: float32 [4096, 1024], P('fsdp')
- small_second_new: float32 [13312], P('fsdp')
- lamb_norms: float32 [2, 5], replicated
All inputs are finite; a program needn't handle non-finite values.
Results may differ from a plain program's by a relative error of at most 0.012.
The roundings to bfloat16 on the way count: a program that leaves them out, or rounds other values in their place, can miss the bound.
Values may be sent and summed in bfloat16 or wider, within the bound.
A program may use at most 256 MiB of HBM per device.

v0:
```python
import math

import jax
import jax.numpy as jnp
from jax import lax
from jax.sharding import PartitionSpec as P

D = 1024
HEADS = 16
HD = 64
FF = 4096
ROT = 16


NORM_EPSILON = 1e-05
ADAM_EPSILON = 1e-06
ROPE_BASE = 10000.0
RATE = 0.5
DECAY = 0.01
BETA_ONE = 0.5
BETA_TWO = 0.5


def shortened(shard):

    def short(part):
        return part.astype(jnp.bfloat16) if part.dtype == jnp.float32 else part

    return jax.tree.map(short, shard)


def split_small(small_vector):
    bounds = [0, D, 2 * D, 3 * D, 4 * D, 7 * D, 8 * D, 8 * D + FF, 9 * D + FF]
    return [small_vector[bounds[number] : bounds[number + 1]] for number in range(8)]


def normalize(values):
    average = jnp.mean(values, axis=-1, keepdims=True)
    centred = values - average
    variance = jnp.mean(centred * centred, axis=-1, keepdims=True)
    inverse = lax.rsqrt(variance + NORM_EPSILON)
    return (centred * inverse, inverse)


def norm_back(grad_out, normalized, inverse, gain_vec):
    scaled = grad_out * gain_vec
    return inverse * (
        scaled
        - jnp.mean(scaled, axis=-1, keepdims=True)
        - normalized * jnp.mean(scaled * normalized, axis=-1, keepdims=True)
    )


def rotary_tables(length):
    half_dims = ROT // 2
    position = jnp.arange(length, dtype=jnp.float32)[:, None]
    number = jnp.arange(half_dims, dtype=jnp.float32)[None, :]
    angle = position * jnp.exp(number * (-2.0 * math.log(ROPE_BASE) / ROT))
    return (jnp.cos(angle)[:, None, :], jnp.sin(angle)[:, None, :])


def rotate(heads_in, cosine_table, sine_table):
    half_dims = ROT // 2
    first_half = heads_in[..., :half_dims]
    second_half = heads_in[..., half_dims:ROT]
    return jnp.concatenate(
        [
            first_half * cosine_table - second_half * sine_table,
            second_half * cosine_table + first_half * sine_table,
            heads_in[..., ROT:],
        ],
        axis=-1,
    )


def rotate_back(grads_in, cosine_table, sine_table):
    half_dims = ROT // 2
    first_half = grads_in[..., :half_dims]
    second_half = grads_in[..., half_dims:ROT]
    return jnp.concatenate(
        [
            first_half * cosine_table + second_half * sine_table,
            second_half * cosine_table - first_half * sine_table,
            grads_in[..., ROT:],
        ],
        axis=-1,
    )


def gelu_slope(values):
    return 0.5 * (1.0 + lax.erf(values * 2.0 ** (-0.5))) + values * jnp.exp(
        -0.5 * values * values
    ) * (2.0 * math.pi) ** (-0.5)


def against(left, right):
    return lax.dot_general(
        left, right, (((1,), (1,)), ((), ())), preferred_element_type=jnp.float32
    )


def outer_sum(columns, right):
    return lax.dot_general(
        columns, right, (((0,), (0,)), ((), ())), preferred_element_type=jnp.float32
    )


def score_block(query_heads, key_heads, allowed):
    scores = jnp.einsum(
        "qhd,khd->hqk", query_heads, key_heads, preferred_element_type=jnp.float32
    ) * HD ** (-0.5)
    return jnp.where(allowed[None], scores, -1e30)


def row_terms(left, right):
    return outer_sum(left, right)


def local_squares(arrays):
    return jnp.stack([jnp.sum(array_in * array_in) for array_in in arrays])


def local(
    tokens_in,
    cotangent,
    lengths,
    qkv_master,
    out_master,
    up_master,
    down_master,
    small_master,
    qkv_first,
    out_first,
    up_first,
    down_first,
    small_first,
    qkv_second,
    out_second,
    up_second,
    down_second,
    small_second,
):
    masters = (qkv_master, out_master, up_master, down_master, small_master)
    firsts = (qkv_first, out_first, up_first, down_first, small_first)
    seconds = (qkv_second, out_second, up_second, down_second, small_second)
    rounded = tuple((master.astype(jnp.bfloat16) for master in masters))
    gathered = jax.tree.map(
        lambda part, own: part.astype(own.dtype),
        lax.all_gather(shortened(rounded), "fsdp", axis=0, tiled=True),
        rounded,
    )
    qkv_weight, out_weight, up_weight, down_weight, small_low = gathered
    gain_one, shift_one, gain_two, shift_two, qkv_bias, out_bias, up_bias, down_bias = split_small(
        small_low.astype(jnp.float32)
    )
    inputs = tokens_in[0].astype(jnp.float32)
    length = inputs.shape[0]
    length_now = lengths[0]
    position = jnp.arange(length)
    live_rows = (position < length_now).astype(jnp.float32)[:, None]
    allowed = (position[None, :] <= position[:, None]) & (position[None, :] < length_now)
    unit_rows, inverse_rows = normalize(inputs)
    normed_one = (unit_rows * gain_one + shift_one).astype(jnp.bfloat16)
    normed_two = (unit_rows * gain_two + shift_two).astype(jnp.bfloat16)
    projected = jnp.dot(normed_one, qkv_weight, preferred_element_type=jnp.float32) + qkv_bias
    projected = projected.reshape(length, 3, HEADS, HD)
    cosine_table, sine_table = rotary_tables(length)
    query_heads = rotate(projected[:, 0], cosine_table, sine_table).astype(jnp.bfloat16)
    key_heads = rotate(projected[:, 1], cosine_table, sine_table).astype(jnp.bfloat16)
    value_heads = projected[:, 2].astype(jnp.bfloat16)
    scores = score_block(query_heads, key_heads, allowed)
    row_top = jnp.max(scores, axis=-1, keepdims=True)
    log_total = row_top + jnp.log(jnp.sum(jnp.exp(scores - row_top), axis=-1, keepdims=True))
    attend_low = jnp.exp(scores - log_total).astype(jnp.bfloat16)
    mixed_heads = jnp.einsum(
        "hqk,khd->qhd", attend_low, value_heads, preferred_element_type=jnp.float32
    )
    mixed_heads = mixed_heads.reshape(length, D).astype(jnp.bfloat16)
    attention = jnp.dot(mixed_heads, out_weight, preferred_element_type=jnp.float32) + out_bias
    hidden = jnp.dot(normed_two, up_weight, preferred_element_type=jnp.float32) + up_bias
    activated = jax.nn.gelu(hidden, approximate=False).astype(jnp.bfloat16)
    feed_out = jnp.dot(activated, down_weight, preferred_element_type=jnp.float32) + down_bias
    output = ((inputs + attention + feed_out) * live_rows).astype(jnp.bfloat16)
    back_weights = jax.tree.map(
        lambda part, own: part.astype(own.dtype),
        lax.all_gather(shortened(rounded), "fsdp", axis=0, tiled=True),
        rounded,
    )
    qkv_back, out_back, up_back, down_back, small_back = back_weights
    back_gains = split_small(small_back.astype(jnp.float32))
    back_rows = cotangent[0].astype(jnp.float32) * live_rows
    back_narrow = back_rows.astype(jnp.bfloat16)
    d_hidden = (against(back_narrow, down_back) * gelu_slope(hidden)).astype(jnp.bfloat16)
    d_mixed = against(back_narrow, out_back).astype(jnp.bfloat16).reshape(length, HEADS, HD)
    scores_again = score_block(query_heads, key_heads, allowed)
    attend_full = jnp.exp(scores_again - log_total)
    d_attend = jnp.einsum("qhd,khd->hqk", d_mixed, value_heads, preferred_element_type=jnp.float32)
    row_inner = jnp.sum(attend_full * d_attend, axis=-1, keepdims=True)
    d_scores = (attend_full * (d_attend - row_inner)).astype(jnp.bfloat16)
    d_queries = jnp.einsum(
        "hqk,khd->qhd", d_scores, key_heads, preferred_element_type=jnp.float32
    ) * HD ** (-0.5)
    d_keys = jnp.einsum(
        "hqk,qhd->khd", d_scores, query_heads, preferred_element_type=jnp.float32
    ) * HD ** (-0.5)
    d_values = jnp.einsum(
        "hqk,qhd->khd",
        attend_full.astype(jnp.bfloat16),
        d_mixed,
        preferred_element_type=jnp.float32,
    )
    d_projected = jnp.stack(
        [
            rotate_back(d_queries, cosine_table, sine_table),
            rotate_back(d_keys, cosine_table, sine_table),
            d_values,
        ],
        axis=1,
    )
    d_projected = d_projected.reshape(length, 3 * D).astype(jnp.bfloat16)
    d_normed_one = against(d_projected, qkv_back)
    d_normed_two = against(d_hidden, up_back)
    input_grad = (
        back_rows
        + norm_back(d_normed_one, unit_rows, inverse_rows, back_gains[0])
        + norm_back(d_normed_two, unit_rows, inverse_rows, back_gains[2])
    )
    back_total = jnp.sum(back_rows, axis=0)
    small_grad = jnp.concatenate(
        [
            jnp.sum(d_normed_one * unit_rows, axis=0),
            jnp.sum(d_normed_one, axis=0),
            jnp.sum(d_normed_two * unit_rows, axis=0),
            jnp.sum(d_normed_two, axis=0),
            jnp.sum(d_projected, axis=0, dtype=jnp.float32),
            back_total,
            jnp.sum(d_hidden, axis=0, dtype=jnp.float32),
            back_total,
        ]
    )
    qkv_grad = lax.psum_scatter(
        row_terms(normed_one, d_projected), "fsdp", scatter_dimension=0, tiled=True
    )
    out_grad = lax.psum_scatter(
        row_terms(mixed_heads, back_narrow), "fsdp", scatter_dimension=0, tiled=True
    )
    up_grad = lax.psum_scatter(
        row_terms(normed_two, d_hidden), "fsdp", scatter_dimension=0, tiled=True
    )
    down_grad = lax.psum_scatter(
        row_terms(activated, back_narrow), "fsdp", scatter_dimension=0, tiled=True
    )
    small_part = lax.psum_scatter(small_grad, "fsdp", scatter_dimension=0, tiled=True)
    reduced = lax.psum((qkv_grad, out_grad, up_grad, down_grad, small_part), "dp")
    updates = []
    first_news = []
    second_news = []
    for first_old, second_old, master, grad_sum in zip(firsts, seconds, masters, reduced):
        first_new = BETA_ONE * first_old + (1.0 - BETA_ONE) * grad_sum
        second_new = BETA_TWO * second_old + (1.0 - BETA_TWO) * grad_sum * grad_sum
        updates.append(first_new / (jnp.sqrt(second_new) + ADAM_EPSILON) + DECAY * master)
        first_news.append(first_new)
        second_news.append(second_new)
    weight_squares, update_squares = lax.psum(
        (local_squares(masters), local_squares(updates)), "fsdp"
    )
    weight_norms = jnp.sqrt(weight_squares)
    update_norms = jnp.sqrt(update_squares)
    new_masters = [
        masters[number] - RATE * (weight_norms[number] / update_norms[number]) * updates[number]
        for number in range(5)
    ]
    lamb_norms = jnp.stack([weight_norms, update_norms])
    return (
        output[None],
        input_grad.astype(jnp.bfloat16)[None],
        new_masters[0],
        new_masters[1],
        new_masters[2],
        new_masters[3],
        new_masters[4],
        first_news[0],
        first_news[1],
        first_news[2],
        first_news[3],
        first_news[4],
        second_news[0],
        second_news[1],
        second_news[2],
        second_news[3],
        second_news[4],
        lamb_norms,
    )


def solution(mesh):
    in_specs = (
        P(("dp", "fsdp"), None, None),
        P(("dp", "fsdp"), None, None),
        P(("dp", "fsdp")),
        P("fsdp", None),
        P("fsdp", None),
        P("fsdp", None),
        P("fsdp", None),
        P("fsdp"),
        P("fsdp", None),
        P("fsdp", None),
        P("fsdp", None),
        P("fsdp", None),
        P("fsdp"),
        P("fsdp", None),
        P("fsdp", None),
        P("fsdp", None),
        P("fsdp", None),
        P("fsdp"),
    )
    out_specs = (
        P(("dp", "fsdp"), None, None),
        P(("dp", "fsdp"), None, None),
        P("fsdp", None),
        P("fsdp", None),
        P("fsdp", None),
        P("fsdp", None),
        P("fsdp"),
        P("fsdp", None),
        P("fsdp", None),
        P("fsdp", None),
        P("fsdp", None),
        P("fsdp"),
        P("fsdp", None),
        P("fsdp", None),
        P("fsdp", None),
        P("fsdp", None),
        P("fsdp"),
        P(),
    )
    return jax.shard_map(local, mesh=mesh, in_specs=in_specs, out_specs=out_specs, check_vma=False)
```

profile of v0, /device:TPU:0, one launch (start us, length us, event | category | flops | bytes accessed | tf_op | source)
XLA Modules:
  0.0 1006.2 jit_solution(3019584502417805161)
XLA Ops:
  16.4 15.8 %all-gather = bf16[8,1,1664]{2,1,0:T(2,128)(2,1)S(1)} all-gather(bf16[1,1,1664]{2,1,0:T(2,128)(2,1)S(1)} %reshape.234), channel_id=1, replica_groups=mesh['dp'=4,'fsdp'=8] {'fsdp'}, dimensions={0}, use_global_device_ids=true | all-gather | bytes 29952 | tf_op jit(solution)/shard_map/all_gather | solution.py:149
  34.2 43.7 %all-gather.6.cloned.1.call-done = bf16[1024,3072]{1,0:T(8,128)(2,1)} async-done(((bf16[128,3072]{1,0:T(8,128)(2,1)}), bf16[1024,3072]{1,0:T(8,128)(2,1)}) %all-gather.6.cloned.1.call-update) | async-done | bytes 6291472 | tf_op jit(solution)/shard_map/all_gather | solution.py:149
  78.0 6.3 convolution_add_fusion.1
  99.0 8.9 all-gather.8.cloned.1.call-done
  113.1 4.2 multiply_reduce_fusion
  123.3 6.5 fusion.65
  130.9 60.8 %all-gather.10.cloned.1.call-done = bf16[1024,4096]{1,0:T(8,128)(2,1)} async-done(((bf16[128,4096]{1,0:T(8,128)(2,1)}), bf16[1024,4096]{1,0:T(8,128)(2,1)}) %all-gather.10.cloned.1.call-update) | async-done | bytes 8388624 | tf_op jit(solution)/shard_map/all_gather | solution.py:149
  191.7 15.3 %fusion.3 = (bf16[256,4096]{1,0:T(8,128)(2,1)}, f32[256,4096]{1,0:T(8,128)}) fusion(f32[4096]{0:T(1024)S(1)} %slice.152, bf16[1024,4096]{1,0:T(8,128)(2,1)} %all-gather.10.cloned.1.call-done, bf16[1,256,1024]{2,1,0:T(8,128)(2,1)S(1)} %copy-done.2, f32[1024]{0:T(1024)S(1)} %get-tuple-element.72, f32[1024]{0:T(1024)S(1)} %get-tuple-element.73, ...), kind=kOutput, calls=%fused_computation.7 | convolution fusion | flops 2218262528 | bytes 15230976 | tf_op jit(solution)/shard_map/dot_general | solution.py:180
  207.0 67.3 %all-gather.12.cloned.1.call-done = bf16[4096,1024]{1,0:T(8,128)(2,1)} async-done(((bf16[512,1024]{1,0:T(8,128)(2,1)}), bf16[4096,1024]{1,0:T(8,128)(2,1)}) %all-gather.12.cloned.1.call-update) | async-done | bytes 8388624 | tf_op jit(solution)/shard_map/all_gather | solution.py:149
  274.4 6.6 convert_reduce_fusion
  282.3 8.3 fusion.103
  291.1 9.8 fusion.99
  301.0 24.0 %reduce-scatter.7.cloned.1.call-done = f32[128,1024]{1,0:T(8,128)} async-done(((f32[1024,1024]{1,0:T(8,128)}), f32[128,1024]{1,0:T(8,128)}) %reduce-scatter.7.cloned.1.call-update) | async-done | bytes 524304 | tf_op jit(solution)/shard_map/reduce_scatter | solution.py:244
  325.1 129.6 %reduce-scatter.5.cloned.1.call-done = f32[128,3072]{1,0:T(8,128)} async-done(((f32[1024,3072]{1,0:T(8,128)}), f32[128,3072]{1,0:T(8,128)}) %reduce-scatter.5.cloned.1.call-update) | async-done | bytes 1572880 | tf_op jit(solution)/shard_map/reduce_scatter | solution.py:241
  454.6 169.0 %reduce-scatter.9.cloned.1.call-done = f32[128,4096]{1,0:T(8,128)} async-done(((f32[1024,4096]{1,0:T(8,128)}), f32[128,4096]{1,0:T(8,128)}) %reduce-scatter.9.cloned.1.call-update) | async-done | bytes 2097168 | tf_op jit(solution)/shard_map/reduce_scatter | solution.py:247
  623.6 169.0 %reduce-scatter.11.cloned.1.call-done = f32[512,1024]{1,0:T(8,128)} async-done(((f32[4096,1024]{1,0:T(8,128)}), f32[512,1024]{1,0:T(8,128)}) %reduce-scatter.11.cloned.1.call-update) | async-done | bytes 2097168 | tf_op jit(solution)/shard_map/reduce_scatter | solution.py:250
  793.9 6.5 fusion.114
  800.5 5.3 fusion.51
  807.5 26.4 %all-reduce = f32[13312]{0:T(1024)S(1)} all-reduce(f32[13312]{0:T(1024)S(1)} %constant_dynamic-update-slice_fusion), channel_id=6, replica_groups=mesh['dp'=4,'fsdp'=8] {'fsdp'}, use_global_device_ids=true, to_apply=%region_34.35.clone | all-reduce | flops 13312 | bytes 106496
  833.9 10.4 %psum.54 = f32[1664]{0:T(1024)S(1)} all-reduce(f32[1664]{0:T(1024)S(1)} %dynamic-slice.1), channel_id=1, replica_groups=mesh['dp'=4,'fsdp'=8] {'dp'}, use_global_device_ids=true, to_apply=%region_35.36 | all-reduce | flops 1664 | bytes 13312 | tf_op jit(solution)/shard_map/psum | solution.py:254
  845.1 7.4 convolution_add_fusion.3
  852.5 82.0 %all-reduce.5.cloned.1.call-done = (f32[128,3072]{1,0:T(8,128)}, f32[128,1024]{1,0:T(8,128)}, f32[128,4096]{1,0:T(8,128)}, f32[512,1024]{1,0:T(8,128)}) async-done(((f32[128,3072]{1,0:T(8,128)}, f32[128,1024]{1,0:T(8,128)}, f32[128,4096]{1,0:T(8,128)}, f32[512,1024]{1,0:T(8,128)}), (f32[128,3072]{1,0:T(8,128)}, f32[128,1024]{1,0:T(8,128)}, f32[128,4096]{1,0:T(8,128)}, ...) | async-done | bytes 6291472 | tf_op jit(solution)/shard_map/psum | solution.py:254
  937.9 5.4 multiply_reduce_fusion.5
  961.6 16.4 %all-reduce.1 = (f32[5]{0:T(128)S(1)}, f32[5]{0:T(128)S(1)}) all-reduce(f32[5]{0:T(128)S(1)} %stack.66, f32[5]{0:T(128)S(1)} %stack.72), channel_id=1, replica_groups=mesh['dp'=4,'fsdp'=8] {'fsdp'}, use_global_device_ids=true, to_apply=%region_14.15 | all-reduce | flops 10 | bytes 80 | tf_op jit(solution)/shard_map/psum | solution.py:264
  (211 shorter events, 78.5 us)
Async XLA Ops:
  7.2 70.8 %all-gather.6.cloned.1.call-start = ((), (), s32[]{:S(2)}) async-start(), calls=%async_computation.4 | async-start | bytes 7077888 | tf_op jit(solution)/shard_map/all_gather | solution.py:149
  9.8 98.1 %all-gather.8.cloned.1.call-start = ((), (), s32[]{:S(2)}) async-start(), calls=%async_computation.5 | async-start | bytes 2359296 | tf_op jit(solution)/shard_map/all_gather | solution.py:149
  11.7 21.2 %copy-start.2 = (bf16[1,256,1024]{2,1,0:T(8,128)(2,1)S(1)}, bf16[1,256,1024]{2,1,0:T(8,128)(2,1)}, u32[]{:S(2)}) copy-start(bf16[1,256,1024]{2,1,0:T(8,128)(2,1)} %param.18) | copy-start | bytes 1572868
  11.7 180.0 %all-gather.10.cloned.1.call-start = ((), (), s32[]{:S(2)}) async-start(), calls=%async_computation.6 | async-start | bytes 9437184 | tf_op jit(solution)/shard_map/all_gather | solution.py:149
  14.5 259.9 %all-gather.12.cloned.1.call-start = ((), (), s32[]{:S(2)}) async-start(), calls=%async_computation.7 | async-start | bytes 9437184 | tf_op jit(solution)/shard_map/all_gather | solution.py:149
  15.7 309.3 %reduce-scatter.7.cloned.1.call-start = ((), (), s32[]{:S(2)}) async-start(), calls=%async_computation.9 | async-start | bytes 4718592 | tf_op jit(solution)/shard_map/reduce_scatter | solution.py:244
  33.1 51.2 %copy-start.47 = (f32[256]{0:T(256)}, f32[256]{0:T(256)S(1)}, u32[]{:S(2)}) copy-start(f32[256]{0:T(256)S(1)} %broadcast_multiply_fusion.4) | copy-start | bytes 3076
  33.4 50.9 %copy-start.51 = (f32[256]{0:T(256)}, f32[256]{0:T(256)S(1)}, u32[]{:S(2)}) copy-start(f32[256]{0:T(256)S(1)} %add_rsqrt_fusion) | copy-start | bytes 3076
  33.5 56.2 %copy-start.41 = (f32[256,8]{0,1:T(8,128)}, f32[256,8]{0,1:T(8,128)S(1)}, u32[]{:S(2)}) copy-start(f32[256,8]{0,1:T(8,128)S(1)} %get-tuple-element.94) | copy-start | bytes 24580
  33.5 56.2 %copy-start.43 = (f32[256,8]{0,1:T(8,128)}, f32[256,8]{0,1:T(8,128)S(1)}, u32[]{:S(2)}) copy-start(f32[256,8]{0,1:T(8,128)S(1)} %get-tuple-element.95) | copy-start | bytes 24580
  34.2 55.6 %copy-start.27 = (pred[256,256]{0,1:T(8,128)(4,1)}, pred[256,256]{0,1:T(8,128)(4,1)S(1)}, u32[]{:S(2)}) copy-start(pred[256,256]{0,1:T(8,128)(4,1)S(1)} %fusion.81) | copy-start | bytes 196612
  98.7 355.9 %reduce-scatter.5.cloned.1.call-start = ((), (), s32[]{:S(2)}) async-start(), calls=%async_computation.8 | async-start | bytes 14155776 | tf_op jit(solution)/shard_map/reduce_scatter | solution.py:241
  129.8 493.8 %reduce-scatter.9.cloned.1.call-start = ((), (), s32[]{:S(2)}) async-start(), calls=%async_computation.10 | async-start | bytes 18874368 | tf_op jit(solution)/shard_map/reduce_scatter | solution.py:247
  191.7 82.7 %copy-start.50 = (f32[256]{0:T(256)S(1)}, f32[256]{0:T(256)}, u32[]{:S(2)}) copy-start(f32[256]{0:T(256)} %fusion.98) | copy-start | bytes 3076
  290.6 502.0 %reduce-scatter.11.cloned.1.call-start = ((), (), s32[]{:S(2)}) async-start(), calls=%async_computation.11 | async-start | bytes 18874368 | tf_op jit(solution)/shard_map/reduce_scatter | solution.py:250
  301.0 491.7 %copy-start.59 = (u32[32]{0:T(128)S(1)}, u32[32]{0:T(128)}, u32[]{:S(2)}) copy-start(u32[32]{0:T(128)} %constant.113) | copy-start | bytes 388
  301.0 633.5 %all-reduce.5.cloned.1.call-start = ((), (), s32[]{:S(2)}) async-start(), calls=%async_computation.12 | async-start | bytes 12582912 | tf_op jit(solution)/shard_map/psum | solution.py:254
  800.4 43.9 %copy-start.46 = (f32[1664]{0:T(1024)S(1)}, f32[1664]{0:T(1024)}, u32[]{:S(2)}) copy-start(f32[1664]{0:T(1024)} %param.25) | copy-start | bytes 19972
  800.5 43.9 %copy-start.56 = (f32[1664]{0:T(1024)S(1)}, f32[1664]{0:T(1024)}, u32[]{:S(2)}) copy-start(f32[1664]{0:T(1024)} %param.35) | copy-start | bytes 19972
  800.5 43.9 %copy-start.57 = (f32[1664]{0:T(1024)S(1)}, f32[1664]{0:T(1024)}, u32[]{:S(2)}) copy-start(f32[1664]{0:T(1024)} %param.30) | copy-start | bytes 19972
  800.5 44.6 %copy-start.58 = (f32[1024]{0:T(1024)S(1)}, f32[1024]{0:T(1024)}, u32[]{:S(2)}) copy-start(f32[1024]{0:T(1024)} %get-tuple-element.71) | copy-start | bytes 12292
  845.1 141.2 %copy-start.54 = (f32[1664]{0:T(1024)}, f32[1664]{0:T(1024)S(1)}, u32[]{:S(2)}) copy-start(f32[1664]{0:T(1024)S(1)} %get-tuple-element.46) | copy-start | bytes 19972
  845.1 141.2 %copy-start.55 = (f32[1664]{0:T(1024)}, f32[1664]{0:T(1024)S(1)}, u32[]{:S(2)}) copy-start(f32[1664]{0:T(1024)S(1)} %get-tuple-element.47) | copy-start | bytes 19972
  845.1 89.3 %copy-start.13 = (f32[128,1024]{1,0:T(8,128)S(1)}, f32[128,1024]{1,0:T(8,128)}, u32[]{:S(2)}) copy-start(f32[128,1024]{1,0:T(8,128)} %param.22) | copy-start | bytes 1572868
  (45 other events, 148.0 us)
Sparse Core Ops, SparseCore 0:
  10.2 67.6 all-gather.5
  80.1 27.7 all-gather.7
  110.1 81.5 all-gather.9
  193.7 80.5 all-gather.11
  276.5 48.5 reduce-scatter.6
  327.2 127.3 reduce-scatter.4
  457.0 166.5 reduce-scatter.8
  626.0 166.5 reduce-scatter.10
  796.3 138.0 all-reduce.4
where the time goes:
time: 1010 us
  waiting for transfers between devices  754 us (75%)
  matrix products  91.3 us (9%)
  blocking collectives  68.9 us (7%)
  other arithmetic  45 us (4%)
  between operations  22.7 us (2%)
  local copies, waits for them, and re-layouts  22.4 us (2%)
    all_gather x4, waiting for transfers between devices, local(): lax.all_gather(shortened(rounded), 'fsdp', axis=0, tiled=True)  181 us
    reduce_scatter x1, waiting for transfers between devices, local(): lax.psum_scatter(row_terms(normed_two, d_hidden), 'fsdp', scatter_dimensi...  169 us
    reduce_scatter x1, waiting for transfers between devices, local(): lax.psum_scatter(row_terms(activated, back_narrow), 'fsdp', scatter_dimen...  169 us
    reduce_scatter x1, waiting for transfers between devices, local(): lax.psum_scatter(row_terms(normed_one, d_projected), 'fsdp', scatter_dime...  130 us
    psum x1, waiting for transfers between devices, local(): lax.psum((qkv_grad, out_grad, up_grad, down_grad, small_part), 'dp')  82 us
    dot_general x4, matrix products, outer_sum(): lax.dot_general(columns, right, (((0,), (0,)), ((), ())), preferred_eleme...  27.5 us
    unnamed x1, blocking collectives  26.4 us
    reduce_scatter x1, waiting for transfers between devices, local(): lax.psum_scatter(row_terms(mixed_heads, back_narrow), 'fsdp', scatter_dim...  24 us
  transfers between devices with their start and end apart: 9, of which 9 were waited for; matrix products, arithmetic and copies ran while one was open for 11% of the time, Pallas kernels for 0%

commit v1 on v0

--- a/solution.py
+++ b/solution.py
@@ -120,7 +120,7 @@
     return jnp.stack([jnp.sum(array_in * array_in) for array_in in arrays])
 
 
-def local(
+def local_rows(
     tokens_in,
     cotangent,
     lengths,
@@ -252,6 +252,186 @@
     )
     small_part = lax.psum_scatter(small_grad, "fsdp", scatter_dimension=0, tiled=True)
     reduced = lax.psum((qkv_grad, out_grad, up_grad, down_grad, small_part), "dp")
+    return (output[None], input_grad.astype(jnp.bfloat16)[None]) + lamb(
+        masters, firsts, seconds, reduced
+    )
+
+
+def local_split(
+    tokens_in,
+    cotangent,
+    lengths,
+    qkv_master,
+    out_master,
+    up_master,
+    down_master,
+    small_master,
+    qkv_first,
+    out_first,
+    up_first,
+    down_first,
+    small_first,
+    qkv_second,
+    out_second,
+    up_second,
+    down_second,
+    small_second,
+):
+    masters = (qkv_master, out_master, up_master, down_master, small_master)
+    firsts = (qkv_first, out_first, up_first, down_first, small_first)
+    seconds = (qkv_second, out_second, up_second, down_second, small_second)
+    qkv_low, out_weight, up_low, down_weight, small_low = (
+        master.astype(jnp.bfloat16) for master in masters
+    )
+    group = lax.axis_size("fsdp")
+    me = lax.axis_index("fsdp")
+    heads = HEADS // group
+    head_cols = heads * HD
+    ff_cols = FF // group
+    rows = qkv_master.shape[0]
+    length = tokens_in.shape[1]
+    tokens = group * length
+
+    inputs_all = lax.all_gather(tokens_in[0], "fsdp", axis=0, tiled=True)
+    cotangent_all = lax.all_gather(cotangent[0], "fsdp", axis=0, tiled=True)
+    lengths_all = lax.all_gather(lengths, "fsdp", axis=0, tiled=True)
+    small_all = lax.all_gather(small_low, "fsdp", axis=0, tiled=True)
+    qkv_weight = lax.all_to_all(
+        qkv_low.reshape(rows, 3, D), "fsdp", split_axis=2, concat_axis=0, tiled=True
+    ).reshape(D, 3 * head_cols)
+    up_weight = lax.all_to_all(up_low, "fsdp", split_axis=1, concat_axis=0, tiled=True)
+    gain_one, shift_one, gain_two, shift_two, qkv_bias, out_bias, up_bias, down_bias = split_small(
+        small_all.astype(jnp.float32)
+    )
+    qkv_bias = lax.dynamic_slice_in_dim(
+        qkv_bias.reshape(3, D), me * head_cols, head_cols, axis=1
+    ).reshape(3 * head_cols)
+    up_bias = lax.dynamic_slice_in_dim(up_bias, me * ff_cols, ff_cols)
+
+    inputs = inputs_all.astype(jnp.float32)
+    position = jnp.arange(length)
+    live = (position[None, :] < lengths_all[:, None]).astype(jnp.float32).reshape(tokens, 1)
+    allowed = (position[None, None, :] <= position[None, :, None]) & (
+        position[None, None, :] < lengths_all[:, None, None]
+    )
+    unit_rows, _ = normalize(inputs)
+    normed_one = (unit_rows * gain_one + shift_one).astype(jnp.bfloat16)
+    normed_two = (unit_rows * gain_two + shift_two).astype(jnp.bfloat16)
+    projected = jnp.dot(normed_one, qkv_weight, preferred_element_type=jnp.float32) + qkv_bias
+    projected = projected.reshape(group, length, 3, heads, HD)
+    cosine_table, sine_table = rotary_tables(length)
+    query_heads = rotate(projected[:, :, 0], cosine_table, sine_table).astype(jnp.bfloat16)
+    key_heads = rotate(projected[:, :, 1], cosine_table, sine_table).astype(jnp.bfloat16)
+    value_heads = projected[:, :, 2].astype(jnp.bfloat16)
+    scores = jnp.einsum(
+        "gqhd,gkhd->ghqk", query_heads, key_heads, preferred_element_type=jnp.float32
+    ) * HD ** (-0.5)
+    scores = jnp.where(allowed[:, None], scores, -1e30)
+    row_top = jnp.max(scores, axis=-1, keepdims=True)
+    raised = jnp.exp(scores - row_top)
+    attend = raised / jnp.sum(raised, axis=-1, keepdims=True)
+    attend_low = attend.astype(jnp.bfloat16)
+    mixed = jnp.einsum(
+        "ghqk,gkhd->gqhd", attend_low, value_heads, preferred_element_type=jnp.float32
+    )
+    mixed = mixed.reshape(tokens, head_cols).astype(jnp.bfloat16)
+    hidden = jnp.dot(normed_two, up_weight, preferred_element_type=jnp.float32) + up_bias
+    activated = jax.nn.gelu(hidden, approximate=False).astype(jnp.bfloat16)
+    out_part = jnp.dot(mixed, out_weight, preferred_element_type=jnp.float32) + jnp.dot(
+        activated, down_weight, preferred_element_type=jnp.float32
+    )
+    out_sum = lax.psum_scatter(
+        out_part.astype(jnp.bfloat16), "fsdp", scatter_dimension=0, tiled=True
+    ).astype(jnp.float32)
+
+    own_inputs = tokens_in[0].astype(jnp.float32)
+    own_live = (position < lengths[0]).astype(jnp.float32)[:, None]
+    own_back = cotangent[0].astype(jnp.float32) * own_live
+    own_unit, own_inverse = normalize(own_inputs)
+    output = ((own_inputs + out_sum + out_bias + down_bias) * own_live).astype(jnp.bfloat16)
+
+    back = (cotangent_all.astype(jnp.float32) * live).astype(jnp.bfloat16)
+    d_hidden = (against(back, down_weight) * gelu_slope(hidden)).astype(jnp.bfloat16)
+    d_mixed = against(back, out_weight).astype(jnp.bfloat16).reshape(group, length, heads, HD)
+    d_attend = jnp.einsum(
+        "gqhd,gkhd->ghqk", d_mixed, value_heads, preferred_element_type=jnp.float32
+    )
+    row_inner = jnp.sum(attend * d_attend, axis=-1, keepdims=True)
+    d_scores = (attend * (d_attend - row_inner)).astype(jnp.bfloat16)
+    d_queries = jnp.einsum(
+        "ghqk,gkhd->gqhd", d_scores, key_heads, preferred_element_type=jnp.float32
+    ) * HD ** (-0.5)
+    d_keys = jnp.einsum(
+        "ghqk,gqhd->gkhd", d_scores, query_heads, preferred_element_type=jnp.float32
+    ) * HD ** (-0.5)
+    d_values = jnp.einsum(
+        "ghqk,gqhd->gkhd", attend_low, d_mixed, preferred_element_type=jnp.float32
+    )
+    d_projected = jnp.stack(
+        [
+            rotate_back(d_queries, cosine_table, sine_table),
+            rotate_back(d_keys, cosine_table, sine_table),
+            d_values,
+        ],
+        axis=2,
+    )
+    d_projected = d_projected.reshape(tokens, 3 * head_cols).astype(jnp.bfloat16)
+    d_normed_one = against(d_projected, qkv_weight)
+    d_normed_two = against(d_hidden, up_weight)
+    scaled_part = d_normed_one * gain_one + d_normed_two * gain_two
+    scaled = lax.psum_scatter(
+        scaled_part.astype(jnp.bfloat16), "fsdp", scatter_dimension=0, tiled=True
+    ).astype(jnp.float32)
+    input_grad = own_back + own_inverse * (
+        scaled
+        - jnp.mean(scaled, axis=-1, keepdims=True)
+        - own_unit * jnp.mean(scaled * own_unit, axis=-1, keepdims=True)
+    )
+
+    back_total = jnp.sum(own_back, axis=0)
+    d_qkv_bias = lax.dynamic_update_slice_in_dim(
+        jnp.zeros((3, D), jnp.float32),
+        jnp.sum(d_projected, axis=0, dtype=jnp.float32).reshape(3, head_cols),
+        me * head_cols,
+        axis=1,
+    ).reshape(3 * D)
+    d_up_bias = lax.dynamic_update_slice_in_dim(
+        jnp.zeros((FF,), jnp.float32),
+        jnp.sum(d_hidden, axis=0, dtype=jnp.float32),
+        me * ff_cols,
+        axis=0,
+    )
+    small_grad = jnp.concatenate(
+        [
+            jnp.sum(d_normed_one * unit_rows, axis=0),
+            jnp.sum(d_normed_one, axis=0),
+            jnp.sum(d_normed_two * unit_rows, axis=0),
+            jnp.sum(d_normed_two, axis=0),
+            d_qkv_bias,
+            back_total,
+            d_up_bias,
+            back_total,
+        ]
+    )
+    small_sum = lax.psum(small_grad, ("dp", "fsdp"))
+    small_rows = small_master.shape[0]
+    small_sum = lax.dynamic_slice_in_dim(small_sum, me * small_rows, small_rows)
+    qkv_term = outer_sum(normed_one, d_projected).astype(jnp.bfloat16)
+    qkv_term = lax.all_to_all(
+        qkv_term.reshape(D, 3, head_cols), "fsdp", split_axis=0, concat_axis=2, tiled=True
+    ).reshape(rows, 3 * D)
+    up_term = outer_sum(normed_two, d_hidden).astype(jnp.bfloat16)
+    up_term = lax.all_to_all(up_term, "fsdp", split_axis=0, concat_axis=1, tiled=True)
+    out_term = outer_sum(mixed, back).astype(jnp.bfloat16)
+    down_term = outer_sum(activated, back).astype(jnp.bfloat16)
+    summed = lax.psum((qkv_term, out_term, up_term, down_term), "dp")
+    reduced = tuple(part.astype(jnp.float32) for part in summed) + (small_sum,)
+    return (output[None], input_grad.astype(jnp.bfloat16)[None]) + lamb(
+        masters, firsts, seconds, reduced
+    )
+
+
+def lamb(masters, firsts, seconds, reduced):
     updates = []
     first_news = []
     second_news = []
@@ -271,26 +451,7 @@
         for number in range(5)
     ]
     lamb_norms = jnp.stack([weight_norms, update_norms])
-    return (
-        output[None],
-        input_grad.astype(jnp.bfloat16)[None],
-        new_masters[0],
-        new_masters[1],
-        new_masters[2],
-        new_masters[3],
-        new_masters[4],
-        first_news[0],
-        first_news[1],
-        first_news[2],
-        first_news[3],
-        first_news[4],
-        second_news[0],
-        second_news[1],
-        second_news[2],
-        second_news[3],
-        second_news[4],
-        lamb_norms,
-    )
+    return tuple(new_masters) + tuple(first_news) + tuple(second_news) + (lamb_norms,)
 
 
 def solution(mesh):
@@ -334,4 +495,5 @@
         P("fsdp"),
         P(),
     )
+    local = local_split if HEADS % mesh.shape["fsdp"] == 0 else local_rows
     return jax.shard_map(local, mesh=mesh, in_specs=in_specs, out_specs=out_specs, check_vma=False)

time: 1010 us -> 561 us (0.56)
  waiting for transfers between devices: 754 us -> 220 us
  local copies, waits for them, and re-layouts: 22.4 us -> 69.8 us
  blocking collectives: 68.9 us -> 107 us
  matrix products: 91.3 us -> 69 us
  starting transfers between devices: 1.3 us -> 19.6 us
    reduce_scatter x4 -> x2, waiting for transfers between devices: 492 us -> 83.1 us  [the longest x1 49 us: local_split(): lax.psum_scatter(out_part.astype(jnp.bfloat16), 'fsdp', scatter_dimension...]
    all_gather x4 -> x2, waiting for transfers between devices: 181 us -> 0.01 us  [the longest x1 0.01 us: local_split(): inputs_all = lax.all_gather(tokens_in[0], 'fsdp', axis=0, tiled=True)]
    all_to_all x0 -> x4, waiting for transfers between devices: none -> 69.4 us  [the longest x1 51.5 us: local_split(): lax.all_to_all(qkv_low.reshape(rows, 3, D), 'fsdp', split_axis=2, concat_...]
    psum x2, blocking collectives: 26.8 us -> 53.1 us  [the longest x1 38.4 us: local_split(): small_sum = lax.psum(small_grad, ('dp', 'fsdp'))]
    all_to_all x0 -> x4, starting transfers between devices: none -> 19.2 us  [the longest x1 6.33 us: local_split(): lax.all_to_all(qkv_low.reshape(rows, 3, D), 'fsdp', split_axis=2, concat_...]
    unnamed x130 -> x132, local copies, waits for them, and re-layouts: 5.79 us -> 25 us
    dot_general x4, matrix products: 27.5 us -> 11.2 us  [outer_sum(): lax.dot_general(columns, right, (((0,), (0,)), ((), ())), preferred_eleme...]
    reshape x0 -> x7, local copies, waits for them, and re-layouts: none -> 16.2 us  [the longest x1 7.21 us: local_split(): projected = projected.reshape(group, length, 3, heads, HD)]
  transfers between devices with their start and end apart: 9 -> 9, of which waited for: 9 -> 6; matrix products, arithmetic and copies ran while one was open for 11% -> 20% of each run, Pallas kernels for 0% -> 0%
where the time goes in v1:
time: 561 us; the launch traced here: 557 us
  waiting for transfers between devices  220 us (39%)
  blocking collectives  107 us (19%)
  local copies, waits for them, and re-layouts  69.8 us (12%)
  matrix products  69 us (12%)
  other arithmetic  49.1 us (9%)
  between operations  22 us (4%)
  starting transfers between devices  19.6 us (3%)
    psum x1, waiting for transfers between devices, local_split(): summed = lax.psum((qkv_term, out_term, up_term, down_term), 'dp')  66.2 us
    all_to_all x1, waiting for transfers between devices, local_split(): lax.all_to_all(qkv_low.reshape(rows, 3, D), 'fsdp', split_axis=2, concat_...  51.5 us
    reduce_scatter x1, waiting for transfers between devices, local_split(): lax.psum_scatter(out_part.astype(jnp.bfloat16), 'fsdp', scatter_dimension...  49 us
    unnamed x1, blocking collectives  39.8 us
    psum x1, blocking collectives, local_split(): small_sum = lax.psum(small_grad, ('dp', 'fsdp'))  38.4 us
    reduce_scatter x1, waiting for transfers between devices, local_split(): lax.psum_scatter(scaled_part.astype(jnp.bfloat16), 'fsdp', scatter_dimens...  34.2 us
    unnamed x132, local copies, waits for them, and re-layouts  25 us
    reduce_sum x5, other arithmetic, local_squares(): return jnp.stack([jnp.sum(array_in * array_in) for array_in in arrays])  18.6 us
  transfers between devices with their start and end apart: 9, of which 6 were waited for; matrix products, arithmetic and copies ran while one was open for 20% of the time, Pallas kernels for 0%

profile of v1, /device:TPU:0, one launch (start us, length us, event | category | flops | bytes accessed | tf_op | source)
XLA Modules:
  0.0 557.2 jit_solution(9255853674114406320)
XLA Ops:
  12.1 6.3 %all-to-all-start = ((bf16[128,3,1024]{0,1,2:T(4,128)(2,1)}), bf16[128,3,1024]{0,1,2:T(4,128)(2,1)S(1)}, u32[]{:S(2)}, u32[]{:S(2)}) async-start(bf16[128,3,1024]{0,1,2:T(4,128)(2,1)} %copy.84), calls=%async_computation | async-start | bytes 2097152 | tf_op jit(solution)/shard_map/all_to_all | solution.py:299
  19.9 51.5 %all-to-all-done = bf16[128,3,1024]{0,1,2:T(4,128)(2,1)S(1)} async-done(((bf16[128,3,1024]{0,1,2:T(4,128)(2,1)}), bf16[128,3,1024]{0,1,2:T(4,128)(2,1)S(1)}, u32[]{:S(2)}, u32[]{:S(2)}) %all-to-all-start) | async-done | bytes 786464 | tf_op jit(solution)/shard_map/all_to_all | solution.py:299
  71.3 4.2 all-to-all-start.1
  77.6 39.8 %all-reduce = s32[8]{0:T(128)S(1)} all-reduce(s32[8]{0:T(128)S(1)} %dynamic-update-slice), channel_id=1, replica_groups=mesh['dp'=4,'fsdp'=8] {'fsdp'}, use_global_device_ids=true, to_apply=%add | all-reduce | flops 8 | bytes 64
  117.4 14.5 %all-gather.2 = bf16[8,1,1664]{2,1,0:T(2,128)(2,1)S(1)} all-gather(bf16[1,1,1664]{2,1,0:T(2,128)(2,1)S(1)} %reshape.275), channel_id=1, replica_groups=mesh['dp'=4,'fsdp'=8] {'fsdp'}, dimensions={0}, use_global_device_ids=true | all-gather | bytes 29952 | tf_op jit(solution)/shard_map/all_gather | solution.py:298
  153.2 7.2 %reshape.280 = f32[8,256,3,2,64]{4,3,2,1,0:T(2,128)} reshape(f32[2048,384]{1,0:T(8,128)} %convolution_add_fusion) | data formatting | bytes 6291456 | tf_op jit(solution)/shard_map/reshape | solution.py:321
  163.6 4.7 fusion.96
  185.3 4.4 copy.115
  192.7 5.2 fusion.100
  212.5 4.4 all-to-all-start.2
  216.9 13.9 %fusion.18 = (bf16[2048,512]{1,0:T(8,128)(2,1)}, f32[2048,512]{1,0:T(8,128)S(1)}) fusion(f32[512]{0:T(512)S(1)} %copy-done.50, bf16[2048,1024]{1,0:T(8,128)(2,1)} %get-tuple-element.58, bf16[1024,512]{1,0:T(8,128)(2,1)} %bitcast.210), kind=kOutput, calls=%fused_computation.25 | convolution fusion | flops 2216689664 | bytes 11536384 | tf_op jit(solution)/shard_map/dot_general | solution.py:338
  230.9 4.6 convert_reduce_fusion.1
  243.5 4.2 all-to-all-start.3
  259.6 14.7 %all-to-all-done.3 = bf16[8,128,512]{2,1,0:T(8,128)(2,1)} async-done(((bf16[8,128,512]{2,1,0:T(8,128)(2,1)}), bf16[8,128,512]{2,1,0:T(8,128)(2,1)}, u32[]{:S(2)}, u32[]{:S(2)}) %all-to-all-start.3) | async-done | bytes 1048608 | tf_op jit(solution)/shard_map/all_to_all | solution.py:424
  281.2 6.2 %fusion.89 = (f32[1024]{0:T(1024)S(1)}, f32[1024]{0:T(1024)S(1)}, bf16[2048,1024]{1,0:T(8,128)(2,1)}, f32[1024]{0:T(1024)S(1)}, f32[1024]{0:T(1024)S(1)}) fusion(f32[2048]{0:T(1024)S(1)} %copy-done.35, f32[2048]{0:T(1024)S(1)} %broadcast_multiply_fusion, bf16[1,2048,1024]{2,1,0:T(8,128)(2,1)S(1)} %copy-done.1, f32[1024]{0:T(1024)S(1)} %copy-done.43, ...), kind=kOutput, calls=%fused_computation.194 | convolution fusion | flops 2174742528 | bytes 19963904 | tf_op jit(solution)/shard_map/dot_general | solution.py:97
  287.5 4.6 fusion.72
  297.3 66.2 %all-reduce.5.cloned.1.call-done = (bf16[128,3072]{1,0:T(8,128)(2,1)}, bf16[128,1024]{1,0:T(8,128)(2,1)}, bf16[128,4096]{1,0:T(8,128)(2,1)}, bf16[512,1024]{1,0:T(8,128)(2,1)}) async-done(((bf16[128,3072]{1,0:T(8,128)(2,1)}, bf16[128,1024]{1,0:T(8,128)(2,1)}, bf16[128,4096]{1,0:T(8,128)(2,1)}, bf16[512,1024]{1,0:T(8,128)(2,1)}), (bf16[128,3072]{1,0:T(8,128)(2,1)}, bf16[128,1024]{1,0:T(8,128)(2,1)}, ...) | async-done | bytes 3145744 | tf_op jit(solution)/shard_map/psum | solution.py:427
  366.8 6.2 %multiply_reduce_fusion.5 = (f32[]{:T(128)}, f32[]{:T(128)}, f32[128,3072]{1,0:T(8,128)}, f32[128,3072]{1,0:T(8,128)}) fusion(f32[128,3072]{1,0:T(8,128)} %param.21, bf16[128,3072]{1,0:T(8,128)(2,1)} %get-tuple-element.36, f32[128,3072]{1,0:T(8,128)} %param.31, f32[128,3072]{1,0:T(8,128)} %param.26), kind=kLoop, calls=%fused_computation.79 | loop fusion | flops 5898238 | bytes 8650760 | tf_op jit(solution)/shard_map/reduce_sum | solution.py:120
  373.0 4.2 multiply_reduce_fusion.2
  377.4 4.2 multiply_reduce_fusion.1
  381.7 34.2 %reduce-scatter.5.cloned.1.call-done = bf16[256,1024]{1,0:T(8,128)(2,1)} async-done(((bf16[2048,1024]{1,0:T(8,128)(2,1)}), bf16[256,1024]{1,0:T(8,128)(2,1)}) %reduce-scatter.5.cloned.1.call-update) | async-done | bytes 524304 | tf_op jit(solution)/shard_map/reduce_scatter | solution.py:382
  417.3 49.0 %reduce-scatter.3.cloned.1.call-done = bf16[256,1024]{1,0:T(8,128)(2,1)} async-done(((bf16[2048,1024]{1,0:T(8,128)(2,1)}), bf16[256,1024]{1,0:T(8,128)(2,1)}) %reduce-scatter.3.cloned.1.call-update) | async-done | bytes 524304 | tf_op jit(solution)/shard_map/reduce_scatter | solution.py:343
  469.2 38.4 %psum.54 = f32[13312]{0:T(1024)S(1)} all-reduce(f32[13312]{0:T(1024)S(1)} %constant_dynamic-update-slice_fusion), channel_id=1, replica_groups=mesh['dp'=4,'fsdp'=8] {'dp','fsdp'}, use_global_device_ids=true, to_apply=%region_32.33 | all-reduce | flops 13312 | bytes 106496 | tf_op jit(solution)/shard_map/psum | solution.py:416
  514.9 14.7 %all-reduce.1 = (f32[5]{0:T(128)S(1)}, f32[5]{0:T(128)S(1)}) all-reduce(f32[5]{0:T(128)S(1)} %stack.66, f32[5]{0:T(128)S(1)} %stack.72), channel_id=1, replica_groups=mesh['dp'=4,'fsdp'=8] {'fsdp'}, use_global_device_ids=true, to_apply=%region_16.17 | all-reduce | flops 10 | bytes 80 | tf_op jit(solution)/shard_map/psum | solution.py:444
  (227 shorter events, 127.6 us)
Async XLA Ops:
  7.2 11.3 %copy-start.2 = (f32[128,4096]{1,0:T(8,128)S(1)}, f32[128,4096]{1,0:T(8,128)}, u32[]{:S(2)}) copy-start(f32[128,4096]{1,0:T(8,128)} %param.23) | copy-start | bytes 6291460
  7.2 131.2 %all-gather.6.cloned.1.call-start = ((), (), s32[]{:S(2)}) async-start(), calls=%async_computation.8 | async-start | bytes 4718592 | tf_op jit(solution)/shard_map/all_gather | solution.py:295
  7.9 160.4 %all-gather.8.cloned.1.call-start = ((), (), s32[]{:S(2)}) async-start(), calls=%async_computation.9 | async-start | bytes 4718592 | tf_op jit(solution)/shard_map/all_gather | solution.py:296
  10.5 65.7 %copy-start.53 = (u32[32]{0:T(128)S(1)}, u32[32]{0:T(128)}, u32[]{:S(2)}) copy-start(u32[32]{0:T(128)} %constant.46) | copy-start | bytes 388
  10.5 106.9 %copy-start.32 = (f32[1664]{0:T(1024)S(1)}, f32[1664]{0:T(1024)}, u32[]{:S(2)}) copy-start(f32[1664]{0:T(1024)} %param.25) | copy-start | bytes 19972
  12.1 59.2 %all-to-all-start = ((bf16[128,3,1024]{0,1,2:T(4,128)(2,1)}), bf16[128,3,1024]{0,1,2:T(4,128)(2,1)S(1)}, u32[]{:S(2)}, u32[]{:S(2)}) async-start(bf16[128,3,1024]{0,1,2:T(4,128)(2,1)} %copy.84), calls=%async_computation | async-start | bytes 2097152 | tf_op jit(solution)/shard_map/all_to_all | solution.py:299
  71.3 64.6 %all-to-all-start.1 = ((bf16[128,8,512]{0,2,1:T(8,128)(2,1)}), bf16[128,8,512]{0,2,1:T(8,128)(2,1)}, u32[]{:S(2)}, u32[]{:S(2)}) async-start(bf16[128,8,512]{0,2,1:T(8,128)(2,1)} %bitcast.12), calls=%async_computation.1 | async-start | bytes 2097152 | tf_op jit(solution)/shard_map/all_to_all | solution.py:302
  132.0 36.3 %copy-start.48 = (f32[1,2,8,128]{3,1,2,0:T(2,128)}, f32[1,2,8,128]{3,1,2,0:T(2,128)S(1)}, u32[]{:S(2)}) copy-start(f32[1,2,8,128]{3,1,2,0:T(2,128)S(1)} %copy.119) | copy-start | bytes 24580
  135.8 11.2 %copy-start.17 = (bf16[8,128,3,128]{1,0,3,2:T(8,128)(2,1)}, bf16[8,128,3,128]{1,0,3,2:T(8,128)(2,1)S(1)}, u32[]{:S(2)}) copy-start(bf16[8,128,3,128]{1,0,3,2:T(8,128)(2,1)S(1)} %copy.86) | copy-start | bytes 2359300
  212.5 31.0 %all-to-all-start.2 = ((bf16[1024,3,128]{2,1,0:T(4,128)(2,1)}), bf16[1024,3,128]{2,1,0:T(4,128)(2,1)}, u32[]{:S(2)}, u32[]{:S(2)}) async-start(bf16[1024,3,128]{2,1,0:T(4,128)(2,1)} %copy.102), calls=%async_computation.4 | async-start | bytes 2097152 | tf_op jit(solution)/shard_map/all_to_all | solution.py:420
  216.9 14.0 %copy-start.3 = (f32[512,1024]{1,0:T(8,128)S(1)}, f32[512,1024]{1,0:T(8,128)}, u32[]{:S(2)}) copy-start(f32[512,1024]{1,0:T(8,128)} %param.24) | copy-start | bytes 6291460
  216.9 14.0 %copy-start.49 = (f32[1,2,8,128]{3,1,2,0:T(2,128)S(1)}, f32[1,2,8,128]{3,1,2,0:T(2,128)}, u32[]{:S(2)}) copy-start(f32[1,2,8,128]{3,1,2,0:T(2,128)} %copy-done.48) | copy-start | bytes 24580
  216.9 14.0 %copy-start.51 = (bf16[1,2048,1024]{2,1,0:T(8,128)(2,1)S(1)}, bf16[1,2048,1024]{2,1,0:T(8,128)(2,1)}, u32[]{:S(2)}) copy-start(bf16[1,2048,1024]{2,1,0:T(8,128)(2,1)} %all-gather.8.cloned.1.call-done) | copy-start | bytes 12582916
  243.5 30.8 %all-to-all-start.3 = ((bf16[8,128,512]{2,1,0:T(8,128)(2,1)}), bf16[8,128,512]{2,1,0:T(8,128)(2,1)}, u32[]{:S(2)}, u32[]{:S(2)}) async-start(bf16[8,128,512]{2,1,0:T(8,128)(2,1)} %bitcast.212), calls=%async_computation.5 | async-start | bytes 2097152 | tf_op jit(solution)/shard_map/all_to_all | solution.py:424
  247.7 115.8 %all-reduce.5.cloned.1.call-start = ((), (), s32[]{:S(2)}) async-start(), calls=%async_computation.10 | async-start | bytes 6291456 | tf_op jit(solution)/shard_map/psum | solution.py:427
  276.7 139.1 %reduce-scatter.5.cloned.1.call-start = ((), (), s32[]{:S(2)}) async-start(), calls=%async_computation.7 | async-start | bytes 4718592 | tf_op jit(solution)/shard_map/reduce_scatter | solution.py:382
  287.4 178.8 %reduce-scatter.3.cloned.1.call-start = ((), (), s32[]{:S(2)}) async-start(), calls=%async_computation.6 | async-start | bytes 4718592 | tf_op jit(solution)/shard_map/reduce_scatter | solution.py:343
  377.4 88.8 %copy-start.40 = (f32[1024]{0:T(1024)S(1)}, f32[1024]{0:T(1024)}, u32[]{:S(2)}) copy-start(f32[1024]{0:T(1024)} %get-tuple-element.70) | copy-start | bytes 12292
  377.4 88.8 %copy-start.41 = (f32[1024]{0:T(1024)S(1)}, f32[1024]{0:T(1024)}, u32[]{:S(2)}) copy-start(f32[1024]{0:T(1024)} %get-tuple-element.71) | copy-start | bytes 12292
  381.6 125.9 %copy-start.33 = (f32[1664]{0:T(1024)S(1)}, f32[1664]{0:T(1024)}, u32[]{:S(2)}) copy-start(f32[1664]{0:T(1024)} %param.25) | copy-start | bytes 19972
  381.6 125.9 %copy-start.46 = (f32[1664]{0:T(1024)S(1)}, f32[1664]{0:T(1024)}, u32[]{:S(2)}) copy-start(f32[1664]{0:T(1024)} %param.35) | copy-start | bytes 19972
  381.7 125.9 %copy-start.47 = (f32[1664]{0:T(1024)S(1)}, f32[1664]{0:T(1024)}, u32[]{:S(2)}) copy-start(f32[1664]{0:T(1024)} %param.30) | copy-start | bytes 19972
  508.3 37.0 %copy-start.36 = (f32[1664]{0:T(1024)}, f32[1664]{0:T(1024)S(1)}, u32[]{:S(2)}) copy-start(f32[1664]{0:T(1024)S(1)} %get-tuple-element.40) | copy-start | bytes 19972
  508.3 37.0 %copy-start.37 = (f32[1664]{0:T(1024)}, f32[1664]{0:T(1024)S(1)}, u32[]{:S(2)}) copy-start(f32[1664]{0:T(1024)S(1)} %get-tuple-element.41) | copy-start | bytes 19972
  (41 other events, 188.3 us)
Sparse Core Ops, SparseCore 0:
  9.6 70.7 all-gather.5
  82.1 56.0 all-gather.7
  276.8 86.7 all-reduce.4
  365.8 49.9 reduce-scatter.4
  418.1 48.1 reduce-scatter.2

commit v2 on v0

v2 whole, which is shorter than its diff:
```python
import math

import jax
import jax.numpy as jnp
from jax import lax
from jax.sharding import PartitionSpec as P

D = 1024
HEADS = 16
HD = 64
FF = 4096
ROT = 16


NORM_EPSILON = 1e-05
ADAM_EPSILON = 1e-06
ROPE_BASE = 10000.0
RATE = 0.5
DECAY = 0.01
BETA_ONE = 0.5
BETA_TWO = 0.5


def split_small(small_vector):
    bounds = [0, D, 2 * D, 3 * D, 4 * D, 7 * D, 8 * D, 8 * D + FF, 9 * D + FF]
    return [small_vector[bounds[number] : bounds[number + 1]] for number in range(8)]


def normalize(values):
    average = jnp.mean(values, axis=-1, keepdims=True)
    centred = values - average
    variance = jnp.mean(centred * centred, axis=-1, keepdims=True)
    inverse = lax.rsqrt(variance + NORM_EPSILON)
    return (centred * inverse, inverse)


def rotary_tables(length):
    half_dims = ROT // 2
    position = jnp.arange(length, dtype=jnp.float32)[:, None]
    number = jnp.arange(half_dims, dtype=jnp.float32)[None, :]
    angle = position * jnp.exp(number * (-2.0 * math.log(ROPE_BASE) / ROT))
    return (jnp.cos(angle)[:, None, :], jnp.sin(angle)[:, None, :])


def rotate(heads_in, cosine_table, sine_table):
    half_dims = ROT // 2
    first_half = heads_in[..., :half_dims]
    second_half = heads_in[..., half_dims:ROT]
    return jnp.concatenate(
        [
            first_half * cosine_table - second_half * sine_table,
            second_half * cosine_table + first_half * sine_table,
            heads_in[..., ROT:],
        ],
        axis=-1,
    )


def rotate_back(grads_in, cosine_table, sine_table):
    half_dims = ROT // 2
    first_half = grads_in[..., :half_dims]
    second_half = grads_in[..., half_dims:ROT]
    return jnp.concatenate(
        [
            first_half * cosine_table + second_half * sine_table,
            second_half * cosine_table - first_half * sine_table,
            grads_in[..., ROT:],
        ],
        axis=-1,
    )


def gelu_slope(values):
    return 0.5 * (1.0 + lax.erf(values * 2.0 ** (-0.5))) + values * jnp.exp(
        -0.5 * values * values
    ) * (2.0 * math.pi) ** (-0.5)


def against(left, right):
    return lax.dot_general(
        left, right, (((1,), (1,)), ((), ())), preferred_element_type=jnp.float32
    )


def outer_sum(columns, right):
    return lax.dot_general(
        columns, right, (((0,), (0,)), ((), ())), preferred_element_type=jnp.float32
    )


def local_squares(arrays):
    return jnp.stack([jnp.sum(array_in * array_in) for array_in in arrays])


def sliced(master, part, parts, pieces):
    rows, columns = master.shape
    width = columns // (pieces * parts)
    return lax.dynamic_index_in_dim(
        master.reshape(rows, pieces, parts, width), part, axis=2, keepdims=False
    ).reshape(rows, pieces * width)


def joined(slices, pieces):
    parts, rows, columns = slices.shape
    width = columns // pieces
    return (
        slices.reshape(parts, rows, pieces, width)
        .transpose(1, 2, 0, 3)
        .reshape(rows, pieces * parts * width)
    )


def layer(x_all, cotangent_all, lengths_all, weights, small_all, part):
    qkv_weight, out_weight, up_weight, down_weight = weights
    group, length, _ = x_all.shape
    tokens = group * length
    head_cols = out_weight.shape[0]
    heads = head_cols // HD
    gain_one, shift_one, gain_two, shift_two, qkv_bias, up_bias = small_all
    inputs = x_all.reshape(tokens, D).astype(jnp.float32)
    position = jnp.arange(length)
    live = (position[None, :] < lengths_all[:, None]).astype(jnp.float32).reshape(tokens, 1)
    allowed = (position[None, None, :] <= position[None, :, None]) & (
        position[None, None, :] < lengths_all[:, None, None]
    )
    unit_rows, _ = normalize(inputs)
    normed_one = (unit_rows * gain_one + shift_one).astype(jnp.bfloat16)
    normed_two = (unit_rows * gain_two + shift_two).astype(jnp.bfloat16)
    projected = jnp.dot(normed_one, qkv_weight, preferred_element_type=jnp.float32) + qkv_bias
    projected = projected.reshape(group, length, 3, heads, HD)
    cosine_table, sine_table = rotary_tables(length)
    query_heads = rotate(projected[:, :, 0], cosine_table, sine_table).astype(jnp.bfloat16)
    key_heads = rotate(projected[:, :, 1], cosine_table, sine_table).astype(jnp.bfloat16)
    value_heads = projected[:, :, 2].astype(jnp.bfloat16)
    scores = jnp.einsum(
        "gqhd,gkhd->ghqk", query_heads, key_heads, preferred_element_type=jnp.float32
    ) * HD ** (-0.5)
    scores = jnp.where(allowed[:, None], scores, -1e30)
    row_top = jnp.max(scores, axis=-1, keepdims=True)
    raised = jnp.exp(scores - row_top)
    attend = raised / jnp.sum(raised, axis=-1, keepdims=True)
    attend_low = attend.astype(jnp.bfloat16)
    mixed = jnp.einsum(
        "ghqk,gkhd->gqhd", attend_low, value_heads, preferred_element_type=jnp.float32
    )
    mixed = mixed.reshape(tokens, head_cols).astype(jnp.bfloat16)
    hidden = jnp.dot(normed_two, up_weight, preferred_element_type=jnp.float32) + up_bias
    activated = jax.nn.gelu(hidden, approximate=False).astype(jnp.bfloat16)
    out_part = jnp.dot(mixed, out_weight, preferred_element_type=jnp.float32) + jnp.dot(
        activated, down_weight, preferred_element_type=jnp.float32
    )

    back = (cotangent_all.reshape(tokens, D).astype(jnp.float32) * live).astype(jnp.bfloat16)
    d_hidden = (against(back, down_weight) * gelu_slope(hidden)).astype(jnp.bfloat16)
    d_mixed = against(back, out_weight).astype(jnp.bfloat16).reshape(group, length, heads, HD)
    d_attend = jnp.einsum(
        "gqhd,gkhd->ghqk", d_mixed, value_heads, preferred_element_type=jnp.float32
    )
    row_inner = jnp.sum(attend * d_attend, axis=-1, keepdims=True)
    d_scores = (attend * (d_attend - row_inner)).astype(jnp.bfloat16)
    d_queries = jnp.einsum(
        "ghqk,gkhd->gqhd", d_scores, key_heads, preferred_element_type=jnp.float32
    ) * HD ** (-0.5)
    d_keys = jnp.einsum(
        "ghqk,gqhd->gkhd", d_scores, query_heads, preferred_element_type=jnp.float32
    ) * HD ** (-0.5)
    d_values = jnp.einsum(
        "ghqk,gqhd->gkhd", attend_low, d_mixed, preferred_element_type=jnp.float32
    )
    d_projected = jnp.stack(
        [
            rotate_back(d_queries, cosine_table, sine_table),
            rotate_back(d_keys, cosine_table, sine_table),
            d_values,
        ],
        axis=2,
    )
    d_projected = d_projected.reshape(tokens, 3 * head_cols).astype(jnp.bfloat16)
    d_normed_one = against(d_projected, qkv_weight)
    d_normed_two = against(d_hidden, up_weight)
    scaled_part = d_normed_one * gain_one + d_normed_two * gain_two
    norm_sums = jnp.stack(
        [
            jnp.sum(d_normed_one * unit_rows, axis=0),
            jnp.sum(d_normed_one, axis=0),
            jnp.sum(d_normed_two * unit_rows, axis=0),
            jnp.sum(d_normed_two, axis=0),
        ]
    )
    d_qkv_bias = jnp.sum(d_projected, axis=0, dtype=jnp.float32)
    d_up_bias = jnp.sum(d_hidden, axis=0, dtype=jnp.float32)
    terms = (
        outer_sum(normed_one, d_projected),
        outer_sum(mixed, back),
        outer_sum(normed_two, d_hidden),
        outer_sum(activated, back),
    )
    return (
        out_part.astype(jnp.bfloat16),
        scaled_part.astype(jnp.bfloat16),
        tuple(term.astype(jnp.bfloat16) for term in terms),
        (norm_sums, d_qkv_bias, d_up_bias),
    )


def local_split(
    tokens_in,
    cotangent,
    lengths,
    qkv_master,
    out_master,
    up_master,
    down_master,
    small_master,
    qkv_first,
    out_first,
    up_first,
    down_first,
    small_first,
    qkv_second,
    out_second,
    up_second,
    down_second,
    small_second,
):
    masters = (qkv_master, out_master, up_master, down_master, small_master)
    firsts = (qkv_first, out_first, up_first, down_first, small_first)
    seconds = (qkv_second, out_second, up_second, down_second, small_second)
    parts, shards = lax.axis_size("dp"), lax.axis_size("fsdp")
    part, shard = lax.axis_index("dp"), lax.axis_index("fsdp")
    length = tokens_in.shape[1]
    head_cols = D // parts
    ff_cols = FF // parts
    ff_rows = down_master.shape[0] // parts

    qkv_own = sliced(qkv_master, part, parts, 3).astype(jnp.bfloat16)
    up_own = sliced(up_master, part, parts, shards).astype(jnp.bfloat16)
    down_own = lax.dynamic_slice_in_dim(down_master, part * ff_rows, ff_rows).astype(jnp.bfloat16)
    out_own = out_master.astype(jnp.bfloat16)
    small_own = small_master.astype(jnp.bfloat16)

    def over_shards(own):
        return lax.all_gather(own, "fsdp", axis=0, tiled=True)

    x_all = lax.all_gather(tokens_in, "dp", axis=0, tiled=True)
    cotangent_all = lax.all_gather(cotangent, "dp", axis=0, tiled=True)
    lengths_all = lax.all_gather(lengths, "dp", axis=0, tiled=True)
    qkv_weight, up_weight, down_weight = (over_shards(w) for w in (qkv_own, up_own, down_own))
    out_weight = lax.dynamic_slice_in_dim(over_shards(out_own), part * head_cols, head_cols)
    gain_one, shift_one, gain_two, shift_two, qkv_bias, out_bias, up_bias, down_bias = split_small(
        over_shards(small_own).astype(jnp.float32)
    )
    qkv_bias = sliced(qkv_bias[None], part, parts, 3)[0]
    up_bias = sliced(up_bias[None], part, parts, shards)[0]

    out_part, scaled_part, terms, sums = layer(
        x_all,
        cotangent_all,
        lengths_all,
        (qkv_weight, out_weight, up_weight, down_weight),
        (gain_one, shift_one, gain_two, shift_two, qkv_bias, up_bias),
        part,
    )
    out_sum = lax.psum_scatter(out_part, "dp", scatter_dimension=0, tiled=True)
    scaled = lax.psum_scatter(scaled_part, "dp", scatter_dimension=0, tiled=True)
    out_sum, scaled = out_sum.astype(jnp.float32), scaled.astype(jnp.float32)

    inputs = tokens_in[0].astype(jnp.float32)
    live = (jnp.arange(length) < lengths[0]).astype(jnp.float32)[:, None]
    back = cotangent[0].astype(jnp.float32) * live
    unit_rows, inverse_rows = normalize(inputs)
    output = ((inputs + out_sum + out_bias + down_bias) * live).astype(jnp.bfloat16)
    input_grad = back + inverse_rows * (
        scaled
        - jnp.mean(scaled, axis=-1, keepdims=True)
        - unit_rows * jnp.mean(scaled * unit_rows, axis=-1, keepdims=True)
    )

    norm_sums, d_qkv_bias, d_up_bias = sums
    back_total = jnp.sum(back, axis=0)

    def spread(values, pieces):
        wide = jnp.zeros((pieces, parts, values.shape[0] // pieces), jnp.float32)
        return lax.dynamic_update_index_in_dim(
            wide, values.reshape(pieces, -1), part, axis=1
        ).reshape(-1)

    small_grad = jnp.concatenate(
        [
            norm_sums.reshape(4 * D),
            spread(d_qkv_bias, 3),
            back_total,
            spread(d_up_bias, shards),
            back_total,
        ]
    )
    small_sum = lax.psum(small_grad, ("dp", "fsdp"))
    small_rows = small_master.shape[0]
    small_sum = lax.dynamic_slice_in_dim(small_sum, shard * small_rows, small_rows)

    qkv_term, out_term, up_term, down_term = terms
    out_wide = lax.dynamic_update_slice_in_dim(
        jnp.zeros((D, D), jnp.bfloat16), out_term, part * head_cols, axis=0
    )

    def to_owner(term):
        own = lax.psum_scatter(term, "fsdp", scatter_dimension=0, tiled=True)
        return lax.all_gather(own, "dp", axis=0, tiled=False).astype(jnp.float32)

    qkv_sum = joined(to_owner(qkv_term), 3)
    up_sum = joined(to_owner(up_term), shards)
    down_sum = to_owner(down_term).reshape(down_master.shape)
    out_sum_grad = lax.psum(
        lax.psum_scatter(out_wide, "fsdp", scatter_dimension=0, tiled=True), "dp"
    ).astype(jnp.float32)
    reduced = (qkv_sum, out_sum_grad, up_sum, down_sum, small_sum)
    return (output[None], input_grad.astype(jnp.bfloat16)[None]) + lamb(
        masters, firsts, seconds, reduced
    )


def lamb(masters, firsts, seconds, reduced):
    updates = []
    first_news = []
    second_news = []
    for first_old, second_old, master, grad_sum in zip(firsts, seconds, masters, reduced):
        first_new = BETA_ONE * first_old + (1.0 - BETA_ONE) * grad_sum
        second_new = BETA_TWO * second_old + (1.0 - BETA_TWO) * grad_sum * grad_sum
        updates.append(first_new / (jnp.sqrt(second_new) + ADAM_EPSILON) + DECAY * master)
        first_news.append(first_new)
        second_news.append(second_new)
    weight_squares, update_squares = lax.psum(
        (local_squares(masters), local_squares(updates)), "fsdp"
    )
    weight_norms = jnp.sqrt(weight_squares)
    update_norms = jnp.sqrt(update_squares)
    new_masters = [
        masters[number] - RATE * (weight_norms[number] / update_norms[number]) * updates[number]
        for number in range(5)
    ]
    lamb_norms = jnp.stack([weight_norms, update_norms])
    return tuple(new_masters) + tuple(first_news) + tuple(second_news) + (lamb_norms,)


def solution(mesh):
    in_specs = (
        P(("dp", "fsdp"), None, None),
        P(("dp", "fsdp"), None, None),
        P(("dp", "fsdp")),
        P("fsdp", None),
        P("fsdp", None),
        P("fsdp", None),
        P("fsdp", None),
        P("fsdp"),
        P("fsdp", None),
        P("fsdp", None),
        P("fsdp", None),
        P("fsdp", None),
        P("fsdp"),
        P("fsdp", None),
        P("fsdp", None),
        P("fsdp", None),
        P("fsdp", None),
        P("fsdp"),
    )
    out_specs = (
        P(("dp", "fsdp"), None, None),
        P(("dp", "fsdp"), None, None),
        P("fsdp", None),
        P("fsdp", None),
        P("fsdp", None),
        P("fsdp", None),
        P("fsdp"),
        P("fsdp", None),
        P("fsdp", None),
        P("fsdp", None),
        P("fsdp", None),
        P("fsdp"),
        P("fsdp", None),
        P("fsdp", None),
        P("fsdp", None),
        P("fsdp", None),
        P("fsdp"),
        P(),
    )
    return jax.shard_map(local_split, mesh=mesh, in_specs=in_specs, out_specs=out_specs, check_vma=False)
```

time: 1010 us -> 638 us (0.63)
  waiting for transfers between devices: 754 us -> 298 us
  local copies, waits for them, and re-layouts: 22.4 us -> 80.2 us
  blocking collectives: 68.9 us -> 93.4 us
  other arithmetic: 45 us -> 60.6 us
  matrix products: 91.3 us -> 78.1 us
    reduce_scatter x4 -> x6, waiting for transfers between devices: 492 us -> 170 us  [the longest x3 95.4 us: to_owner(): own = lax.psum_scatter(term, 'fsdp', scatter_dimension=0, tiled=True)]
    all_gather x4 -> x8, waiting for transfers between devices: 181 us -> 94.8 us  [the longest x4 90 us: over_shards(): return lax.all_gather(own, 'fsdp', axis=0, tiled=True)]
    psum x1, waiting for transfers between devices: 82 us -> 32.2 us  [local_split(): lax.psum(lax.psum_scatter(out_wide, 'fsdp', scatter_dimension=0, tiled=Tr...]
    unnamed x130 -> x143, local copies, waits for them, and re-layouts: 5.79 us -> 33.9 us
    psum x2, blocking collectives: 26.8 us -> 54.6 us  [the longest x1 39.9 us: local_split(): small_sum = lax.psum(small_grad, ('dp', 'fsdp'))]
    reshape x0 -> x9, local copies, waits for them, and re-layouts: none -> 18.9 us  [the longest x6 9.27 us: joined(): return slices.reshape(parts, rows, pieces, width).transpose(1, 2, 0, 3).r...]
    unnamed x1, blocking collectives: 26.4 us -> 8.01 us
    all_gather x1 -> x2, blocking collectives: 15.8 us -> 30.8 us  [the longest x1 15.7 us: over_shards(): return lax.all_gather(own, 'fsdp', axis=0, tiled=True)]
  transfers between devices with their start and end apart: 9 -> 15, of which waited for: 9 -> 13; matrix products, arithmetic and copies ran while one was open for 11% -> 29% of each run, Pallas kernels for 0% -> 0%
where the time goes in v2:
time: 638 us; the launch traced here: 634 us
  waiting for transfers between devices  298 us (47%)
  blocking collectives  93.4 us (15%)
  local copies, waits for them, and re-layouts  80.2 us (13%)
  matrix products  78.1 us (12%)
  other arithmetic  60.6 us (9%)
  between operations  22 us (3%)
    reduce_scatter x3, waiting for transfers between devices, to_owner(): own = lax.psum_scatter(term, 'fsdp', scatter_dimension=0, tiled=True)  95.4 us
    all_gather x4, waiting for transfers between devices, over_shards(): return lax.all_gather(own, 'fsdp', axis=0, tiled=True)  90 us
    psum x1, blocking collectives, local_split(): small_sum = lax.psum(small_grad, ('dp', 'fsdp'))  39.9 us
    reduce_scatter x1, waiting for transfers between devices, local_split(): out_sum = lax.psum_scatter(out_part, 'dp', scatter_dimension=0, tiled=True)  37.1 us
    unnamed x143, local copies, waits for them, and re-layouts  33.9 us
    psum x1, waiting for transfers between devices, local_split(): lax.psum(lax.psum_scatter(out_wide, 'fsdp', scatter_dimension=0, tiled=Tr...  32.2 us
    reduce_scatter x1, waiting for transfers between devices, local_split(): lax.psum_scatter(out_wide, 'fsdp', scatter_dimension=0, tiled=True)  30 us
    reduce_sum x6, other arithmetic, local_squares(): return jnp.stack([jnp.sum(array_in * array_in) for array_in in arrays])  21.3 us
  transfers between devices with their start and end apart: 15, of which 13 were waited for; matrix products, arithmetic and copies ran while one was open for 29% of the time, Pallas kernels for 0%

profile of v2, /device:TPU:0, one launch (start us, length us, event | category | flops | bytes accessed | tf_op | source)
XLA Modules:
  0.0 634.1 jit_solution(11582230660681982558)
XLA Ops:
  17.1 15.7 %all-gather.3 = bf16[8,1,1664]{2,1,0:T(2,128)(2,1)S(1)} all-gather(bf16[1,1,1664]{2,1,0:T(2,128)(2,1)S(1)} %reshape.376), channel_id=1, replica_groups=mesh['dp'=4,'fsdp'=8] {'fsdp'}, dimensions={0}, use_global_device_ids=true | all-gather | bytes 29952 | tf_op jit(solution)/shard_map/all_gather | solution.py:243
  36.3 8.0 %all-reduce = s32[4]{0:T(128)S(1)} all-reduce(s32[4]{0:T(128)S(1)} %dynamic-update-slice), channel_id=1, replica_groups=mesh['dp'=4,'fsdp'=8] {'dp'}, use_global_device_ids=true, to_apply=%add | all-reduce | flops 4 | bytes 32
  54.4 23.0 %all-gather.15.cloned.1.call-done = bf16[1024,768]{0,1:T(8,128)(2,1)} async-done(((bf16[128,768]{0,1:T(8,128)(2,1)}), bf16[1024,768]{0,1:T(8,128)(2,1)}) %all-gather.15.cloned.1.call-update) | async-done | bytes 1572880 | tf_op jit(solution)/shard_map/all_gather | solution.py:243
  77.4 5.6 convolution_add_fusion
  82.9 6.4 %reshape.381 = f32[4,256,3,4,64]{4,3,2,1,0:T(4,128)} reshape(f32[1024,768]{1,0:T(8,128)} %convolution_add_fusion) | data formatting | bytes 6291456 | tf_op jit(solution)/shard_map/reshape | solution.py:130
  124.9 21.7 %all-gather.19.cloned.1.call-done = bf16[1024,1024]{0,1:T(8,128)(2,1)} async-done(((bf16[128,1024]{0,1:T(8,128)(2,1)}), bf16[1024,1024]{0,1:T(8,128)(2,1)}) %all-gather.19.cloned.1.call-update) | async-done | bytes 2097168 | tf_op jit(solution)/shard_map/all_gather | solution.py:243
  146.6 14.6 %fusion.3 = (bf16[1024,1024]{1,0:T(8,128)(2,1)}, f32[1024,1024]{1,0:T(8,128)}) fusion(f32[1024]{0:T(1024)S(1)} %bitcast.220, bf16[1024,1024]{1,0:T(8,128)(2,1)} %get-tuple-element.89, bf16[1024,1024]{0,1:T(8,128)(2,1)} %all-gather.19.cloned.1.call-done), kind=kOutput, calls=%fused_computation.5 | convolution fusion | flops 2216689664 | bytes 10489856 | tf_op jit(solution)/shard_map/dot_general | solution.py:147
  161.2 15.7 %all-gather.21.cloned.1.call-done = bf16[1024,1024]{1,0:T(8,128)(2,1)} async-done(((bf16[128,1024]{1,0:T(8,128)(2,1)}), bf16[1024,1024]{1,0:T(8,128)(2,1)}) %all-gather.21.cloned.1.call-update) | async-done | bytes 2097168 | tf_op jit(solution)/shard_map/all_gather | solution.py:243
  176.8 8.0 %convert_reduce_fusion = (f32[1024]{0:T(1024)}, bf16[1024,1024]{1,0:T(8,128)(2,1)}) fusion(f32[1024,1024]{1,0:T(8,128)} %get-tuple-element.138, f32[1024]{0:T(1024)S(1)} %bitcast.221, bf16[1024,1024]{1,0:T(8,128)(2,1)} %fusion.10, bf16[1024,1024]{1,0:T(8,128)(2,1)} %all-gather.21.cloned.1.call-done), kind=kOutput, calls=%fused_computation.16 | convolution fusion | flops 2161114112 | bytes 10493952 | tf_op jit(solution)/shard_map/dot_general | solution.py:80
  184.9 30.0 %reduce-scatter.13.cloned.1.call-done = bf16[128,1024]{1,0:T(8,128)(2,1)} async-done(((bf16[1024,1024]{1,0:T(8,128)(2,1)}), bf16[128,1024]{1,0:T(8,128)(2,1)}) %reduce-scatter.13.cloned.1.call-update) | async-done | bytes 262160 | tf_op jit(solution)/shard_map/reduce_scatter | solution.py:314
  214.9 5.9 convolution_convert_fusion.1
  221.2 6.0 convolution_convert_fusion
  227.2 32.2 %all-reduce.4.cloned.1.call-done = bf16[128,1024]{1,0:T(8,128)(2,1)} async-done(((bf16[128,1024]{1,0:T(8,128)(2,1)}), bf16[128,1024]{1,0:T(8,128)(2,1)}) %all-reduce.4.cloned.1.call-update) | async-done | bytes 262160 | tf_op jit(solution)/shard_map/psum | solution.py:313
  262.5 35.6 %reduce-scatter.15.cloned.1.call-done = bf16[128,1024]{1,0:T(8,128)(2,1)} async-done(((bf16[1024,1024]{1,0:T(8,128)(2,1)}), bf16[128,1024]{1,0:T(8,128)(2,1)}) %reduce-scatter.15.cloned.1.call-update) | async-done | bytes 262160 | tf_op jit(solution)/shard_map/reduce_scatter | solution.py:307
  301.1 34.5 %reduce-scatter.17.cloned.1.call-done = bf16[128,1024]{1,0:T(8,128)(2,1)} async-done(((bf16[1024,1024]{1,0:T(8,128)(2,1)}), bf16[128,1024]{1,0:T(8,128)(2,1)}) %reduce-scatter.17.cloned.1.call-update) | async-done | bytes 262160 | tf_op jit(solution)/shard_map/reduce_scatter | solution.py:307
  335.7 29.7 %all-gather.17.cloned.1.call-done = bf16[1024,1024]{1,0:T(8,128)(2,1)} async-done(((bf16[128,1024]{1,0:T(8,128)(2,1)}), bf16[1024,1024]{1,0:T(8,128)(2,1)}) %all-gather.17.cloned.1.call-update) | async-done | bytes 2097168 | tf_op jit(solution)/shard_map/all_gather | solution.py:243
  422.1 7.5 %multiply_reduce_fusion.4 = (f32[]{:T(128)}, f32[]{:T(128)}, f32[512,1024]{1,0:T(8,128)}, f32[512,1024]{1,0:T(8,128)}) fusion(f32[512,1024]{1,0:T(8,128)} %param.24, bf16[512,1024]{1,0:T(8,128)(2,1)} %all-gather.27.cloned.1.call-done, f32[512,1024]{1,0:T(8,128)} %param.34, f32[512,1024]{1,0:T(8,128)} %param.29), kind=kLoop, calls=%fused_computation.61 | loop fusion | flops 7864318 | bytes 11534344 | tf_op jit(solution)/shard_map/reduce_sum | solution.py:92
  434.0 25.2 %reduce-scatter.11.cloned.1.call-done = bf16[128,768]{1,0:T(8,128)(2,1)} async-done(((bf16[1024,768]{1,0:T(8,128)(2,1)}), bf16[128,768]{1,0:T(8,128)(2,1)}) %reduce-scatter.11.cloned.1.call-update) | async-done | bytes 196624 | tf_op jit(solution)/shard_map/reduce_scatter | solution.py:307
  459.2 15.2 %all-gather = bf16[512,768]{1,0:T(8,128)(2,1)S(1)} all-gather(bf16[128,768]{1,0:T(8,128)(2,1)} %reduce-scatter.11.cloned.1.call-done), channel_id=2, replica_groups=mesh['dp'=4,'fsdp'=8] {'dp'}, dimensions={0}, use_global_device_ids=true | all-gather | bytes 983040 | tf_op jit(solution)/shard_map/all_gather | solution.py:308
  488.9 7.3 %reduce-scatter.9.cloned.1.call-done = bf16[256,1024]{1,0:T(8,128)(2,1)} async-done(((bf16[1024,1024]{1,0:T(8,128)(2,1)}), bf16[256,1024]{1,0:T(8,128)(2,1)}) %reduce-scatter.9.cloned.1.call-update) | async-done | bytes 524304 | tf_op jit(solution)/shard_map/reduce_scatter | solution.py:265
  497.7 37.1 %reduce-scatter.7.cloned.1.call-done = bf16[256,1024]{1,0:T(8,128)(2,1)} async-done(((bf16[1024,1024]{1,0:T(8,128)(2,1)}), bf16[256,1024]{1,0:T(8,128)(2,1)}) %reduce-scatter.7.cloned.1.call-update) | async-done | bytes 524304 | tf_op jit(solution)/shard_map/reduce_scatter | solution.py:264
  537.6 39.9 %psum.30 = f32[13312]{0:T(1024)S(1)} all-reduce(f32[13312]{0:T(1024)S(1)} %constant_dynamic-update-slice_fusion), channel_id=1, replica_groups=mesh['dp'=4,'fsdp'=8] {'dp','fsdp'}, use_global_device_ids=true, to_apply=%region_33.34 | all-reduce | flops 13312 | bytes 106496 | tf_op jit(solution)/shard_map/psum | solution.py:297
  587.8 14.7 %all-reduce.1 = (f32[5]{0:T(128)S(1)}, f32[5]{0:T(128)S(1)}) all-reduce(f32[5]{0:T(128)S(1)} %stack.81, f32[5]{0:T(128)S(1)} %stack.92), channel_id=1, replica_groups=mesh['dp'=4,'fsdp'=8] {'fsdp'}, use_global_device_ids=true, to_apply=%region_16.17 | all-reduce | flops 10 | bytes 80 | tf_op jit(solution)/shard_map/psum | solution.py:332
  618.6 5.4 multiply_subtract_fusion
  (270 shorter events, 167.4 us)
Async XLA Ops:
  7.2 40.8 %all-gather.13.cloned.1.call-start = ((), (), s32[]{:S(2)}) async-start(), calls=%async_computation.6 | async-start | bytes 2621440 | tf_op jit(solution)/shard_map/all_gather | solution.py:245
  7.9 69.4 %all-gather.15.cloned.1.call-start = ((), (), s32[]{:S(2)}) async-start(), calls=%async_computation.7 | async-start | bytes 1769472 | tf_op jit(solution)/shard_map/all_gather | solution.py:243
  12.9 102.3 %all-gather.23.cloned.1.call-start = ((), (), s32[]{:S(2)}) async-start(), calls=%async_computation.12 | async-start | bytes 2621440 | tf_op jit(solution)/shard_map/all_gather | solution.py:246
  13.6 133.0 %all-gather.19.cloned.1.call-start = ((), (), s32[]{:S(2)}) async-start(), calls=%async_computation.9 | async-start | bytes 2359296 | tf_op jit(solution)/shard_map/all_gather | solution.py:243
  15.2 161.6 %all-gather.21.cloned.1.call-start = ((), (), s32[]{:S(2)}) async-start(), calls=%async_computation.10 | async-start | bytes 2359296 | tf_op jit(solution)/shard_map/all_gather | solution.py:243
  17.1 197.8 %reduce-scatter.13.cloned.1.call-start = ((), (), s32[]{:S(2)}) async-start(), calls=%async_computation.15 | async-start | bytes 2359296 | tf_op jit(solution)/shard_map/reduce_scatter | solution.py:314
  120.6 138.8 %all-reduce.4.cloned.1.call-start = ((), (), s32[]{:S(2)}) async-start(), calls=%async_computation.16 | async-start | bytes 524288 | tf_op jit(solution)/shard_map/psum | solution.py:313
  214.9 83.3 %reduce-scatter.15.cloned.1.call-start = ((), (), s32[]{:S(2)}) async-start(), calls=%async_computation.17 | async-start | bytes 2359296 | tf_op jit(solution)/shard_map/reduce_scatter | solution.py:307
  220.9 114.7 %reduce-scatter.17.cloned.1.call-start = ((), (), s32[]{:S(2)}) async-start(), calls=%async_computation.18 | async-start | bytes 2359296 | tf_op jit(solution)/shard_map/reduce_scatter | solution.py:307
  227.1 32.3 %copy-start.27 = (f32[128,1024]{1,0:T(8,128)S(1)}, f32[128,1024]{1,0:T(8,128)}, u32[]{:S(2)}) copy-start(f32[128,1024]{1,0:T(8,128)} %param.32) | copy-start | bytes 1572868
  227.2 138.3 %all-gather.17.cloned.1.call-start = ((), (), s32[]{:S(2)}) async-start(), calls=%async_computation.8 | async-start | bytes 2359296 | tf_op jit(solution)/shard_map/all_gather | solution.py:243
  262.5 150.9 %all-gather.25.cloned.1.call-start = ((), (), s32[]{:S(2)}) async-start(), calls=%async_computation.19 | async-start | bytes 1310720 | tf_op jit(solution)/shard_map/all_gather | solution.py:308
  298.2 123.9 %all-gather.27.cloned.1.call-start = ((), (), s32[]{:S(2)}) async-start(), calls=%async_computation.20 | async-start | bytes 1310720 | tf_op jit(solution)/shard_map/all_gather | solution.py:308
  335.7 123.5 %reduce-scatter.11.cloned.1.call-start = ((), (), s32[]{:S(2)}) async-start(), calls=%async_computation.14 | async-start | bytes 1769472 | tf_op jit(solution)/shard_map/reduce_scatter | solution.py:307
  386.9 109.3 %reduce-scatter.9.cloned.1.call-start = ((), (), s32[]{:S(2)}) async-start(), calls=%async_computation.13 | async-start | bytes 2621440 | tf_op jit(solution)/shard_map/reduce_scatter | solution.py:265
  396.4 138.4 %reduce-scatter.7.cloned.1.call-start = ((), (), s32[]{:S(2)}) async-start(), calls=%async_computation.11 | async-start | bytes 2621440 | tf_op jit(solution)/shard_map/reduce_scatter | solution.py:264
  485.8 49.0 %copy-start.18 = (bf16[1,256,1024]{2,1,0:T(8,128)(2,1)S(1)}, bf16[1,256,1024]{2,1,0:T(8,128)(2,1)}, u32[]{:S(2)}) copy-start(bf16[1,256,1024]{2,1,0:T(8,128)(2,1)} %param.19) | copy-start | bytes 1572868
  485.8 49.0 %copy-start.45 = (f32[1024]{0:T(1024)S(1)}, f32[1024]{0:T(1024)}, u32[]{:S(2)}) copy-start(f32[1024]{0:T(1024)} %get-tuple-element.102) | copy-start | bytes 12292
  485.8 49.0 %copy-start.46 = (f32[1024]{0:T(1024)S(1)}, f32[1024]{0:T(1024)}, u32[]{:S(2)}) copy-start(f32[1024]{0:T(1024)} %get-tuple-element.103) | copy-start | bytes 12292
  488.9 88.5 %copy-start.37 = (f32[1664]{0:T(1024)S(1)}, f32[1664]{0:T(1024)}, u32[]{:S(2)}) copy-start(f32[1664]{0:T(1024)} %param.25) | copy-start | bytes 19972
  488.9 88.5 %copy-start.54 = (f32[1664]{0:T(1024)S(1)}, f32[1664]{0:T(1024)}, u32[]{:S(2)}) copy-start(f32[1664]{0:T(1024)} %param.35) | copy-start | bytes 19972
  488.9 88.5 %copy-start.55 = (f32[1664]{0:T(1024)S(1)}, f32[1664]{0:T(1024)}, u32[]{:S(2)}) copy-start(f32[1664]{0:T(1024)} %param.30) | copy-start | bytes 19972
  578.2 39.8 %copy-start.42 = (f32[1664]{0:T(1024)}, f32[1664]{0:T(1024)S(1)}, u32[]{:S(2)}) copy-start(f32[1664]{0:T(1024)S(1)} %get-tuple-element.75) | copy-start | bytes 19972
  578.2 39.8 %copy-start.43 = (f32[1664]{0:T(1024)}, f32[1664]{0:T(1024)S(1)}, u32[]{:S(2)}) copy-start(f32[1664]{0:T(1024)S(1)} %get-tuple-element.76) | copy-start | bytes 19972
  (50 other events, 277.9 us)
Sparse Core Ops, SparseCore 0:
  9.9 38.0 all-gather.12
  50.2 27.1 all-gather.14
  79.2 34.4 all-gather.22
  115.7 30.8 all-gather.18
  148.6 28.1 all-gather.20
  179.5 35.2 reduce-scatter.12
  217.8 41.5 all-reduce.3
  262.4 35.7 reduce-scatter.14
  301.2 34.4 reduce-scatter.16
  337.8 27.6 all-gather.16
  367.4 26.1 all-gather.24
  395.4 26.6 all-gather.26
  425.1 34.0 reduce-scatter.10
  462.8 33.3 reduce-scatter.8
  499.6 35.1 reduce-scatter.6

commit v3 on v2

--- a/solution.py
+++ b/solution.py
@@ -3,6 +3,8 @@
 import jax
 import jax.numpy as jnp
 from jax import lax
+from jax.experimental import pallas as pl
+from jax.experimental.pallas import tpu as pltpu
 from jax.sharding import PartitionSpec as P
 
 D = 1024
@@ -10,6 +12,7 @@
 HD = 64
 FF = 4096
 ROT = 16
+SMALL = 13312
 
 
 NORM_EPSILON = 1e-05
@@ -201,6 +204,734 @@
         tuple(term.astype(jnp.bfloat16) for term in terms),
         (norm_sums, d_qkv_bias, d_up_bias),
     )
+
+
+MESH_ID = pl.DeviceIdType.MESH
+HALF = 128
+
+
+class Place:
+    def __init__(self):
+        self.part = lax.axis_index("dp")
+        self.shard = lax.axis_index("fsdp")
+        self.z = self.shard // 2
+        self.core = self.shard % 2
+        self.x_part = 2 * (self.part // 2) + 1 - self.part % 2
+        self.y_part = (self.part + 2) % 4
+        self.far_part = 3 - self.part
+        self.across_x = (self.x_part, self.shard)
+        self.across_y = (self.y_part, self.shard)
+        self.across_far = (self.far_part, self.shard)
+        self.other_core = (self.part, 2 * self.z + 1 - self.core)
+        self.up = (self.part, jnp.minimum(self.shard + 2, 7))
+        self.down = (self.part, jnp.maximum(self.shard - 2, 0))
+
+    def shard_after(self, k):
+        return (self.part, (self.shard + k) % 8)
+
+
+def send(source, target, send_sem, recv_sem, device):
+    return pltpu.make_async_remote_copy(
+        src_ref=source,
+        dst_ref=target,
+        send_sem=send_sem,
+        recv_sem=recv_sem,
+        device_id=device,
+        device_id_type=MESH_ID,
+    )
+
+
+def arrived(target, recv_sem, device):
+    send(target, target, recv_sem, recv_sem, device).wait_recv()
+
+
+def sent(source, send_sem, device):
+    send(source, source, send_sem, send_sem, device).wait_send()
+
+
+def greet(at):
+    barrier = pltpu.get_barrier_semaphore()
+    peers = [at.across_x, at.across_y, at.across_far] + [at.shard_after(k) for k in range(1, 8)]
+    for peer in peers:
+        pl.semaphore_signal(barrier, inc=1, device_id=peer, device_id_type=MESH_ID)
+    pl.semaphore_wait(barrier, len(peers))
+
+
+def gather_kernel(
+    x_own,
+    cot_own,
+    len_own,
+    w_own,
+    out_own,
+    small_own,
+    x_all,
+    cot_all,
+    len_all,
+    w_all,
+    out_all,
+    small_all,
+    plane_send,
+    plane_recv,
+    len_send,
+    len_recv,
+    w_send,
+    w_recv,
+    out_send,
+    out_recv,
+    small_send,
+    small_recv,
+):
+    at = Place()
+    z, core, part, shard = at.z, at.core, at.part, at.shard
+    greet(at)
+    spans = ((0, 768), (768, 1792), (1792, 2816))
+
+    def piece(ref, slot, n):
+        return ref.at[slot, :, spans[n][0] : spans[n][1]]
+
+    for n, (low, high) in enumerate(spans):
+        own = w_own.at[:, low:high]
+        target = piece(w_all, shard, n)
+
+        @pl.when(z < 3)
+        def _():
+            send(own, target, w_send.at[0, n, z], w_recv.at[n, shard], at.up).start()
+
+        @pl.when(z > 0)
+        def _():
+            send(own, target, w_send.at[1, n, z], w_recv.at[n, shard], at.down).start()
+
+        send(own, target, w_send.at[2, n, z], w_recv.at[n, shard], at.other_core).start()
+
+    @pl.when(z == part)
+    def _():
+        @pl.when(z < 3)
+        def _():
+            send(out_own, out_all.at[core], out_send.at[0], out_recv.at[core], at.up).start()
+
+        @pl.when(z > 0)
+        def _():
+            send(out_own, out_all.at[core], out_send.at[1], out_recv.at[core], at.down).start()
+
+        send(out_own, out_all.at[core], out_send.at[2], out_recv.at[core], at.other_core).start()
+        out_all[core] = out_own[...]
+
+    activations = ((x_own, x_all), (cot_own, cot_all))
+    for n, (own, whole) in enumerate(activations):
+        send(own, whole.at[part], plane_send.at[n, 0], plane_recv.at[n, 0], at.across_x).start()
+        send(own, whole.at[part], plane_send.at[n, 1], plane_recv.at[n, 1], at.across_y).start()
+    for n, peer in enumerate((at.across_x, at.across_y, at.across_far)):
+        send(len_own, len_all.at[part], len_send.at[n], len_recv.at[n], peer).start()
+    for k in range(1, 8):
+        send(
+            small_own,
+            small_all.at[shard],
+            small_send.at[k - 1],
+            small_recv.at[k - 1],
+            at.shard_after(k),
+        ).start()
+    x_all[part] = x_own[...]
+    cot_all[part] = cot_own[...]
+    len_all[part] = len_own[...]
+    w_all[shard] = w_own[...]
+    small_all[shard] = small_own[...]
+
+    for n in range(3):
+        for k in range(1, 4):
+
+            @pl.when(z >= k)
+            def _():
+                source = 2 * (z - k) + core
+                block = piece(w_all, source, n)
+                arrived(block, w_recv.at[n, source], at.down)
+
+                @pl.when(z < 3)
+                def _():
+                    send(block, block, w_send.at[0, n, z - k], w_recv.at[n, source], at.up).start()
+
+                send(
+                    block, block, w_send.at[2, n, z - k], w_recv.at[n, source], at.other_core
+                ).start()
+
+            @pl.when(z + k <= 3)
+            def _():
+                source = 2 * (z + k) + core
+                block = piece(w_all, source, n)
+                arrived(block, w_recv.at[n, source], at.up)
+
+                @pl.when(z > 0)
+                def _():
+                    send(
+                        block, block, w_send.at[1, n, z + k], w_recv.at[n, source], at.down
+                    ).start()
+
+                send(
+                    block, block, w_send.at[2, n, z + k], w_recv.at[n, source], at.other_core
+                ).start()
+
+    @pl.when(z != part)
+    def _():
+        block = out_all.at[core]
+        arrived(block, out_recv.at[core], at.up)
+
+        @pl.when((z > part) & (z < 3))
+        def _():
+            send(block, block, out_send.at[0], out_recv.at[core], at.up).start()
+
+        @pl.when((z < part) & (z > 0))
+        def _():
+            send(block, block, out_send.at[1], out_recv.at[core], at.down).start()
+
+        send(block, block, out_send.at[2], out_recv.at[core], at.other_core).start()
+
+    for n, (_, whole) in enumerate(activations):
+        arrived(whole.at[at.x_part], plane_recv.at[n, 0], at.across_x)
+        block = whole.at[at.x_part, 0:HALF]
+        send(block, block, plane_send.at[n, 2], plane_recv.at[n, 2], at.across_y).start()
+        arrived(whole.at[at.y_part], plane_recv.at[n, 1], at.across_y)
+        block = whole.at[at.y_part, HALF : 2 * HALF]
+        send(block, block, plane_send.at[n, 3], plane_recv.at[n, 3], at.across_x).start()
+
+    for n, (own, whole) in enumerate(activations):
+        arrived(whole.at[at.far_part, 0:HALF], plane_recv.at[n, 2], at.across_y)
+        arrived(whole.at[at.far_part, HALF : 2 * HALF], plane_recv.at[n, 3], at.across_x)
+        sent(own, plane_send.at[n, 0], at.across_x)
+        sent(own, plane_send.at[n, 1], at.across_y)
+        sent(whole.at[at.x_part, 0:HALF], plane_send.at[n, 2], at.across_y)
+        sent(whole.at[at.y_part, HALF : 2 * HALF], plane_send.at[n, 3], at.across_x)
+    for n, (peer, other) in enumerate(
+        ((at.across_x, at.x_part), (at.across_y, at.y_part), (at.across_far, at.far_part))
+    ):
+        arrived(len_all.at[other], len_recv.at[n], peer)
+        sent(len_own, len_send.at[n], peer)
+    for k in range(1, 8):
+        arrived(small_all.at[(shard + 8 - k) % 8], small_recv.at[k - 1], at.shard_after(8 - k))
+        sent(small_own, small_send.at[k - 1], at.shard_after(k))
+    for n in range(3):
+        for other in range(4):
+            block = piece(w_all, 2 * other + 1 - core, n)
+            arrived(block, w_recv.at[n, 2 * other + 1 - core], at.other_core)
+            sent(block, w_send.at[2, n, other], at.other_core)
+
+            @pl.when((other <= z) & (z < 3))
+            def _():
+                sent(block, w_send.at[0, n, other], at.up)
+
+            @pl.when((other >= z) & (z > 0))
+            def _():
+                sent(block, w_send.at[1, n, other], at.down)
+
+    arrived(out_all.at[1 - core], out_recv.at[1 - core], at.other_core)
+    sent(out_own, out_send.at[2], at.other_core)
+
+    @pl.when((z >= part) & (z < 3))
+    def _():
+        sent(out_own, out_send.at[0], at.up)
+
+    @pl.when((z <= part) & (z > 0))
+    def _():
+        sent(out_own, out_send.at[1], at.down)
+
+
+VMEM_SPEC = pl.BlockSpec(memory_space=pltpu.VMEM)
+
+
+def gather(x_own, cot_own, len_own, w_own, out_own, small_own):
+    shape = jax.ShapeDtypeStruct
+    dma = pltpu.SemaphoreType.DMA
+    return pl.pallas_call(
+        gather_kernel,
+        out_shape=(
+            shape((4,) + x_own.shape, jnp.bfloat16),
+            shape((4,) + x_own.shape, jnp.bfloat16),
+            shape((4,) + len_own.shape, jnp.float32),
+            shape((8,) + w_own.shape, jnp.bfloat16),
+            shape((2,) + out_own.shape, jnp.bfloat16),
+            shape((8,) + small_own.shape, jnp.float32),
+        ),
+        in_specs=[VMEM_SPEC] * 6,
+        out_specs=(VMEM_SPEC,) * 6,
+        scratch_shapes=[
+            dma((2, 4)),
+            dma((2, 4)),
+            dma((3,)),
+            dma((3,)),
+            dma((3, 3, 4)),
+            dma((3, 8)),
+            dma((3,)),
+            dma((2,)),
+            dma((7,)),
+            dma((7,)),
+        ],
+        compiler_params=pltpu.CompilerParams(
+            collective_id=0, has_side_effects=True, vmem_limit_bytes=60 << 20
+        ),
+        name="gather",
+    )(x_own, cot_own, len_own, w_own, out_own, small_own)
+
+
+def reduce_kernel(
+    out_part,
+    dx_part,
+    terms,
+    out_term,
+    small_part,
+    out_sum,
+    dx_sum,
+    terms_all,
+    out_grad,
+    small_sum,
+    plane_one,
+    plane_two,
+    plane_turn,
+    core_in,
+    line_sum,
+    line_in,
+    out_core_in,
+    out_line,
+    out_line_in,
+    small_in,
+    small_own,
+    small_plane,
+    plane_send,
+    plane_recv,
+    core_send,
+    core_recv,
+    line_send,
+    line_recv,
+    out_send,
+    out_recv,
+    all_send,
+    all_recv,
+    small_send,
+    small_recv,
+):
+    at = Place()
+    z, core, part, shard = at.z, at.core, at.part, at.shard
+    greet(at)
+    spans = ((1792, 2816), (768, 1792), (0, 768))
+    first, second = slice(0, HALF), slice(HALF, 2 * HALF)
+    f32, bf16 = jnp.float32, jnp.bfloat16
+
+    for n, (low, high) in enumerate(spans):
+        for other in range(4):
+            send(
+                terms.at[2 * other + 1 - core, :, low:high],
+                core_in.at[other, :, low:high],
+                core_send.at[n, other],
+                core_recv.at[n, other],
+                at.other_core,
+            ).start()
+    send(out_term.at[1 - core], out_core_in, out_send.at[0], out_recv.at[0], at.other_core).start()
+    for k in range(1, 8):
+        send(
+            small_part.at[(shard + k) % 8],
+            small_in.at[k - 1],
+            small_send.at[k - 1],
+            small_recv.at[k - 1],
+            at.shard_after(k),
+        ).start()
+
+    parts = (out_part, dx_part)
+    routes = (
+        (first, at.across_x, at.x_part, at.across_y, at.y_part),
+        (second, at.across_y, at.y_part, at.across_x, at.x_part),
+    )
+    for n, term in enumerate(parts):
+        for r, (rows, peer, peer_part, _, _) in enumerate(routes):
+            for m, target in enumerate((at.far_part, peer_part)):
+                send(
+                    term.at[target, rows],
+                    plane_one.at[n, r, m],
+                    plane_send.at[n, r, m],
+                    plane_recv.at[n, r, m],
+                    peer,
+                ).start()
+
+    def forward(n, target):
+        low, high = spans[n]
+        block = line_sum.at[target, :, low:high]
+
+        @pl.when(z < target)
+        def _():
+            @pl.when(z > 0)
+            def _():
+                arrived(line_in.at[target, :, low:high], line_recv.at[n, target], at.down)
+                block[...] = (
+                    block[...].astype(f32) + line_in[target, :, low:high].astype(f32)
+                ).astype(bf16)
+
+            send(
+                block,
+                line_in.at[target, :, low:high],
+                line_send.at[n, target],
+                line_recv.at[n, target],
+                at.up,
+            ).start()
+
+        @pl.when(z > target)
+        def _():
+            @pl.when(z < 3)
+            def _():
+                arrived(line_in.at[target, :, low:high], line_recv.at[n, target], at.up)
+                block[...] = (
+                    block[...].astype(f32) + line_in[target, :, low:high].astype(f32)
+                ).astype(bf16)
+
+            @pl.when(z - 1 == target)
+            def _():
+                send(
+                    block,
+                    line_in.at[4, :, low:high],
+                    line_send.at[n, target],
+                    line_recv.at[n, 4],
+                    at.down,
+                ).start()
+
+            @pl.when(z - 1 > target)
+            def _():
+                send(
+                    block,
+                    line_in.at[target, :, low:high],
+                    line_send.at[n, target],
+                    line_recv.at[n, target],
+                    at.down,
+                ).start()
+
+    def own_line(n):
+        low, high = spans[n]
+        block = line_sum.at[z, :, low:high]
+
+        @pl.when(z > 0)
+        def _():
+            arrived(line_in.at[z, :, low:high], line_recv.at[n, z], at.down)
+            block[...] = (block[...].astype(f32) + line_in[z, :, low:high].astype(f32)).astype(bf16)
+
+        @pl.when(z < 3)
+        def _():
+            arrived(line_in.at[4, :, low:high], line_recv.at[n, 4], at.up)
+            block[...] = (block[...].astype(f32) + line_in[4, :, low:high].astype(f32)).astype(bf16)
+
+        terms_all[part, :, low:high] = block[...]
+        own = terms_all.at[part, :, low:high]
+        send(own, own, all_send.at[n, 0], all_recv.at[n, 0], at.across_x).start()
+        send(own, own, all_send.at[n, 1], all_recv.at[n, 1], at.across_y).start()
+
+    for n, (low, high) in enumerate(spans):
+        for other in (3, 0, 2, 1):
+            arrived(core_in.at[other, :, low:high], core_recv.at[n, other], at.other_core)
+            line_sum[other, :, low:high] = (
+                terms[2 * other + core, :, low:high].astype(f32)
+                + core_in[other, :, low:high].astype(f32)
+            ).astype(bf16)
+        for target in (3, 0, 2, 1):
+            forward(n, target)
+
+    arrived(out_core_in, out_recv.at[0], at.other_core)
+    out_line[...] = (out_term[core].astype(f32) + out_core_in[...].astype(f32)).astype(bf16)
+
+    @pl.when((z < part) & (z > 0))
+    def _():
+        arrived(out_line_in.at[0], out_recv.at[1], at.down)
+        out_line[...] = (out_line[...].astype(f32) + out_line_in[0].astype(f32)).astype(bf16)
+
+    @pl.when((z > part) & (z < 3))
+    def _():
+        arrived(out_line_in.at[1], out_recv.at[2], at.up)
+        out_line[...] = (out_line[...].astype(f32) + out_line_in[1].astype(f32)).astype(bf16)
+
+    @pl.when(z < part)
+    def _():
+        send(out_line, out_line_in.at[0], out_send.at[1], out_recv.at[1], at.up).start()
+
+    @pl.when(z > part)
+    def _():
+        send(out_line, out_line_in.at[1], out_send.at[1], out_recv.at[2], at.down).start()
+
+    for n, term in enumerate(parts):
+        for r, (rows, peer, _, turn, turn_part) in enumerate(routes):
+            arrived(plane_one.at[n, r, 0], plane_recv.at[n, r, 0], peer)
+            plane_turn[n, r] = (
+                term[turn_part, rows].astype(f32) + plane_one[n, r, 0].astype(f32)
+            ).astype(bf16)
+            send(
+                plane_turn.at[n, r],
+                plane_two.at[n, r],
+                plane_send.at[n, r, 2],
+                plane_recv.at[n, r, 2],
+                turn,
+            ).start()
+
+    total = small_part[shard]
+    for k in range(1, 8):
+        arrived(small_in.at[k - 1], small_recv.at[k - 1], at.shard_after(8 - k))
+        total = total + small_in[k - 1]
+    small_own[...] = total
+    plane_peers = (
+        (at.across_x, at.x_part),
+        (at.across_y, at.y_part),
+        (at.across_far, at.far_part),
+    )
+    for n, (peer, _) in enumerate(plane_peers):
+        send(
+            small_own, small_plane.at[part], small_send.at[7 + n], small_recv.at[7 + n], peer
+        ).start()
+    small_plane[part] = total
+
+    for n, (term, result) in enumerate(((out_part, out_sum), (dx_part, dx_sum))):
+        for r, (rows, peer, _, turn, _) in enumerate(routes):
+            arrived(plane_one.at[n, r, 1], plane_recv.at[n, r, 1], peer)
+            arrived(plane_two.at[n, r], plane_recv.at[n, r, 2], turn)
+            result[rows] = (
+                term[part, rows].astype(f32)
+                + plane_one[n, r, 1].astype(f32)
+                + plane_two[n, r].astype(f32)
+            )
+
+    for n in range(3):
+        own_line(n)
+
+    @pl.when(z == part)
+    def _():
+        @pl.when(z > 0)
+        def _():
+            arrived(out_line_in.at[0], out_recv.at[1], at.down)
+            out_line[...] = (out_line[...].astype(f32) + out_line_in[0].astype(f32)).astype(bf16)
+
+        @pl.when(z < 3)
+        def _():
+            arrived(out_line_in.at[1], out_recv.at[2], at.up)
+            out_line[...] = (out_line[...].astype(f32) + out_line_in[1].astype(f32)).astype(bf16)
+
+        for n, (peer, _) in enumerate(plane_peers):
+            send(out_line, out_grad, out_send.at[2 + n], out_recv.at[3], peer).start()
+        out_grad[...] = out_line[...]
+
+    @pl.when(z != part)
+    def _():
+        arrived(out_grad, out_recv.at[3], at.across_x)
+
+    for n, (low, high) in enumerate(spans):
+        arrived(terms_all.at[at.x_part, :, low:high], all_recv.at[n, 0], at.across_x)
+        block = terms_all.at[at.x_part, 0:64, low:high]
+        send(block, block, all_send.at[n, 2], all_recv.at[n, 2], at.across_y).start()
+        arrived(terms_all.at[at.y_part, :, low:high], all_recv.at[n, 1], at.across_y)
+        block = terms_all.at[at.y_part, 64:128, low:high]
+        send(block, block, all_send.at[n, 3], all_recv.at[n, 3], at.across_x).start()
+
+    for n, (peer, other) in enumerate(plane_peers):
+        arrived(small_plane.at[other], small_recv.at[7 + n], peer)
+    small_sum[...] = (small_plane[0] + small_plane[1]) + (small_plane[2] + small_plane[3])
+
+    for n, (low, high) in enumerate(spans):
+        arrived(terms_all.at[at.far_part, 0:64, low:high], all_recv.at[n, 2], at.across_y)
+        arrived(terms_all.at[at.far_part, 64:128, low:high], all_recv.at[n, 3], at.across_x)
+        whole = terms_all.at[part, :, low:high]
+        sent(whole, all_send.at[n, 0], at.across_x)
+        sent(whole, all_send.at[n, 1], at.across_y)
+        sent(terms_all.at[part, 0:64, low:high], all_send.at[n, 2], at.across_y)
+        sent(terms_all.at[part, 64:128, low:high], all_send.at[n, 3], at.across_x)
+        for other in range(4):
+            block = line_sum.at[other, :, low:high]
+            sent(block, core_send.at[n, other], at.other_core)
+
+            @pl.when(z != other)
+            def _():
+                sent(block, line_send.at[n, other], at.up)
+
+    for n in range(2):
+        for r in range(2):
+            for m in range(3):
+                sent(plane_turn.at[n, r], plane_send.at[n, r, m], at.across_x)
+    sent(out_line, out_send.at[0], at.other_core)
+
+    @pl.when(z != part)
+    def _():
+        sent(out_line, out_send.at[1], at.up)
+
+    @pl.when(z == part)
+    def _():
+        for n, (peer, _) in enumerate(plane_peers):
+            sent(out_line, out_send.at[2 + n], peer)
+
+    for k in range(1, 8):
+        sent(small_own, small_send.at[k - 1], at.shard_after(k))
+    for n, (peer, _) in enumerate(plane_peers):
+        sent(small_own, small_send.at[7 + n], peer)
+
+
+def reduce(out_part, dx_part, terms, out_term, small_part):
+    shape = jax.ShapeDtypeStruct
+    dma = pltpu.SemaphoreType.DMA
+    vmem = pltpu.VMEM
+    _, length, width = out_part.shape
+    _, rows, wide = terms.shape
+    bf16, f32 = jnp.bfloat16, jnp.float32
+    small = small_part.shape[1:]
+    return pl.pallas_call(
+        reduce_kernel,
+        out_shape=(
+            shape((length, width), f32),
+            shape((length, width), f32),
+            shape((4, rows, wide), bf16),
+            shape((rows, width), bf16),
+            shape(small, f32),
+        ),
+        in_specs=[VMEM_SPEC] * 5,
+        out_specs=(VMEM_SPEC,) * 5,
+        scratch_shapes=[
+            vmem((2, 2, 2, HALF, width), bf16),
+            vmem((2, 2, HALF, width), bf16),
+            vmem((2, 2, HALF, width), bf16),
+            vmem((4, rows, wide), bf16),
+            vmem((4, rows, wide), bf16),
+            vmem((5, rows, wide), bf16),
+            vmem((rows, width), bf16),
+            vmem((rows, width), bf16),
+            vmem((2, rows, width), bf16),
+            vmem((7,) + small, f32),
+            vmem(small, f32),
+            vmem((4,) + small, f32),
+            dma((2, 2, 3)),
+            dma((2, 2, 3)),
+            dma((3, 4)),
+            dma((3, 4)),
+            dma((3, 4)),
+            dma((3, 5)),
+            dma((5,)),
+            dma((4,)),
+            dma((3, 4)),
+            dma((3, 4)),
+            dma((10,)),
+            dma((10,)),
+        ],
+        compiler_params=pltpu.CompilerParams(
+            collective_id=1, has_side_effects=True, vmem_limit_bytes=60 << 20
+        ),
+        name="reduce",
+    )(out_part, dx_part, terms, out_term, small_part)
+
+
+def nt(a,b): return lax.dot_general(a,b,(((1,),(1,)),((),())),preferred_element_type=jnp.float32)
+def tn(a,b): return lax.dot_general(a,b,(((0,),(0,)),((),())),preferred_element_type=jnp.float32)
+def nn(a,b): return jnp.dot(a,b,preferred_element_type=jnp.float32)
+def flat(v): return v.reshape(v.shape[0]*v.shape[1], v.shape[2])
+
+def compute_kernel(x_ref,cot_ref,len_ref,w_ref,wout_ref,gains_ref,qb_ref,ub_ref,tab_ref,
+                   outp_ref,dxp_ref,g_ref,gout_ref,sums_ref,dqb_ref,dub_ref,
+                   unit_s,n1_s,n2_s,back_s,mix_s,dp_s,act_s,dh_s,sc_s):
+    group,length,_=x_ref.shape
+    hc=wout_ref.shape[0]*wout_ref.shape[1]
+    nh=hc//HD
+    Q=3*hc; U=ub_ref.shape[1]
+    RB=64
+    sums_ref[...]=jnp.zeros_like(sums_ref); dqb_ref[...]=jnp.zeros_like(dqb_ref); dub_ref[...]=jnp.zeros_like(dub_ref)
+    row=lax.broadcasted_iota(jnp.int32,(length,length),0)
+    col=lax.broadcasted_iota(jnp.int32,(length,length),1)
+    causal=col<=row
+    lane=lax.broadcasted_iota(jnp.int32,(length,hc),1)
+    def norm_rows(s):
+        @pl.loop(0,length//RB)
+        def _(i):
+            r=pl.ds(pl.multiple_of(i*RB,RB),RB)
+            x=x_ref[s,r,:].astype(jnp.float32)
+            mean=jnp.mean(x,axis=-1,keepdims=True)
+            c=x-mean
+            var=jnp.mean(c*c,axis=-1,keepdims=True)
+            u=c*lax.rsqrt(var+1e-5)
+            unit_s[s,r,:]=u
+            n1_s[s,r,:]=(u*gains_ref[0:1]+gains_ref[1:2]).astype(jnp.bfloat16)
+            n2_s[s,r,:]=(u*gains_ref[2:3]+gains_ref[3:4]).astype(jnp.bfloat16)
+            rows=lax.broadcasted_iota(jnp.int32,(RB,1),0)+i*RB
+            live=rows.astype(jnp.float32)<len_ref[s][0:1,0:1]
+            back_s[s,r,:]=jnp.where(live,cot_ref[s,r,:],jnp.zeros((),jnp.bfloat16))
+    def attn(s):
+        norm_rows(s)
+        w=flat(w_ref[:,:,0:Q])
+        wout=flat(wout_ref[...])
+        p=nn(n1_s[s],w)+qb_ref[...]
+        C=tab_ref[0];S1=tab_ref[1];S2=tab_ref[2]
+        def rot(v): return v*C+pltpu.roll(v,hc-8,1)*S1+pltpu.roll(v,8,1)*S2
+        def rotb(v): return v*C-pltpu.roll(v,hc-8,1)*S1-pltpu.roll(v,8,1)*S2
+        q=rot(p[:,0:hc]).astype(jnp.bfloat16); k=rot(p[:,hc:2*hc]).astype(jnp.bfloat16); v=p[:,2*hc:].astype(jnp.bfloat16)
+        back=back_s[s]
+        dm=nt(back,wout).astype(jnp.bfloat16)
+        allowed=causal&(col.astype(jnp.float32)<len_ref[s][0:1,0:1])
+        zero=jnp.zeros((),jnp.bfloat16)
+        mixed=jnp.zeros((length,hc),jnp.float32); dq=mixed; dk=mixed; dv=mixed
+        for h in range(nh):
+            m=(lane>=h*HD)&(lane<(h+1)*HD)
+            qh=jnp.where(m,q,zero);kh=jnp.where(m,k,zero);vh=jnp.where(m,v,zero);dmh=jnp.where(m,dm,zero)
+            sc=jnp.where(allowed,nt(qh,k)*HD**-0.5,-1e30)
+            e=jnp.exp(sc-jnp.max(sc,axis=-1,keepdims=True))
+            A=e*(1.0/jnp.sum(e,axis=-1,keepdims=True))
+            Ab=A.astype(jnp.bfloat16)
+            mixed=mixed+nn(Ab,vh)
+            dA=nt(dmh,v)
+            dS=(A*(dA-jnp.sum(A*dA,axis=-1,keepdims=True))).astype(jnp.bfloat16)
+            dq=dq+nn(dS,kh); dk=dk+tn(dS,qh); dv=dv+tn(Ab,dmh)
+        mix_s[s]=mixed.astype(jnp.bfloat16)
+        dq=rotb(dq*HD**-0.5).astype(jnp.bfloat16); dk=rotb(dk*HD**-0.5).astype(jnp.bfloat16); dv=dv.astype(jnp.bfloat16)
+        dp_s[s,:,0:hc]=dq; dp_s[s,:,hc:2*hc]=dk; dp_s[s,:,2*hc:]=dv
+        for i,t in enumerate((dq,dk,dv)):
+            dqb_ref[:,i*hc:(i+1)*hc]+=jnp.sum(t.astype(jnp.float32),axis=0,keepdims=True)
+        dn=nt(dp_s[s],w)
+        sums_ref[0:1]+=jnp.sum(dn*unit_s[s],axis=0,keepdims=True)
+        sums_ref[1:2]+=jnp.sum(dn,axis=0,keepdims=True)
+        sc_s[s]=dn*gains_ref[0:1]
+    @pl.loop(0,group)
+    def _(s): attn(s)
+    def grads(lhs_s,rhs,lo,hi):
+        @pl.loop(0,w_ref.shape[0])
+        def _(f):
+            c=pl.ds(pl.multiple_of(f*128,128),128)
+            g_ref[f,:,lo:hi]=tn(flat(lhs_s[:,:,c]),rhs).astype(jnp.bfloat16)
+    for i in range(wout_ref.shape[0]):
+        gout_ref[i]=tn(flat(mix_s[:,:,i*128:(i+1)*128]),flat(back_s[...])).astype(jnp.bfloat16)
+    grads(n1_s,flat(dp_s[...]),0,Q)
+    def mlp(s):
+        wup=flat(w_ref[:,:,Q:Q+U]); wdown=flat(w_ref[:,:,Q+U:])
+        h=nn(n2_s[s],wup)+ub_ref[...]
+        cdf=0.5*(1.0+lax.erf(h*2.0**-0.5))
+        act=(h*cdf).astype(jnp.bfloat16)
+        act_s[s]=act
+        slope=cdf+h*jnp.exp(-0.5*h*h)*(2*math.pi)**-0.5
+        outp_ref[s]=(nn(act,wdown)+nn(mix_s[s],flat(wout_ref[...]))).astype(jnp.bfloat16)
+        dh=(nt(back_s[s],wdown)*slope).astype(jnp.bfloat16)
+        dh_s[s]=dh
+        dub_ref[...]+=jnp.sum(dh.astype(jnp.float32),axis=0,keepdims=True)
+        dn=nt(dh,wup)
+        sums_ref[2:3]+=jnp.sum(dn*unit_s[s],axis=0,keepdims=True)
+        sums_ref[3:4]+=jnp.sum(dn,axis=0,keepdims=True)
+        dxp_ref[s]=(sc_s[s]+dn*gains_ref[2:3]).astype(jnp.bfloat16)
+    @pl.loop(0,group)
+    def _(s): mlp(s)
+    grads(n2_s,flat(dh_s[...]),Q,Q+U)
+    grads(act_s,flat(back_s[...]),Q+U,Q+2*U)
+
+def rope_tables(length, heads):
+    cosine, sine = (table[:, 0] for table in rotary_tables(length))
+    rest = (length, HD - ROT)
+    none = jnp.zeros_like(sine)
+    tables = (
+        jnp.concatenate([cosine, cosine, jnp.ones(rest)], axis=1),
+        jnp.concatenate([-sine, none, jnp.zeros(rest)], axis=1),
+        jnp.concatenate([none, sine, jnp.zeros(rest)], axis=1),
+    )
+    return jnp.stack([jnp.tile(table, (1, heads)) for table in tables])
+
+
+def compute(x_all,cot_all,lens,w_all,wout,gains,qb,ub,tab):
+    group,length,_=x_all.shape
+    Q=qb.shape[1];U=ub.shape[1];hc=Q//3
+    V=pl.BlockSpec(memory_space=pltpu.VMEM)
+    S=jax.ShapeDtypeStruct
+    big=lambda w,t: pltpu.VMEM((group,length,w),t)
+    return pl.pallas_call(compute_kernel,
+        out_shape=(S((group,length,D),jnp.bfloat16),S((group,length,D),jnp.bfloat16),S(w_all.shape,jnp.bfloat16),S(wout.shape,jnp.bfloat16),S((4,D),jnp.float32),S((1,Q),jnp.float32),S((1,U),jnp.float32)),
+        in_specs=[V]*9,out_specs=(V,)*7,
+        scratch_shapes=[big(D,jnp.float32),big(D,jnp.bfloat16),big(D,jnp.bfloat16),big(D,jnp.bfloat16),big(hc,jnp.bfloat16),big(Q,jnp.bfloat16),big(U,jnp.bfloat16),big(U,jnp.bfloat16),big(D,jnp.float32)],
+        compiler_params=pltpu.CompilerParams(vmem_limit_bytes=62<<20),name="compute")(x_all,cot_all,lens,w_all,wout,gains,qb,ub,tab)
 
 
 def local_split(
@@ -238,45 +969,70 @@
     down_own = lax.dynamic_slice_in_dim(down_master, part * ff_rows, ff_rows).astype(jnp.bfloat16)
     out_own = out_master.astype(jnp.bfloat16)
     small_own = small_master.astype(jnp.bfloat16)
-
-    def over_shards(own):
-        return lax.all_gather(own, "fsdp", axis=0, tiled=True)
-
-    x_all = lax.all_gather(tokens_in, "dp", axis=0, tiled=True)
-    cotangent_all = lax.all_gather(cotangent, "dp", axis=0, tiled=True)
-    lengths_all = lax.all_gather(lengths, "dp", axis=0, tiled=True)
-    qkv_weight, up_weight, down_weight = (over_shards(w) for w in (qkv_own, up_own, down_own))
-    out_weight = lax.dynamic_slice_in_dim(over_shards(out_own), part * head_cols, head_cols)
-    gain_one, shift_one, gain_two, shift_two, qkv_bias, out_bias, up_bias, down_bias = split_small(
-        over_shards(small_own).astype(jnp.float32)
-    )
-    qkv_bias = sliced(qkv_bias[None], part, parts, 3)[0]
-    up_bias = sliced(up_bias[None], part, parts, shards)[0]
-
-    out_part, scaled_part, terms, sums = layer(
-        x_all,
-        cotangent_all,
-        lengths_all,
-        (qkv_weight, out_weight, up_weight, down_weight),
-        (gain_one, shift_one, gain_two, shift_two, qkv_bias, up_bias),
-        part,
-    )
-    out_sum = lax.psum_scatter(out_part, "dp", scatter_dimension=0, tiled=True)
-    scaled = lax.psum_scatter(scaled_part, "dp", scatter_dimension=0, tiled=True)
-    out_sum, scaled = out_sum.astype(jnp.float32), scaled.astype(jnp.float32)
+    own = (parts, shards) == (4, 8)
+
+    def small_vectors(small_all):
+        vectors = split_small(small_all)
+        vectors[4] = sliced(vectors[4][None], part, parts, 3)[0]
+        vectors[6] = sliced(vectors[6][None], part, parts, shards)[0]
+        return vectors
+
+    if own:
+        small_rows = small_master.shape[0]
+        padded = jnp.pad(small_own.astype(jnp.float32), (0, 2048 - small_rows)).reshape(16, 128)
+        x_all, cotangent_all, lengths_all, w_all, out_all, small_all = gather(
+            tokens_in[0],
+            cotangent[0],
+            jnp.broadcast_to(lengths.astype(jnp.float32)[:, None], (8, 128)),
+            jnp.concatenate([qkv_own, up_own, down_own], axis=1),
+            out_own,
+            padded,
+        )
+        small_all = small_all.reshape(shards, 2048)[:, :small_rows].reshape(SMALL)
+        gain_one, shift_one, gain_two, shift_two, qkv_bias, out_bias, up_bias, down_bias = (
+            small_vectors(small_all)
+        )
+        out_part, scaled_part, terms, out_term, norm_sums, d_qkv_bias, d_up_bias = compute(
+            x_all,
+            cotangent_all,
+            lengths_all,
+            w_all,
+            out_all,
+            jnp.stack([gain_one, shift_one, gain_two, shift_two]),
+            qkv_bias[None],
+            up_bias[None],
+            rope_tables(length, head_cols // HD),
+        )
+        d_qkv_bias, d_up_bias = d_qkv_bias[0], d_up_bias[0]
+    else:
+
+        def over_shards(own):
+            return lax.all_gather(own, "fsdp", axis=0, tiled=True)
+
+        x_all = lax.all_gather(tokens_in, "dp", axis=0, tiled=True)
+        cotangent_all = lax.all_gather(cotangent, "dp", axis=0, tiled=True)
+        lengths_all = lax.all_gather(lengths, "dp", axis=0, tiled=True)
+        qkv_weight, up_weight, down_weight = (over_shards(w) for w in (qkv_own, up_own, down_own))
+        out_weight = lax.dynamic_slice_in_dim(over_shards(out_own), part * head_cols, head_cols)
+        gain_one, shift_one, gain_two, shift_two, qkv_bias, out_bias, up_bias, down_bias = (
+            small_vectors(over_shards(small_own).astype(jnp.float32))
+        )
+        out_part, scaled_part, terms, sums = layer(
+            x_all,
+            cotangent_all,
+            lengths_all,
+            (qkv_weight, out_weight, up_weight, down_weight),
+            (gain_one, shift_one, gain_two, shift_two, qkv_bias, up_bias),
+            part,
+        )
+        norm_sums, d_qkv_bias, d_up_bias = sums
+        out_sum = lax.psum_scatter(out_part, "dp", scatter_dimension=0, tiled=True)
+        scaled = lax.psum_scatter(scaled_part, "dp", scatter_dimension=0, tiled=True)
+        out_sum, scaled = out_sum.astype(jnp.float32), scaled.astype(jnp.float32)
 
     inputs = tokens_in[0].astype(jnp.float32)
     live = (jnp.arange(length) < lengths[0]).astype(jnp.float32)[:, None]
     back = cotangent[0].astype(jnp.float32) * live
-    unit_rows, inverse_rows = normalize(inputs)
-    output = ((inputs + out_sum + out_bias + down_bias) * live).astype(jnp.bfloat16)
-    input_grad = back + inverse_rows * (
-        scaled
-        - jnp.mean(scaled, axis=-1, keepdims=True)
-        - unit_rows * jnp.mean(scaled * unit_rows, axis=-1, keepdims=True)
-    )
-
-    norm_sums, d_qkv_bias, d_up_bias = sums
     back_total = jnp.sum(back, axis=0)
 
     def spread(values, pieces):
@@ -294,26 +1050,51 @@
             back_total,
         ]
     )
-    small_sum = lax.psum(small_grad, ("dp", "fsdp"))
-    small_rows = small_master.shape[0]
-    small_sum = lax.dynamic_slice_in_dim(small_sum, shard * small_rows, small_rows)
-
-    qkv_term, out_term, up_term, down_term = terms
-    out_wide = lax.dynamic_update_slice_in_dim(
-        jnp.zeros((D, D), jnp.bfloat16), out_term, part * head_cols, axis=0
-    )
-
-    def to_owner(term):
-        own = lax.psum_scatter(term, "fsdp", scatter_dimension=0, tiled=True)
-        return lax.all_gather(own, "dp", axis=0, tiled=False).astype(jnp.float32)
-
-    qkv_sum = joined(to_owner(qkv_term), 3)
-    up_sum = joined(to_owner(up_term), shards)
-    down_sum = to_owner(down_term).reshape(down_master.shape)
-    out_sum_grad = lax.psum(
-        lax.psum_scatter(out_wide, "fsdp", scatter_dimension=0, tiled=True), "dp"
-    ).astype(jnp.float32)
-    reduced = (qkv_sum, out_sum_grad, up_sum, down_sum, small_sum)
+    if own:
+        padded = jnp.pad(small_grad.reshape(shards, small_rows), ((0, 0), (0, 2048 - small_rows)))
+        out_sum, scaled, terms_all, out_grad, small_sum = reduce(
+            out_part, scaled_part, terms, out_term, padded.reshape(shards, 16, 128)
+        )
+        small_sum = small_sum.reshape(2048)[:small_rows]
+        terms_all = terms_all.astype(jnp.float32)
+        qkv_width, up_width = 3 * head_cols, ff_cols
+        reduced = (
+            joined(terms_all[:, :, :qkv_width], 3),
+            out_grad.astype(jnp.float32),
+            joined(terms_all[:, :, qkv_width : qkv_width + up_width], shards),
+            terms_all[:, :, qkv_width + up_width :].reshape(down_master.shape),
+            small_sum,
+        )
+    else:
+        small_sum = lax.psum(small_grad, ("dp", "fsdp"))
+        small_rows = small_master.shape[0]
+        small_sum = lax.dynamic_slice_in_dim(small_sum, shard * small_rows, small_rows)
+        qkv_term, out_term, up_term, down_term = terms
+        out_wide = lax.dynamic_update_slice_in_dim(
+            jnp.zeros((D, D), jnp.bfloat16), out_term, part * head_cols, axis=0
+        )
+
+        def to_owner(term):
+            own = lax.psum_scatter(term, "fsdp", scatter_dimension=0, tiled=True)
+            return lax.all_gather(own, "dp", axis=0, tiled=False).astype(jnp.float32)
+
+        reduced = (
+            joined(to_owner(qkv_term), 3),
+            lax.psum(
+                lax.psum_scatter(out_wide, "fsdp", scatter_dimension=0, tiled=True), "dp"
+            ).astype(jnp.float32),
+            joined(to_owner(up_term), shards),
+            to_owner(down_term).reshape(down_master.shape),
+            small_sum,
+        )
+
+    unit_rows, inverse_rows = normalize(inputs)
+    output = ((inputs + out_sum + out_bias + down_bias) * live).astype(jnp.bfloat16)
+    input_grad = back + inverse_rows * (
+        scaled
+        - jnp.mean(scaled, axis=-1, keepdims=True)
+        - unit_rows * jnp.mean(scaled * unit_rows, axis=-1, keepdims=True)
+    )
     return (output[None], input_grad.astype(jnp.bfloat16)[None]) + lamb(
         masters, firsts, seconds, reduced
     )

time: 638 us -> 370 us (0.58)
  waiting for transfers between devices: 298 us -> 0 us
  Pallas kernels: 0 us -> 233 us
  matrix products: 78.1 us -> 0 us
  blocking collectives: 93.4 us -> 36.4 us
  local copies, waits for them, and re-layouts: 80.2 us -> 52.2 us
  other arithmetic: 60.6 us -> 39.6 us
  between operations: 22 us -> 8.44 us
    pallas_call x0 -> x3, Pallas kernels: none -> 233 us  [the longest x1 99.6 us: reduce(): pl.pallas_call(reduce_kernel, out_shape=(shape((length, width), f32), sha...]
    reduce_scatter x6 -> x0, waiting for transfers between devices: 170 us -> none  [the longest x3 95.4 us: to_owner(): own = lax.psum_scatter(term, 'fsdp', scatter_dimension=0, tiled=True)]
    all_gather x8 -> x0, waiting for transfers between devices: 94.8 us -> none  [the longest x4 90 us: over_shards(): return lax.all_gather(own, 'fsdp', axis=0, tiled=True)]
    dot_general x17 -> x0, matrix products: 72.9 us -> none  [the longest x4 20.2 us: against(): lax.dot_general(left, right, (((1,), (1,)), ((), ())), preferred_element_...]
    psum x1 -> x0, blocking collectives: 39.9 us -> none  [local_split(): small_sum = lax.psum(small_grad, ('dp', 'fsdp'))]
    psum x1 -> x0, waiting for transfers between devices: 32.2 us -> none  [local_split(): lax.psum(lax.psum_scatter(out_wide, 'fsdp', scatter_dimension=0, tiled=Tr...]
    all_gather x2 -> x0, blocking collectives: 30.8 us -> none  [the longest x1 15.7 us: over_shards(): return lax.all_gather(own, 'fsdp', axis=0, tiled=True)]
    psum x1, blocking collectives: 14.7 us -> 36.4 us  [lamb(): lax.psum((local_squares(masters), local_squares(updates)), 'fsdp')]
  transfers between devices with their start and end apart: 15 -> 0, of which waited for: 13 -> 0; matrix products, arithmetic and copies ran while one was open for 29% -> 0% of each run, Pallas kernels for 0% -> 0%
where the time goes in v3:
time: 370 us; the launch traced here: 369 us
  Pallas kernels  233 us (63%)
  local copies, waits for them, and re-layouts  52.2 us (14%)
  other arithmetic  39.6 us (11%)
  blocking collectives  36.4 us (10%)
  between operations  8.44 us (2%)
    pallas_call x1, Pallas kernels, reduce(): pl.pallas_call(reduce_kernel, out_shape=(shape((length, width), f32), sha...  99.6 us
    pallas_call x1, Pallas kernels, gather(): pl.pallas_call(gather_kernel, out_shape=(shape((4,) + x_own.shape, jnp.bf...  85.2 us
    pallas_call x1, Pallas kernels, compute(): pl.pallas_call(compute_kernel, out_shape=(S((group, length, D), jnp.bfloa...  47.8 us
    psum x1, blocking collectives, lamb(): lax.psum((local_squares(masters), local_squares(updates)), 'fsdp')  36.4 us
    reduce_sum x6, other arithmetic, local_squares(): return jnp.stack([jnp.sum(array_in * array_in) for array_in in arrays])  22.3 us
    unnamed x78, local copies, waits for them, and re-layouts  17.5 us
    sub x5, other arithmetic, lamb(): masters[number]  10.1 us

profile of v3, /device:TPU:0, one launch (start us, length us, event | category | flops | bytes accessed | tf_op | source)
XLA Modules:
  0.0 369.2 jit_solution(368387787665903966)
XLA Ops:
  0.7 3.2 copy.49
  6.1 2.4 reshape.164
  8.5 2.2 constant_dynamic-slice_fusion.1
  14.3 85.2 %gather.1 = (bf16[4,256,1024]{2,1,0:T(8,128)(2,1)}, bf16[4,256,1024]{2,1,0:T(8,128)(2,1)}, f32[4,8,128]{2,1,0:T(8,128)}, bf16[8,128,2816]{2,1,0:T(8,128)(2,1)}, ...) custom-call(bf16[256,1024]{1,0:T(8,128)(2,1)} %bitcast.104, bf16[256,1024]{1,0:T(8,128)(2,1)} %bitcast.108, ...), custom_call_target="tpu_custom_call" | custom-call | tf_op jit(solution)/shard_map/gather/pallas_call | solution.py:442
  104.1 47.8 %compute.1 = (bf16[4,256,1024]{2,1,0:T(8,128)(2,1)}, bf16[4,256,1024]{2,1,0:T(8,128)(2,1)}, bf16[8,128,2816]{2,1,0:T(8,128)(2,1)}, bf16[2,128,1024]{2,1,0:T(8,12...) custom-call(bf16[4,256,1024]{2,1,0:T(8,128)(2,1)} %get-tuple-element.36.x_ref, ...), custom_call_target="tpu_custom_call" | custom-call | tf_op jit(solution)/shard_map/compute/pallas_call | solution.py:930
  155.1 99.6 %reduce.1 = (f32[256,1024]{1,0:T(8,128)}, f32[256,1024]{1,0:T(8,128)}, bf16[4,128,2816]{2,1,0:T(8,128)(2,1)}, bf16[128,1024]{1,0:T(8,128)(2,1)}, f32[16,128]{1,0:T(8,128)}) custom-call(bf16[4,256,1024]{2,1,0:T(8,128)(2,1)} %get-tuple-element.42.out_part, bf16[4,256,1024]{2,1,0:T(8,128)(2,1)} %get-tuple-element.43.dx_part, ...), custom_call_target="tpu_custom_call" | custom-call | tf_op jit(solution)/shard_map/reduce/pallas_call | solution.py:771
  254.7 3.2 fusion.31
  258.5 2.7 copy.62
  261.2 3.2 reshape.177
  264.4 7.1 %multiply_reduce_fusion.1 = (f32[]{:T(128)}, f32[]{:T(128)}, f32[128,4096]{1,0:T(8,128)}, f32[128,4096]{1,0:T(8,128)}) fusion(f32[128,4096]{1,0:T(8,128)S(1)} %copy-done.1, f32[128,4096]{1,0:T(8,128)} %reshape.177, f32[128,4096]{1,0:T(8,128)} %param.33, f32[128,4096]{1,0:T(8,128)} %param.28), kind=kLoop, calls=%fused_computation.13 | loop fusion | flops 7340030 | bytes 12582920 | tf_op jit(solution)/shard_map/reduce_sum | solution.py:95
  272.7 3.0 copy.58
  275.8 2.7 copy.59
  278.4 3.0 copy.57
  281.4 3.0 copy.60
  284.5 6.2 %multiply_reduce_fusion.4 = (f32[]{:T(128)}, f32[128,3072]{0,1:T(8,128)}, f32[128,3072]{0,1:T(8,128)}) fusion(f32[128,3072]{0,1:T(8,128)} %copy.49, f32[128,3,4,256]{0,3,2,1:T(8,128)} %copy.59, f32[128,3072]{0,1:T(8,128)} %copy.60, f32[128,3072]{0,1:T(8,128)} %copy.57), kind=kLoop, calls=%fused_computation.19 | loop fusion | flops 4718591 | bytes 9437188 | tf_op jit(solution)/shard_map/reduce_sum | solution.py:95
  290.7 4.1 %multiply_reduce_fusion = (f32[]{:T(128)}, f32[]{:T(128)}, f32[512,1024]{1,0:T(8,128)}, f32[512,1024]{1,0:T(8,128)}) fusion(f32[512,1024]{1,0:T(8,128)S(1)} %copy-done.9, f32[4,128,1024]{2,1,0:T(8,128)S(1)} %copy-done.12, f32[512,1024]{1,0:T(8,128)S(1)} %copy-done.17, f32[512,1024]{1,0:T(8,128)S(1)} %copy-done.18), kind=kLoop, calls=%fused_computation.11 | loop fusion | flops 7340030 | bytes 12582920 | tf_op jit(solution)/shard_map/reduce_sum | solution.py:95
  294.9 1.8 multiply_reduce_fusion.6
  297.3 3.3 stack.80
  300.6 2.4 multiply_reduce_fusion.5
  303.0 3.3 stack.74
  306.3 36.4 %all-reduce.2 = (f32[5]{0:T(128)S(1)}, f32[5]{0:T(128)S(1)}) all-reduce(f32[5]{0:T(128)S(1)} %stack.74, f32[5]{0:T(128)S(1)} %stack.80), channel_id=1, replica_groups=mesh['dp'=4,'fsdp'=8] {'fsdp'}, use_global_device_ids=true, to_apply=%region_10.11 | all-reduce | flops 10 | bytes 80 | tf_op jit(solution)/shard_map/psum | solution.py:1113
  347.8 5.4 %multiply_subtract_fusion = f32[512,1024]{1,0:T(8,128)} fusion(f32[512,1024]{1,0:T(8,128)} %param.24, f32[]{:T(128)} %bitcast.42, f32[512,1024]{1,0:T(8,128)} %get-tuple-element.90, f32[512,1024]{1,0:T(8,128)} %get-tuple-element.89), kind=kLoop, calls=%fused_computation.9 | loop fusion | flops 3145728 | bytes 8388612 | tf_op jit(solution)/shard_map/sub | solution.py:1119
  354.6 2.3 multiply_subtract_fusion.1
  361.3 1.6 copy.64
  (134 shorter events, 25.7 us)
Async XLA Ops:
  0.7 5.4 %copy-start = (f32[128,4096]{1,0:T(8,128)S(1)}, f32[128,4096]{1,0:T(8,128)}, u32[]{:S(2)}) copy-start(f32[128,4096]{1,0:T(8,128)} %param.23) | copy-start | bytes 6291460
  8.5 4.4 %copy-start.13 = (f32[128,1024]{1,0:T(8,128)S(1)}, f32[128,1024]{1,0:T(8,128)}, u32[]{:S(2)}) copy-start(f32[128,1024]{1,0:T(8,128)} %param.22) | copy-start | bytes 1572868
  8.5 5.2 %copy-start.25 = (f32[1664]{0:T(1024)S(1)}, f32[1664]{0:T(1024)}, u32[]{:S(2)}) copy-start(f32[1664]{0:T(1024)} %param.25) | copy-start | bytes 19972
  104.1 49.3 %copy-start.14 = (bf16[1,256,1024]{2,1,0:T(8,128)(2,1)S(1)}, bf16[1,256,1024]{2,1,0:T(8,128)(2,1)}, u32[]{:S(2)}) copy-start(bf16[1,256,1024]{2,1,0:T(8,128)(2,1)} %param.19) | copy-start | bytes 1572868
  261.2 3.2 copy-start.1
  264.4 7.1 %copy-start.8 = (bf16[4,128,2816]{2,1,0:T(8,128)(2,1)S(1)}, bf16[4,128,2816]{2,1,0:T(8,128)(2,1)}, u32[]{:S(2)}) copy-start(bf16[4,128,2816]{2,1,0:T(8,128)(2,1)} %get-tuple-element.51) | copy-start | bytes 8650756
  284.4 6.3 %copy-start.9 = (f32[512,1024]{1,0:T(8,128)S(1)}, f32[512,1024]{1,0:T(8,128)}, u32[]{:S(2)}) copy-start(f32[512,1024]{1,0:T(8,128)} %param.24) | copy-start | bytes 6291460
  284.5 6.3 %copy-start.12 = (f32[4,128,1024]{2,1,0:T(8,128)S(1)}, f32[4,128,1024]{2,1,0:T(8,128)}, u32[]{:S(2)}) copy-start(f32[4,128,1024]{2,1,0:T(8,128)} %get-tuple-element.95) | copy-start | bytes 6291460
  284.5 6.3 %copy-start.17 = (f32[512,1024]{1,0:T(8,128)S(1)}, f32[512,1024]{1,0:T(8,128)}, u32[]{:S(2)}) copy-start(f32[512,1024]{1,0:T(8,128)} %param.34) | copy-start | bytes 6291460
  284.5 6.3 %copy-start.18 = (f32[512,1024]{1,0:T(8,128)S(1)}, f32[512,1024]{1,0:T(8,128)}, u32[]{:S(2)}) copy-start(f32[512,1024]{1,0:T(8,128)} %param.29) | copy-start | bytes 6291460
  290.7 4.1 %copy-start.22 = (f32[128,1024]{1,0:T(8,128)S(1)}, f32[128,1024]{1,0:T(8,128)}, u32[]{:S(2)}) copy-start(f32[128,1024]{1,0:T(8,128)} %param.32) | copy-start | bytes 1572868
  290.7 4.1 %copy-start.23 = (f32[128,1024]{1,0:T(8,128)S(1)}, f32[128,1024]{1,0:T(8,128)}, u32[]{:S(2)}) copy-start(f32[128,1024]{1,0:T(8,128)} %param.27) | copy-start | bytes 1572868
  290.7 4.1 %copy-start.24 = (bf16[128,1024]{1,0:T(8,128)(2,1)S(1)}, bf16[128,1024]{1,0:T(8,128)(2,1)}, u32[]{:S(2)}) copy-start(bf16[128,1024]{1,0:T(8,128)(2,1)} %get-tuple-element.52) | copy-start | bytes 786436
  294.8 1.8 copy-start.30
  296.7 61.6 %copy-start.19 = (f32[128,1024]{1,0:T(8,128)}, f32[128,1024]{1,0:T(8,128)S(1)}, u32[]{:S(2)}) copy-start(f32[128,1024]{1,0:T(8,128)S(1)} %get-tuple-element.93) | copy-start | bytes 1572868
  297.3 55.8 %copy-start.26 = (f32[1664]{0:T(1024)}, f32[1664]{0:T(1024)S(1)}, u32[]{:S(2)}) copy-start(f32[1664]{0:T(1024)S(1)} %get-tuple-element.87) | copy-start | bytes 19972
  297.3 55.8 %copy-start.27 = (f32[1664]{0:T(1024)}, f32[1664]{0:T(1024)S(1)}, u32[]{:S(2)}) copy-start(f32[1664]{0:T(1024)S(1)} %get-tuple-element.88) | copy-start | bytes 19972
  347.8 6.7 %copy-start.10 = (f32[128,4096]{1,0:T(8,128)S(1)}, f32[128,4096]{1,0:T(8,128)}, u32[]{:S(2)}) copy-start(f32[128,4096]{1,0:T(8,128)} %get-tuple-element.91) | copy-start | bytes 6291460
  347.8 6.7 %copy-start.11 = (f32[128,4096]{1,0:T(8,128)S(1)}, f32[128,4096]{1,0:T(8,128)}, u32[]{:S(2)}) copy-start(f32[128,4096]{1,0:T(8,128)} %get-tuple-element.92) | copy-start | bytes 6291460
  354.5 3.7 %copy-start.20 = (f32[128,1024]{1,0:T(8,128)S(1)}, f32[128,1024]{1,0:T(8,128)}, u32[]{:S(2)}) copy-start(f32[128,1024]{1,0:T(8,128)} %get-tuple-element.94) | copy-start | bytes 1572868
  354.5 6.0 %copy-start.3 = (f32[128,3072]{0,1:T(8,128)S(1)}, f32[128,3072]{0,1:T(8,128)}, u32[]{:S(2)}) copy-start(f32[128,3072]{0,1:T(8,128)} %get-tuple-element.85) | copy-start | bytes 4718596
  354.6 6.0 %copy-start.5 = (f32[128,3072]{0,1:T(8,128)S(1)}, f32[128,3072]{0,1:T(8,128)}, u32[]{:S(2)}) copy-start(f32[128,3072]{0,1:T(8,128)} %get-tuple-element.86) | copy-start | bytes 4718596
  356.8 3.7 %copy-start.2 = (f32[128,3072]{0,1:T(8,128)S(1)}, f32[128,3072]{0,1:T(8,128)}, u32[]{:S(2)}) copy-start(f32[128,3072]{0,1:T(8,128)} %copy.49) | copy-start | bytes 4718596
  364.6 2.1 copy-start.16
  (7 other events, 10.9 us)

commit v4 on v3

--- a/solution.py
+++ b/solution.py
@@ -336,61 +336,73 @@
     w_all[shard] = w_own[...]
     small_all[shard] = small_own[...]
 
-    for n in range(3):
-        for k in range(1, 4):
-
-            @pl.when(z >= k)
+    def forward(k, n):
+        @pl.when(z >= k)
+        def _():
+            source = 2 * (z - k) + core
+            block = piece(w_all, source, n)
+            arrived(block, w_recv.at[n, source], at.down)
+
+            @pl.when(z < 3)
             def _():
-                source = 2 * (z - k) + core
-                block = piece(w_all, source, n)
-                arrived(block, w_recv.at[n, source], at.down)
-
-                @pl.when(z < 3)
-                def _():
-                    send(block, block, w_send.at[0, n, z - k], w_recv.at[n, source], at.up).start()
-
-                send(
-                    block, block, w_send.at[2, n, z - k], w_recv.at[n, source], at.other_core
-                ).start()
-
-            @pl.when(z + k <= 3)
+                send(block, block, w_send.at[0, n, z - k], w_recv.at[n, source], at.up).start()
+
+            send(
+                block, block, w_send.at[2, n, z - k], w_recv.at[n, source], at.other_core
+            ).start()
+
+        @pl.when(z + k <= 3)
+        def _():
+            source = 2 * (z + k) + core
+            block = piece(w_all, source, n)
+            arrived(block, w_recv.at[n, source], at.up)
+
+            @pl.when(z > 0)
             def _():
-                source = 2 * (z + k) + core
-                block = piece(w_all, source, n)
-                arrived(block, w_recv.at[n, source], at.up)
-
-                @pl.when(z > 0)
-                def _():
-                    send(
-                        block, block, w_send.at[1, n, z + k], w_recv.at[n, source], at.down
-                    ).start()
-
-                send(
-                    block, block, w_send.at[2, n, z + k], w_recv.at[n, source], at.other_core
-                ).start()
-
-    @pl.when(z != part)
-    def _():
-        block = out_all.at[core]
-        arrived(block, out_recv.at[core], at.up)
-
-        @pl.when((z > part) & (z < 3))
-        def _():
-            send(block, block, out_send.at[0], out_recv.at[core], at.up).start()
-
-        @pl.when((z < part) & (z > 0))
-        def _():
-            send(block, block, out_send.at[1], out_recv.at[core], at.down).start()
-
-        send(block, block, out_send.at[2], out_recv.at[core], at.other_core).start()
-
-    for n, (_, whole) in enumerate(activations):
+                send(block, block, w_send.at[1, n, z + k], w_recv.at[n, source], at.down).start()
+
+            send(
+                block, block, w_send.at[2, n, z + k], w_recv.at[n, source], at.other_core
+            ).start()
+
+    def forward_out(k):
+        @pl.when((z - k == part) | (z + k == part))
+        def _():
+            block = out_all.at[core]
+            arrived(block, out_recv.at[core], at.up)
+
+            @pl.when((z > part) & (z < 3))
+            def _():
+                send(block, block, out_send.at[0], out_recv.at[core], at.up).start()
+
+            @pl.when((z < part) & (z > 0))
+            def _():
+                send(block, block, out_send.at[1], out_recv.at[core], at.down).start()
+
+            send(block, block, out_send.at[2], out_recv.at[core], at.other_core).start()
+
+    def forward_plane(n):
+        whole = activations[n][1]
         arrived(whole.at[at.x_part], plane_recv.at[n, 0], at.across_x)
         block = whole.at[at.x_part, 0:HALF]
         send(block, block, plane_send.at[n, 2], plane_recv.at[n, 2], at.across_y).start()
         arrived(whole.at[at.y_part], plane_recv.at[n, 1], at.across_y)
         block = whole.at[at.y_part, HALF : 2 * HALF]
         send(block, block, plane_send.at[n, 3], plane_recv.at[n, 3], at.across_x).start()
+
+    forward(1, 0)
+    forward(1, 1)
+    forward_plane(0)
+    forward(1, 2)
+    forward_out(1)
+    forward(2, 0)
+    forward_plane(1)
+    forward(2, 1)
+    forward(2, 2)
+    forward_out(2)
+    for n in range(3):
+        forward(3, n)
+    forward_out(3)
 
     for n, (own, whole) in enumerate(activations):
         arrived(whole.at[at.far_part, 0:HALF], plane_recv.at[n, 2], at.across_y)
@@ -478,7 +490,9 @@
     small_part,
     out_sum,
     dx_sum,
-    terms_all,
+    down_all,
+    up_all,
+    qkv_all,
     out_grad,
     small_sum,
     plane_one,
@@ -510,6 +524,7 @@
     z, core, part, shard = at.z, at.core, at.part, at.shard
     greet(at)
     spans = ((1792, 2816), (768, 1792), (0, 768))
+    wholes = (down_all, up_all, qkv_all)
     first, second = slice(0, HALF), slice(HALF, 2 * HALF)
     f32, bf16 = jnp.float32, jnp.bfloat16
 
@@ -612,12 +627,19 @@
             arrived(line_in.at[4, :, low:high], line_recv.at[n, 4], at.up)
             block[...] = (block[...].astype(f32) + line_in[4, :, low:high].astype(f32)).astype(bf16)
 
-        terms_all[part, :, low:high] = block[...]
-        own = terms_all.at[part, :, low:high]
+        wholes[n][part] = block[...]
+        own = wholes[n].at[part]
         send(own, own, all_send.at[n, 0], all_recv.at[n, 0], at.across_x).start()
         send(own, own, all_send.at[n, 1], all_recv.at[n, 1], at.across_y).start()
 
-    for n, (low, high) in enumerate(spans):
+    plane_peers = (
+        (at.across_x, at.x_part),
+        (at.across_y, at.y_part),
+        (at.across_far, at.far_part),
+    )
+
+    def line(n):
+        low, high = spans[n]
         for other in (3, 0, 2, 1):
             arrived(core_in.at[other, :, low:high], core_recv.at[n, other], at.other_core)
             line_sum[other, :, low:high] = (
@@ -627,28 +649,8 @@
         for target in (3, 0, 2, 1):
             forward(n, target)
 
-    arrived(out_core_in, out_recv.at[0], at.other_core)
-    out_line[...] = (out_term[core].astype(f32) + out_core_in[...].astype(f32)).astype(bf16)
-
-    @pl.when((z < part) & (z > 0))
-    def _():
-        arrived(out_line_in.at[0], out_recv.at[1], at.down)
-        out_line[...] = (out_line[...].astype(f32) + out_line_in[0].astype(f32)).astype(bf16)
-
-    @pl.when((z > part) & (z < 3))
-    def _():
-        arrived(out_line_in.at[1], out_recv.at[2], at.up)
-        out_line[...] = (out_line[...].astype(f32) + out_line_in[1].astype(f32)).astype(bf16)
-
-    @pl.when(z < part)
-    def _():
-        send(out_line, out_line_in.at[0], out_send.at[1], out_recv.at[1], at.up).start()
-
-    @pl.when(z > part)
-    def _():
-        send(out_line, out_line_in.at[1], out_send.at[1], out_recv.at[2], at.down).start()
-
-    for n, term in enumerate(parts):
+    def plane_turns(n):
+        term = parts[n]
         for r, (rows, peer, _, turn, turn_part) in enumerate(routes):
             arrived(plane_one.at[n, r, 0], plane_recv.at[n, r, 0], peer)
             plane_turn[n, r] = (
@@ -662,23 +664,8 @@
                 turn,
             ).start()
 
-    total = small_part[shard]
-    for k in range(1, 8):
-        arrived(small_in.at[k - 1], small_recv.at[k - 1], at.shard_after(8 - k))
-        total = total + small_in[k - 1]
-    small_own[...] = total
-    plane_peers = (
-        (at.across_x, at.x_part),
-        (at.across_y, at.y_part),
-        (at.across_far, at.far_part),
-    )
-    for n, (peer, _) in enumerate(plane_peers):
-        send(
-            small_own, small_plane.at[part], small_send.at[7 + n], small_recv.at[7 + n], peer
-        ).start()
-    small_plane[part] = total
-
-    for n, (term, result) in enumerate(((out_part, out_sum), (dx_part, dx_sum))):
+    def plane_ends(n):
+        term, result = parts[n], (out_sum, dx_sum)[n]
         for r, (rows, peer, _, turn, _) in enumerate(routes):
             arrived(plane_one.at[n, r, 1], plane_recv.at[n, r, 1], peer)
             arrived(plane_two.at[n, r], plane_recv.at[n, r, 2], turn)
@@ -688,49 +675,102 @@
                 + plane_two[n, r].astype(f32)
             )
 
-    for n in range(3):
-        own_line(n)
-
-    @pl.when(z == part)
-    def _():
-        @pl.when(z > 0)
+    def out_travels():
+        arrived(out_core_in, out_recv.at[0], at.other_core)
+        out_line[...] = (out_term[core].astype(f32) + out_core_in[...].astype(f32)).astype(bf16)
+
+        @pl.when((z < part) & (z > 0))
         def _():
             arrived(out_line_in.at[0], out_recv.at[1], at.down)
             out_line[...] = (out_line[...].astype(f32) + out_line_in[0].astype(f32)).astype(bf16)
 
-        @pl.when(z < 3)
+        @pl.when((z > part) & (z < 3))
         def _():
             arrived(out_line_in.at[1], out_recv.at[2], at.up)
             out_line[...] = (out_line[...].astype(f32) + out_line_in[1].astype(f32)).astype(bf16)
 
+        @pl.when(z < part)
+        def _():
+            send(out_line, out_line_in.at[0], out_send.at[1], out_recv.at[1], at.up).start()
+
+        @pl.when(z > part)
+        def _():
+            send(out_line, out_line_in.at[1], out_send.at[1], out_recv.at[2], at.down).start()
+
+    def out_ends():
+        @pl.when(z == part)
+        def _():
+            @pl.when(z > 0)
+            def _():
+                arrived(out_line_in.at[0], out_recv.at[1], at.down)
+                out_line[...] = (
+                    out_line[...].astype(f32) + out_line_in[0].astype(f32)
+                ).astype(bf16)
+
+            @pl.when(z < 3)
+            def _():
+                arrived(out_line_in.at[1], out_recv.at[2], at.up)
+                out_line[...] = (
+                    out_line[...].astype(f32) + out_line_in[1].astype(f32)
+                ).astype(bf16)
+
+            for n, (peer, _) in enumerate(plane_peers):
+                send(out_line, out_grad, out_send.at[2 + n], out_recv.at[3], peer).start()
+            out_grad[...] = out_line[...]
+
+        @pl.when(z != part)
+        def _():
+            arrived(out_grad, out_recv.at[3], at.across_x)
+
+    def small_travels():
+        total = small_part[shard]
+        for k in range(1, 8):
+            arrived(small_in.at[k - 1], small_recv.at[k - 1], at.shard_after(8 - k))
+            total = total + small_in[k - 1]
+        small_own[...] = total
         for n, (peer, _) in enumerate(plane_peers):
-            send(out_line, out_grad, out_send.at[2 + n], out_recv.at[3], peer).start()
-        out_grad[...] = out_line[...]
-
-    @pl.when(z != part)
-    def _():
-        arrived(out_grad, out_recv.at[3], at.across_x)
-
-    for n, (low, high) in enumerate(spans):
-        arrived(terms_all.at[at.x_part, :, low:high], all_recv.at[n, 0], at.across_x)
-        block = terms_all.at[at.x_part, 0:64, low:high]
+            send(
+                small_own, small_plane.at[part], small_send.at[7 + n], small_recv.at[7 + n], peer
+            ).start()
+        small_plane[part] = total
+
+    def share(n):
+        whole = wholes[n]
+        arrived(whole.at[at.x_part], all_recv.at[n, 0], at.across_x)
+        block = whole.at[at.x_part, 0:64]
         send(block, block, all_send.at[n, 2], all_recv.at[n, 2], at.across_y).start()
-        arrived(terms_all.at[at.y_part, :, low:high], all_recv.at[n, 1], at.across_y)
-        block = terms_all.at[at.y_part, 64:128, low:high]
+        arrived(whole.at[at.y_part], all_recv.at[n, 1], at.across_y)
+        block = whole.at[at.y_part, 64:128]
         send(block, block, all_send.at[n, 3], all_recv.at[n, 3], at.across_x).start()
 
+    line(0)
+    plane_turns(0)
+    line(1)
+    own_line(0)
+    plane_turns(1)
+    out_travels()
+    line(2)
+    small_travels()
+    own_line(1)
+    share(0)
+    plane_ends(0)
+    plane_ends(1)
+    out_ends()
+    own_line(2)
+    share(1)
+    share(2)
     for n, (peer, other) in enumerate(plane_peers):
         arrived(small_plane.at[other], small_recv.at[7 + n], peer)
     small_sum[...] = (small_plane[0] + small_plane[1]) + (small_plane[2] + small_plane[3])
 
     for n, (low, high) in enumerate(spans):
-        arrived(terms_all.at[at.far_part, 0:64, low:high], all_recv.at[n, 2], at.across_y)
-        arrived(terms_all.at[at.far_part, 64:128, low:high], all_recv.at[n, 3], at.across_x)
-        whole = terms_all.at[part, :, low:high]
-        sent(whole, all_send.at[n, 0], at.across_x)
-        sent(whole, all_send.at[n, 1], at.across_y)
-        sent(terms_all.at[part, 0:64, low:high], all_send.at[n, 2], at.across_y)
-        sent(terms_all.at[part, 64:128, low:high], all_send.at[n, 3], at.across_x)
+        whole = wholes[n]
+        arrived(whole.at[at.far_part, 0:64], all_recv.at[n, 2], at.across_y)
+        arrived(whole.at[at.far_part, 64:128], all_recv.at[n, 3], at.across_x)
+        sent(whole.at[part], all_send.at[n, 0], at.across_x)
+        sent(whole.at[part], all_send.at[n, 1], at.across_y)
+        sent(whole.at[part, 0:64], all_send.at[n, 2], at.across_y)
+        sent(whole.at[part, 64:128], all_send.at[n, 3], at.across_x)
         for other in range(4):
             block = line_sum.at[other, :, low:high]
             sent(block, core_send.at[n, other], at.other_core)
@@ -773,12 +813,14 @@
         out_shape=(
             shape((length, width), f32),
             shape((length, width), f32),
-            shape((4, rows, wide), bf16),
+            shape((4, rows, 1024), bf16),
+            shape((4, rows, 1024), bf16),
+            shape((4, rows, 768), bf16),
             shape((rows, width), bf16),
             shape(small, f32),
         ),
         in_specs=[VMEM_SPEC] * 5,
-        out_specs=(VMEM_SPEC,) * 5,
+        out_specs=(VMEM_SPEC,) * 7,
         scratch_shapes=[
             vmem((2, 2, 2, HALF, width), bf16),
             vmem((2, 2, HALF, width), bf16),
@@ -1052,19 +1094,10 @@
     )
     if own:
         padded = jnp.pad(small_grad.reshape(shards, small_rows), ((0, 0), (0, 2048 - small_rows)))
-        out_sum, scaled, terms_all, out_grad, small_sum = reduce(
+        out_sum, scaled, down_grad, up_grad, qkv_grad, out_grad, small_sum = reduce(
             out_part, scaled_part, terms, out_term, padded.reshape(shards, 16, 128)
         )
-        small_sum = small_sum.reshape(2048)[:small_rows]
-        terms_all = terms_all.astype(jnp.float32)
-        qkv_width, up_width = 3 * head_cols, ff_cols
-        reduced = (
-            joined(terms_all[:, :, :qkv_width], 3),
-            out_grad.astype(jnp.float32),
-            joined(terms_all[:, :, qkv_width : qkv_width + up_width], shards),
-            terms_all[:, :, qkv_width + up_width :].reshape(down_master.shape),
-            small_sum,
-        )
+        reduced = (qkv_grad, out_grad, up_grad, down_grad, small_sum[: small_rows // 128])
     else:
         small_sum = lax.psum(small_grad, ("dp", "fsdp"))
         small_rows = small_master.shape[0]
@@ -1095,9 +1128,202 @@
         - jnp.mean(scaled, axis=-1, keepdims=True)
         - unit_rows * jnp.mean(scaled * unit_rows, axis=-1, keepdims=True)
     )
-    return (output[None], input_grad.astype(jnp.bfloat16)[None]) + lamb(
+    update = lamb_split if own else lamb
+    return (output[None], input_grad.astype(jnp.bfloat16)[None]) + update(
         masters, firsts, seconds, reduced
     )
+
+
+def lamb_rows(first_old, second_old, master, grad):
+    first_new = BETA_ONE * first_old + (1.0 - BETA_ONE) * grad
+    second_new = BETA_TWO * second_old + (1.0 - BETA_TWO) * grad * grad
+    update = first_new / (jnp.sqrt(second_new) + ADAM_EPSILON) + DECAY * master
+    return first_new, second_new, update
+
+
+def lane_sums(values):
+    squares = jnp.sum(values * values, axis=0, keepdims=True)
+    total = squares[:, 0:128]
+    for n in range(1, squares.shape[1] // 128):
+        total = total + squares[:, n * 128 : (n + 1) * 128]
+    return total
+
+
+def moments_kernel(*refs):
+    qkv_grad, out_grad, up_grad, down_grad, small_grad = refs[0:5]
+    masters, firsts, seconds = refs[5:10], refs[10:15], refs[15:20]
+    first_news, second_news, updates = refs[20:25], refs[25:30], refs[30:35]
+    squares = refs[35]
+    step = pl.program_id(0)
+
+    @pl.when(step == 0)
+    def _():
+        squares[...] = jnp.zeros_like(squares)
+
+    def one(number, span, grad):
+        index = (slice(None), span)
+        first_new, second_new, update = lamb_rows(
+            firsts[number][index], seconds[number][index], masters[number][index], grad
+        )
+        first_news[number][index] = first_new
+        second_news[number][index] = second_new
+        updates[number][index] = update
+        return lane_sums(masters[number][index]), lane_sums(update)
+
+    def add(number, pairs):
+        weight, update = pairs[0]
+        for more_weight, more_update in pairs[1:]:
+            weight, update = weight + more_weight, update + more_update
+        squares[number : number + 1] += weight
+        squares[8 + number : 9 + number] += update
+
+    f32 = jnp.float32
+    parts = qkv_grad.shape[0]
+    width = qkv_grad.shape[2] // 3
+    add(
+        0,
+        [
+            one(
+                0,
+                slice((c * parts + d) * width, (c * parts + d + 1) * width),
+                qkv_grad[d, :, c * width : (c + 1) * width].astype(f32),
+            )
+            for c in range(3)
+            for d in range(parts)
+        ],
+    )
+    add(1, [one(1, slice(None), out_grad[...].astype(f32))])
+    pieces = up_grad.shape[2] // 128
+    add(
+        2,
+        [
+            one(
+                2,
+                slice((g * parts + d) * 128, (g * parts + d + 1) * 128),
+                up_grad[d, :, g * 128 : (g + 1) * 128].astype(f32),
+            )
+            for g in range(pieces)
+            for d in range(parts)
+        ],
+    )
+    add(3, [one(3, slice(None), down_grad[0].astype(f32))])
+
+    @pl.when(step == 0)
+    def _():
+        first_new, second_new, update = lamb_rows(
+            firsts[4][...], seconds[4][...], masters[4][...], small_grad[...]
+        )
+        first_news[4][...] = first_new
+        second_news[4][...] = second_new
+        updates[4][...] = update
+        squares[4:5] += lane_sums(masters[4][...])
+        squares[12:13] += lane_sums(update)
+
+
+def lamb_specs(masters, steps):
+    specs = [pl.BlockSpec((m.shape[0] // steps, m.shape[1]), lambda i: (i, 0)) for m in masters[:4]]
+    return specs + [pl.BlockSpec(masters[4].shape, lambda i: (0, 0))]
+
+
+def moments(grads, masters, firsts, seconds, steps=8):
+    qkv_grad, out_grad, up_grad, down_grad, small_grad = grads
+    shape = jax.ShapeDtypeStruct
+    each = lamb_specs(masters, steps)
+    rows = qkv_grad.shape[1]
+    halves = steps // qkv_grad.shape[0]
+    grad_specs = [
+        pl.BlockSpec((qkv_grad.shape[0], rows // steps, qkv_grad.shape[2]), lambda i: (0, i, 0)),
+        each[1],
+        pl.BlockSpec((up_grad.shape[0], rows // steps, up_grad.shape[2]), lambda i: (0, i, 0)),
+        pl.BlockSpec(
+            (1, rows // halves, down_grad.shape[2]), lambda i: (i // halves, i % halves, 0)
+        ),
+        each[4],
+    ]
+    out = [shape(m.shape, jnp.float32) for m in masters]
+    results = pl.pallas_call(
+        moments_kernel,
+        grid=(steps,),
+        in_specs=grad_specs + each * 3,
+        out_specs=each * 3 + [pl.BlockSpec((16, 128), lambda i: (0, 0))],
+        out_shape=out * 3 + [shape((16, 128), jnp.float32)],
+        compiler_params=pltpu.CompilerParams(vmem_limit_bytes=40 << 20),
+        name="moments",
+    )(*grads, *masters, *firsts, *seconds)
+    return results[0:5], results[5:10], results[10:15], results[15]
+
+
+def norms_kernel(squares, total, steps, everyone, send_sem, recv_sem):
+    shard, part = lax.axis_index("fsdp"), lax.axis_index("dp")
+    peers = [(part, (shard + k) % 8) for k in range(1, 8)]
+    barrier = pltpu.get_barrier_semaphore()
+    for peer in peers:
+        pl.semaphore_signal(barrier, inc=1, device_id=peer, device_id_type=MESH_ID)
+    pl.semaphore_wait(barrier, 7)
+    for k in range(1, 8):
+        send(
+            squares, everyone.at[shard], send_sem.at[k - 1], recv_sem.at[k - 1], peers[k - 1]
+        ).start()
+    everyone[shard] = squares[...]
+    for k in range(1, 8):
+        arrived(everyone.at[(shard + 8 - k) % 8], recv_sem.at[k - 1], peers[7 - k])
+    for k in range(1, 8):
+        sent(squares, send_sem.at[k - 1], peers[k - 1])
+    summed = everyone[0]
+    for k in range(1, 8):
+        summed = summed + everyone[k]
+    norms = jnp.sqrt(jnp.sum(summed, axis=1, keepdims=True))
+    total[...] = jnp.broadcast_to(norms, (16, 128))
+    steps[...] = jnp.broadcast_to(RATE * (norms[0:8] / norms[8:16]), (8, 128))
+
+
+def norms(squares):
+    shape = jax.ShapeDtypeStruct
+    dma = pltpu.SemaphoreType.DMA
+    return pl.pallas_call(
+        norms_kernel,
+        out_shape=(shape((16, 128), jnp.float32), shape((8, 128), jnp.float32)),
+        in_specs=[VMEM_SPEC],
+        out_specs=(VMEM_SPEC,) * 2,
+        scratch_shapes=[pltpu.VMEM((8, 16, 128), jnp.float32), dma((7,)), dma((7,))],
+        compiler_params=pltpu.CompilerParams(collective_id=2, has_side_effects=True),
+        name="norms",
+    )(squares)
+
+
+def step_kernel(*refs):
+    scales, masters, updates, news = refs[0], refs[1:6], refs[6:11], refs[11:16]
+    for number in range(5):
+        scale = scales[number : number + 1, 0:1]
+        news[number][...] = masters[number][...] - scale * updates[number][...]
+
+
+def step_masters(scales, masters, updates, steps=8):
+    each = lamb_specs(masters, steps)
+    return pl.pallas_call(
+        step_kernel,
+        grid=(steps,),
+        in_specs=[pl.BlockSpec((8, 128), lambda i: (0, 0))] + each * 2,
+        out_specs=each,
+        out_shape=[jax.ShapeDtypeStruct(m.shape, jnp.float32) for m in masters],
+        compiler_params=pltpu.CompilerParams(vmem_limit_bytes=40 << 20),
+        name="step_masters",
+    )(scales, *masters, *updates)
+
+
+def lamb_split(masters, firsts, seconds, grads):
+    def tall(arrays):
+        return tuple(arrays[:4]) + (arrays[4].reshape(-1, 128),)
+
+    def flat_small(arrays):
+        return tuple(arrays[:4]) + (arrays[4].reshape(-1),)
+
+    masters, firsts, seconds = tall(masters), tall(firsts), tall(seconds)
+    first_news, second_news, updates, squares = moments(grads, masters, firsts, seconds)
+    total, scales = norms(squares)
+    news = step_masters(scales, masters, updates)
+    lamb_norms = jnp.stack([total[0:5, 0], total[8:13, 0]])
+    return flat_small(news) + flat_small(first_news) + flat_small(second_news) + (lamb_norms,)
 
 
 def lamb(masters, firsts, seconds, reduced):

time: 370 us -> 291 us (0.79)
  blocking collectives: 36.4 us -> 0 us
  other arithmetic: 39.6 us -> 14 us
  local copies, waits for them, and re-layouts: 52.2 us -> 33.7 us
  Pallas kernels: 233 us -> 240 us
  between operations: 8.44 us -> 1.76 us
    psum x1 -> x0, blocking collectives: 36.4 us -> none  [lamb(): lax.psum((local_squares(masters), local_squares(updates)), 'fsdp')]
    pallas_call x0 -> x3, Pallas kernels: none -> 33 us  [the longest x1 14.6 us: norms(): pl.pallas_call(norms_kernel, out_shape=(shape((16, 128), jnp.float32), sh...]
    pallas_call x1, Pallas kernels: 85.2 us -> 61.5 us  [gather(): pl.pallas_call(gather_kernel, out_shape=(shape((4,) + x_own.shape, jnp.bf...]
    reduce_sum x6 -> x0, other arithmetic: 22.3 us -> none  [local_squares(): return jnp.stack([jnp.sum(array_in * array_in) for array_in in arrays])]
    sub x5 -> x0, other arithmetic: 10.1 us -> none  [lamb(): masters[number]]
    slice x5 -> x1, local copies, waits for them, and re-layouts: 8.69 us -> 0.14 us  [lamb_split(): lamb_norms = jnp.stack([total[0:5, 0], total[8:13, 0]])]
    another operation x5 -> x1, local copies, waits for them, and re-layouts: 6.58 us -> 0.01 us  [the longest x2 6.57 us: local_squares(): return jnp.stack([jnp.sum(array_in * array_in) for array_in in arrays])]
    transpose x3 -> x0, local copies, waits for them, and re-layouts: 5.46 us -> none  [joined(): return slices.reshape(parts, rows, pieces, width).transpose(1, 2, 0, 3).r...]
where the time goes in v4:
time: 291 us; the launch traced here: 289 us
  Pallas kernels  240 us (82%)
  local copies, waits for them, and re-layouts  33.7 us (12%)
  other arithmetic  14 us (5%)
    pallas_call x1, Pallas kernels, reduce(): pl.pallas_call(reduce_kernel, out_shape=(shape((length, width), f32), sha...  97.7 us
    pallas_call x1, Pallas kernels, gather(): pl.pallas_call(gather_kernel, out_shape=(shape((4,) + x_own.shape, jnp.bf...  61.5 us
    pallas_call x1, Pallas kernels, compute(): pl.pallas_call(compute_kernel, out_shape=(S((group, length, D), jnp.bfloa...  47.8 us
    unnamed x72, local copies, waits for them, and re-layouts  21.3 us
    pallas_call x1, Pallas kernels, norms(): pl.pallas_call(norms_kernel, out_shape=(shape((16, 128), jnp.float32), sh...  14.6 us
    pallas_call x1, Pallas kernels, moments(): pl.pallas_call(moments_kernel, grid=(steps,), in_specs=grad_specs + each...  14.1 us

profile of v4, /device:TPU:0, one launch (start us, length us, event | category | flops | bytes accessed | tf_op | source)
XLA Modules:
  0.0 289.4 jit_solution(886050002002661471)
XLA Ops:
  1.5 1.2 convert_reduce_fusion
  2.7 1.3 fusion.9
  4.6 1.2 fusion.14
  7.5 1.8 dynamic-slice_convert_fusion
  11.4 1.8 copy.45
  14.9 2.4 reshape.150
  17.3 2.2 constant_dynamic-slice_fusion.1
  20.5 61.5 %gather.1 = (bf16[4,256,1024]{2,1,0:T(8,128)(2,1)}, bf16[4,256,1024]{2,1,0:T(8,128)(2,1)}, f32[4,8,128]{2,1,0:T(8,128)}, bf16[8,128,2816]{2,1,0:T(8,128)(2,1)}, ...) custom-call(bf16[256,1024]{1,0:T(8,128)(2,1)} %bitcast.72, bf16[256,1024]{1,0:T(8,128)(2,1)} %bitcast.73, ...), custom_call_target="tpu_custom_call" | custom-call | tf_op jit(solution)/shard_map/gather/pallas_call | solution.py:454
  84.8 47.8 %compute.1 = (bf16[4,256,1024]{2,1,0:T(8,128)(2,1)}, bf16[4,256,1024]{2,1,0:T(8,128)(2,1)}, bf16[8,128,2816]{2,1,0:T(8,128)(2,1)}, bf16[2,128,1024]{2,1,0:T(8,12...) custom-call(bf16[4,256,1024]{2,1,0:T(8,128)(2,1)} %get-tuple-element.61.x_ref, ...), custom_call_target="tpu_custom_call" | custom-call | tf_op jit(solution)/shard_map/compute/pallas_call | solution.py:972
  135.7 97.7 %reduce.5 = (f32[256,1024]{1,0:T(8,128)}, f32[256,1024]{1,0:T(8,128)}, bf16[4,128,1024]{2,1,0:T(8,128)(2,1)}, bf16[4,128,1024]{2,1,0:T(8,128)(2,1)}, bf16[4,128,...) custom-call(bf16[4,256,1024]{2,1,0:T(8,128)(2,1)} %get-tuple-element.67.out_part, ...), custom_call_target="tpu_custom_call" | custom-call | tf_op jit(solution)/shard_map/reduce/pallas_call | solution.py:811
  233.4 1.7 fusion.20
  235.2 3.3 %fusion.16 = (bf16[1,256,1024]{2,1,0:T(8,128)(2,1)}, bf16[1,256,1024]{2,1,0:T(8,128)(2,1)}) fusion(f32[256,1024]{1,0:T(8,128)} %get-tuple-element.75, f32[256]{0:T(256)S(1)} %broadcast_multiply_fusion, f32[256]{0:T(256)S(1)} %broadcast_multiply_fusion.1, f32[256]{0:T(256)S(1)} %add_rsqrt_fusion, f32[256]{0:T(256)S(1)} %broadcast_multiply_fusion.2, ...), kind=kLoop, calls=%fused_computation.22 | loop fusion | flops 4194304 | bytes 4207616 | tf_op jit(solution)/shard_map/broadcast_in_dim | solution.py:1132
  238.5 1.2 copy-done.14
  239.7 1.1 copy-done.15
  242.5 14.1 %moments.1 = (f32[128,3072]{1,0:T(8,128)}, f32[128,1024]{1,0:T(8,128)}, f32[128,4096]{1,0:T(8,128)}, f32[512,1024]{1,0:T(8,128)}, f32[13,128]{1,0:T(8,128)}, /*i...) custom-call(bf16[4,128,768]{2,1,0:T(8,128)(2,1)S(1)} %copy-done.15, ...), custom_call_target="tpu_custom_call" | custom-call | tf_op jit(solution)/shard_map/moments/pallas_call | solution.py:1244
  256.7 1.3 copy-done.6
  258.0 1.1 copy-done.9
  260.5 14.6 %norms.1 = (f32[16,128]{1,0:T(8,128)}, f32[8,128]{1,0:T(8,128)}) custom-call(f32[16,128]{1,0:T(8,128)} %copy-done.25), custom_call_target="tpu_custom_call" | custom-call | tf_op jit(solution)/shard_map/norms/pallas_call | solution.py:1283
  275.2 1.4 copy-done.3
  276.6 1.6 copy-done.4
  278.2 1.6 copy-done.7
  279.8 1.6 copy-done.8
  281.3 1.4 copy-done.10
  284.5 4.2 %step_masters.1 = (f32[128,3072]{1,0:T(8,128)}, f32[128,1024]{1,0:T(8,128)}, f32[128,4096]{1,0:T(8,128)}, f32[512,1024]{1,0:T(8,128)}, f32[13,128]{1,0:T(8,128)}) custom-call(f32[8,128]{1,0:T(8,128)S(1)} %copy-done.26, f32[128,3072]{1,0:T(8,128)S(1)} %copy-done.3, f32[128,1024]{1,0:T(8,128)S(1)} %copy-done.5, f32[128,4096]{1,0:T(8,128)S(1)} %copy-done.1, ...), custom_call_target="tpu_custom_call" | custom-call | tf_op jit(solution)/shard_map/step_masters/pallas_call | solution.py:1303
  (107 shorter events, 18.5 us)
Async XLA Ops:
  7.4 3.2 %copy-start.5 = (f32[128,1024]{1,0:T(8,128)S(1)}, f32[128,1024]{1,0:T(8,128)}, u32[]{:S(2)}) copy-start(f32[128,1024]{1,0:T(8,128)} %refs_2_.1) | copy-start | bytes 1572868
  10.6 4.3 %copy-start = (f32[128,4096]{1,0:T(8,128)S(1)}, f32[128,4096]{1,0:T(8,128)}, u32[]{:S(2)}) copy-start(f32[128,4096]{1,0:T(8,128)} %refs_3_.1) | copy-start | bytes 6291460
  17.3 2.3 copy-start.29
  135.7 97.7 %copy-start.27 = (bf16[1,256,1024]{2,1,0:T(8,128)(2,1)S(1)}, bf16[1,256,1024]{2,1,0:T(8,128)(2,1)}, u32[]{:S(2)}) copy-start(bf16[1,256,1024]{2,1,0:T(8,128)(2,1)} %param.18) | copy-start | bytes 1572868
  135.7 99.4 %copy-start.28 = (bf16[1,256,1024]{2,1,0:T(8,128)(2,1)S(1)}, bf16[1,256,1024]{2,1,0:T(8,128)(2,1)}, u32[]{:S(2)}) copy-start(bf16[1,256,1024]{2,1,0:T(8,128)(2,1)} %param.19) | copy-start | bytes 1572868
  135.7 102.7 %copy-start.16 = (f32[128,1024]{1,0:T(8,128)S(1)}, f32[128,1024]{1,0:T(8,128)}, u32[]{:S(2)}) copy-start(f32[128,1024]{1,0:T(8,128)} %refs_11_.1) | copy-start | bytes 1572868
  135.7 102.7 %copy-start.17 = (f32[128,1024]{1,0:T(8,128)S(1)}, f32[128,1024]{1,0:T(8,128)}, u32[]{:S(2)}) copy-start(f32[128,1024]{1,0:T(8,128)} %refs_16_.1) | copy-start | bytes 1572868
  233.4 5.0 %copy-start.12 = (f32[128,3072]{1,0:T(8,128)S(1)}, f32[128,3072]{1,0:T(8,128)}, u32[]{:S(2)}) copy-start(f32[128,3072]{1,0:T(8,128)} %refs_15_.1) | copy-start | bytes 4718596
  233.4 5.0 %copy-start.23 = (f32[1664]{0:T(1024)S(1)}, f32[1664]{0:T(1024)}, u32[]{:S(2)}) copy-start(f32[1664]{0:T(1024)} %param.35) | copy-start | bytes 19972
  235.1 3.3 %copy-start.2 = (f32[128,3072]{1,0:T(8,128)S(1)}, f32[128,3072]{1,0:T(8,128)}, u32[]{:S(2)}) copy-start(f32[128,3072]{1,0:T(8,128)} %refs_1_.1) | copy-start | bytes 4718596
  235.1 3.3 %copy-start.11 = (f32[128,3072]{1,0:T(8,128)S(1)}, f32[128,3072]{1,0:T(8,128)}, u32[]{:S(2)}) copy-start(f32[128,3072]{1,0:T(8,128)} %refs_10_.1) | copy-start | bytes 4718596
  235.1 3.3 %copy-start.13 = (bf16[4,128,1024]{2,1,0:T(8,128)(2,1)S(1)}, bf16[4,128,1024]{2,1,0:T(8,128)(2,1)}, u32[]{:S(2)}) copy-start(bf16[4,128,1024]{2,1,0:T(8,128)(2,1)} %get-tuple-element.79.refs_3_) | copy-start | bytes 3145732
  235.1 3.3 %copy-start.21 = (f32[1664]{0:T(1024)S(1)}, f32[1664]{0:T(1024)}, u32[]{:S(2)}) copy-start(f32[1664]{0:T(1024)} %param.25) | copy-start | bytes 19972
  235.2 3.3 %copy-start.22 = (f32[1664]{0:T(1024)S(1)}, f32[1664]{0:T(1024)}, u32[]{:S(2)}) copy-start(f32[1664]{0:T(1024)} %param.30) | copy-start | bytes 19972
  238.5 1.2 copy-start.14
  242.5 32.6 %copy-start.1 = (f32[128,4096]{1,0:T(8,128)S(1)}, f32[128,4096]{1,0:T(8,128)}, u32[]{:S(2)}) copy-start(f32[128,4096]{1,0:T(8,128)} %refs_3_.1) | copy-start | bytes 6291460
  256.7 1.3 copy-start.6
  258.0 1.1 copy-start.9
  275.2 1.4 copy-start.3
  276.6 1.6 copy-start.4
  278.2 1.6 copy-start.7
  279.8 1.6 copy-start.8
  281.3 1.4 copy-start.10
  284.5 4.2 %copy-start.30 = (f32[16,128]{1,0:T(8,128)S(1)}, f32[16,128]{1,0:T(8,128)}, u32[]{:S(2)}) copy-start(f32[16,128]{1,0:T(8,128)} %get-tuple-element.103) | copy-start | bytes 24580
  (7 other events, 5.9 us)

commit v5 on v2

--- a/solution.py
+++ b/solution.py
@@ -2,7 +2,10 @@
 
 import jax
 import jax.numpy as jnp
+import numpy as np
 from jax import lax
+from jax.experimental import pallas as pl
+from jax.experimental.pallas import tpu as pltpu
 from jax.sharding import PartitionSpec as P
 
 D = 1024
@@ -10,6 +13,7 @@
 HD = 64
 FF = 4096
 ROT = 16
+SMALL = 13312
 
 
 NORM_EPSILON = 1e-05
@@ -201,6 +205,1018 @@
         tuple(term.astype(jnp.bfloat16) for term in terms),
         (norm_sums, d_qkv_bias, d_up_bias),
     )
+
+
+MESH_ID = pl.DeviceIdType.MESH
+HALF = 128
+
+
+class Place:
+    def __init__(self):
+        self.part = lax.axis_index("dp")
+        self.shard = lax.axis_index("fsdp")
+        self.z = self.shard // 2
+        self.core = self.shard % 2
+        self.x_part = 2 * (self.part // 2) + 1 - self.part % 2
+        self.y_part = (self.part + 2) % 4
+        self.far_part = 3 - self.part
+        self.across_x = (self.x_part, self.shard)
+        self.across_y = (self.y_part, self.shard)
+        self.across_far = (self.far_part, self.shard)
+        self.other_core = (self.part, 2 * self.z + 1 - self.core)
+        self.up = (self.part, jnp.minimum(self.shard + 2, 7))
+        self.down = (self.part, jnp.maximum(self.shard - 2, 0))
+
+    def shard_after(self, k):
+        return (self.part, (self.shard + k) % 8)
+
+
+def send(source, target, send_sem, recv_sem, device):
+    return pltpu.make_async_remote_copy(
+        src_ref=source,
+        dst_ref=target,
+        send_sem=send_sem,
+        recv_sem=recv_sem,
+        device_id=device,
+        device_id_type=MESH_ID,
+    )
+
+
+def arrived(target, recv_sem, device):
+    send(target, target, recv_sem, recv_sem, device).wait_recv()
+
+
+def sent(source, send_sem, device):
+    send(source, source, send_sem, send_sem, device).wait_send()
+
+
+def greet(at):
+    barrier = pltpu.get_barrier_semaphore()
+    peers = [at.across_x, at.across_y, at.across_far] + [at.shard_after(k) for k in range(1, 8)]
+    for peer in peers:
+        pl.semaphore_signal(barrier, inc=1, device_id=peer, device_id_type=MESH_ID)
+    pl.semaphore_wait(barrier, len(peers))
+
+
+SPANS = ((0, 768), (768, 1792), (1792, 2816))
+Q, U, N = 0, 1, 2
+
+
+def nt(left, right):
+    return lax.dot_general(
+        left, right, (((1,), (1,)), ((), ())), preferred_element_type=jnp.float32
+    )
+
+
+def tn(left, right):
+    return lax.dot_general(
+        left, right, (((0,), (0,)), ((), ())), preferred_element_type=jnp.float32
+    )
+
+
+def nn(left, right):
+    return jnp.dot(left, right, preferred_element_type=jnp.float32)
+
+
+def flat(value):
+    return value.reshape(value.shape[0] * value.shape[1], value.shape[2])
+
+
+def layer_kernel(
+    length_own,
+    x_own,
+    cot_own,
+    qkv_master,
+    out_master,
+    up_master,
+    down_master,
+    small_master,
+    tables,
+    output,
+    input_grad,
+    qkv_all,
+    up_all,
+    down_all,
+    out_grad,
+    small_sum,
+    x_all,
+    cot_all,
+    len_all,
+    w_all,
+    out_all,
+    small_own,
+    small_all,
+    vectors,
+    qkv_bias,
+    up_bias,
+    stats,
+    normed_one,
+    normed_two,
+    back,
+    heads_qkv,
+    mixed,
+    d_projected,
+    hidden,
+    d_hidden,
+    out_part,
+    dx_part,
+    terms,
+    out_term,
+    sums,
+    d_qkv_bias,
+    d_up_bias,
+    small_part,
+    plane_one,
+    plane_two,
+    plane_turn,
+    core_in,
+    line_in,
+    out_core_in,
+    out_line,
+    out_line_in,
+    small_in,
+    small_total,
+    small_plane,
+    load_sem,
+    plane_send,
+    plane_recv,
+    len_send,
+    len_recv,
+    w_send,
+    w_recv,
+    out_send,
+    out_recv,
+    small_send,
+    small_recv,
+    part_send,
+    part_recv,
+    core_send,
+    core_recv,
+    line_send,
+    line_recv,
+    rows_send,
+    rows_recv,
+    all_send,
+    all_recv,
+    keep_sem,
+    total_send,
+    total_recv,
+):
+    f32, bf16 = jnp.float32, jnp.bfloat16
+    at = Place()
+    z, core, part, shard = at.z, at.core, at.part, at.shard
+    length = x_own.shape[0]
+    head_cols = mixed.shape[2]
+    activated = normed_one
+    place_x, place_y = part % 2, part // 2
+
+    def near_first(i):
+        return 2 * ((place_y + i // 2) % 2) + (place_x + i % 2) % 2
+
+    def far_first(i):
+        return 2 * ((place_y + 1 - i % 2) % 2) + (place_x + 1 - i // 2) % 2
+
+    def piece(ref, slot, n):
+        return ref.at[slot, :, SPANS[n][0] : SPANS[n][1]]
+
+    plane_peers = (
+        (at.across_x, at.x_part),
+        (at.across_y, at.y_part),
+        (at.across_far, at.far_part),
+    )
+
+    stage = [hidden.at[n, 0:128] for n in range(4)]
+    loads = []
+    for c in range(3):
+        columns = pl.ds(pl.multiple_of(c * D + part * head_cols, 128), head_cols)
+        target = stage[0].at[:, c * head_cols : (c + 1) * head_cols]
+        loads.append((qkv_master.at[:, columns], target))
+    loads.append((out_master, stage[1]))
+    for g in range(8):
+        columns = pl.ds(pl.multiple_of(g * (FF // 8) + part * 128, 128), 128)
+        loads.append((up_master.at[:, columns], stage[2].at[:, g * 128 : (g + 1) * 128]))
+    rows = pl.ds(pl.multiple_of(part * 128, 128), 128)
+    loads.append((down_master.at[rows], stage[3]))
+    loads.append((x_own, x_all.at[part]))
+    loads.append((cot_own, cot_all.at[part]))
+
+    def load(n):
+        return pltpu.make_async_copy(loads[n][0], loads[n][1], load_sem.at[n])
+
+    for n in range(len(loads)):
+        load(n).start()
+    len_all[part] = jnp.full((8, 128), length_own[0], jnp.int32).astype(f32)
+    small_own[...] = jnp.zeros_like(small_own)
+    small_own[0:13] = small_master[...].astype(bf16).astype(f32)
+    small_all[shard] = small_own[...]
+    greet(at)
+
+    activations = ((x_own, x_all), (cot_own, cot_all))
+    for n, (own, whole) in enumerate(activations):
+        send(own, whole.at[part], plane_send.at[n, 0], plane_recv.at[n, 0], at.across_x).start()
+        send(own, whole.at[part], plane_send.at[n, 1], plane_recv.at[n, 1], at.across_y).start()
+
+    def cast(n, first, last):
+        for m in range(first, last):
+            load(m).wait()
+        low, high = SPANS[n]
+        w_all[shard, :, low:high] = stage[(0, 2, 3)[n]][:, 0 : high - low].astype(bf16)
+
+    def send_own(n):
+        block = piece(w_all, shard, n)
+
+        @pl.when(z < 3)
+        def _():
+            send(block, block, w_send.at[0, n, z], w_recv.at[n, shard], at.up).start()
+
+        @pl.when(z > 0)
+        def _():
+            send(block, block, w_send.at[1, n, z], w_recv.at[n, shard], at.down).start()
+
+        send(block, block, w_send.at[2, n, z], w_recv.at[n, shard], at.other_core).start()
+
+    def forward(k, n):
+        @pl.when(z >= k)
+        def _():
+            source = 2 * (z - k) + core
+            block = piece(w_all, source, n)
+            arrived(block, w_recv.at[n, source], at.down)
+
+            @pl.when(z < 3)
+            def _():
+                send(block, block, w_send.at[0, n, z - k], w_recv.at[n, source], at.up).start()
+
+            send(
+                block, block, w_send.at[2, n, z - k], w_recv.at[n, source], at.other_core
+            ).start()
+
+        @pl.when(z + k <= 3)
+        def _():
+            source = 2 * (z + k) + core
+            block = piece(w_all, source, n)
+            arrived(block, w_recv.at[n, source], at.up)
+
+            @pl.when(z > 0)
+            def _():
+                send(block, block, w_send.at[1, n, z + k], w_recv.at[n, source], at.down).start()
+
+            send(
+                block, block, w_send.at[2, n, z + k], w_recv.at[n, source], at.other_core
+            ).start()
+
+    def from_core(n):
+        for other in range(4):
+            source = 2 * other + 1 - core
+            arrived(piece(w_all, source, n), w_recv.at[n, source], at.other_core)
+
+    def send_out_rows():
+        block = out_all.at[core]
+
+        @pl.when(z < 3)
+        def _():
+            send(block, block, out_send.at[0], out_recv.at[core], at.up).start()
+
+        @pl.when(z > 0)
+        def _():
+            send(block, block, out_send.at[1], out_recv.at[core], at.down).start()
+
+        send(block, block, out_send.at[2], out_recv.at[core], at.other_core).start()
+
+    def forward_out(k):
+        @pl.when((z - k == part) | (z + k == part))
+        def _():
+            block = out_all.at[core]
+            arrived(block, out_recv.at[core], at.up)
+
+            @pl.when((z > part) & (z < 3))
+            def _():
+                send(block, block, out_send.at[0], out_recv.at[core], at.up).start()
+
+            @pl.when((z < part) & (z > 0))
+            def _():
+                send(block, block, out_send.at[1], out_recv.at[core], at.down).start()
+
+            send(block, block, out_send.at[2], out_recv.at[core], at.other_core).start()
+
+    def forward_x(n):
+        whole = activations[n][1]
+        arrived(whole.at[at.x_part], plane_recv.at[n, 0], at.across_x)
+        block = whole.at[at.x_part, 0:HALF]
+        send(block, block, plane_send.at[n, 2], plane_recv.at[n, 2], at.across_y).start()
+
+    def forward_y(n):
+        whole = activations[n][1]
+        arrived(whole.at[at.y_part], plane_recv.at[n, 1], at.across_y)
+        block = whole.at[at.y_part, HALF : 2 * HALF]
+        send(block, block, plane_send.at[n, 3], plane_recv.at[n, 3], at.across_x).start()
+
+    def far_halves(n):
+        whole = activations[n][1]
+        arrived(whole.at[at.far_part, 0:HALF], plane_recv.at[n, 2], at.across_y)
+        arrived(whole.at[at.far_part, HALF : 2 * HALF], plane_recv.at[n, 3], at.across_x)
+
+    cast(Q, 0, 3)
+    send_own(Q)
+    load(3).wait()
+
+    @pl.when(z == part)
+    def _():
+        out_all[core] = stage[1][...].astype(bf16)
+        send_out_rows()
+
+    for n, (peer, _) in enumerate(plane_peers):
+        send(len_all.at[part], len_all.at[part], len_send.at[n], len_recv.at[n], peer).start()
+    for k in range(1, 8):
+        send(
+            small_own,
+            small_all.at[shard],
+            small_send.at[k - 1],
+            small_recv.at[k - 1],
+            at.shard_after(k),
+        ).start()
+    cast(U, 4, 12)
+    cast(N, 12, 13)
+    load(13).wait()
+    load(14).wait()
+    forward(1, Q)
+    forward_out(1)
+    forward(2, Q)
+    send_own(U)
+    send_own(N)
+    for n, (peer, other) in enumerate(plane_peers):
+        arrived(len_all.at[other], len_recv.at[n], peer)
+    for k in range(1, 8):
+        arrived(small_all.at[(shard + 8 - k) % 8], small_recv.at[k - 1], at.shard_after(8 - k))
+    for number, row in enumerate((0, 8, 16, 24, 56, 96)):
+        for n in range(8):
+            source = row + n
+            vectors[number : number + 1, n * 128 : (n + 1) * 128] = small_all[
+                source // 13, source % 13 : source % 13 + 1
+            ]
+    for c in range(3):
+        for n in range(2):
+            source = 32 + 8 * c + 2 * part + n
+            columns = slice((2 * c + n) * 128, (2 * c + n + 1) * 128)
+            qkv_bias[:, columns] = small_all[source // 13, pl.ds(source % 13, 1)]
+    for g in range(8):
+        source = 64 + 4 * g + part
+        up_bias[:, g * 128 : (g + 1) * 128] = small_all[source // 13, pl.ds(source % 13, 1)]
+
+    sums[...] = jnp.zeros_like(sums)
+    d_qkv_bias[...] = jnp.zeros_like(d_qkv_bias)
+    d_up_bias[...] = jnp.zeros_like(d_up_bias)
+    block_rows = 64
+
+    def norm_rows(s):
+        @pl.loop(0, length // block_rows)
+        def _(i):
+            r = pl.ds(pl.multiple_of(i * block_rows, block_rows), block_rows)
+            values = x_all[s, r, :].astype(f32)
+            mean = jnp.mean(values, axis=-1, keepdims=True)
+            centred = values - mean
+            inverse = lax.rsqrt(
+                jnp.mean(centred * centred, axis=-1, keepdims=True) + NORM_EPSILON
+            )
+            stats[s, r, 0:1] = mean
+            stats[s, r, 1:2] = inverse
+            unit = centred * inverse
+            normed_one[s, r, :] = (unit * vectors[0:1] + vectors[1:2]).astype(bf16)
+            normed_two[s, r, :] = (unit * vectors[2:3] + vectors[3:4]).astype(bf16)
+
+    def live_rows(s):
+        index = lax.broadcasted_iota(jnp.int32, (length, 1), 0)
+        return index.astype(f32) < len_all[s][0:1, 0:1]
+
+    def rotate(value, sign):
+        return (
+            value * tables[0]
+            + sign * pltpu.roll(value, head_cols - ROT // 2, 1) * tables[1]
+            + sign * pltpu.roll(value, ROT // 2, 1) * tables[2]
+        )
+
+    def project(s):
+        norm_rows(s)
+        low, high = SPANS[Q]
+        value = nn(normed_one[s], flat(w_all[:, :, low:high])) + qkv_bias[...]
+        heads_qkv[s, :, 0:head_cols] = rotate(value[:, 0:head_cols], 1.0).astype(bf16)
+        heads_qkv[s, :, head_cols : 2 * head_cols] = rotate(
+            value[:, head_cols : 2 * head_cols], 1.0
+        ).astype(bf16)
+        heads_qkv[s, :, 2 * head_cols :] = value[:, 2 * head_cols :].astype(bf16)
+
+    def attend(s):
+        cot = cot_all[s]
+        back[s] = jnp.where(live_rows(s), cot, jnp.zeros_like(cot))
+        queries = heads_qkv[s, :, 0:head_cols]
+        keys = heads_qkv[s, :, head_cols : 2 * head_cols]
+        values = heads_qkv[s, :, 2 * head_cols :]
+        d_mixed = nt(back[s], flat(out_all[...])).astype(bf16)
+        row = lax.broadcasted_iota(jnp.int32, (length, length), 0)
+        column = lax.broadcasted_iota(jnp.int32, (length, length), 1)
+        allowed = (column <= row) & (column.astype(f32) < len_all[s][0:1, 0:1])
+        lane = lax.broadcasted_iota(jnp.int32, (length, head_cols), 1)
+        zero = jnp.zeros((), bf16)
+        mixed_sum = jnp.zeros((length, head_cols), f32)
+        d_queries = d_keys = d_values = mixed_sum
+        for h in range(head_cols // HD):
+            of_head = (lane >= h * HD) & (lane < (h + 1) * HD)
+            q_h, k_h, v_h, d_h = (
+                jnp.where(of_head, t, zero) for t in (queries, keys, values, d_mixed)
+            )
+            scores = jnp.where(allowed, nt(q_h, keys) * HD**-0.5, -1e30)
+            raised = jnp.exp(scores - jnp.max(scores, axis=-1, keepdims=True))
+            weights = raised * (1.0 / jnp.sum(raised, axis=-1, keepdims=True))
+            low = weights.astype(bf16)
+            mixed_sum = mixed_sum + nn(low, v_h)
+            d_weights = nt(d_h, values)
+            inner = jnp.sum(weights * d_weights, axis=-1, keepdims=True)
+            d_scores = (weights * (d_weights - inner)).astype(bf16)
+            d_queries = d_queries + nn(d_scores, k_h)
+            d_keys = d_keys + tn(d_scores, q_h)
+            d_values = d_values + tn(low, d_h)
+        mixed[s] = mixed_sum.astype(bf16)
+        for n, value in enumerate(
+            (rotate(d_queries * HD**-0.5, -1.0), rotate(d_keys * HD**-0.5, -1.0), d_values)
+        ):
+            rounded = value.astype(bf16)
+            columns = slice(n * head_cols, (n + 1) * head_cols)
+            d_projected[s, :, columns] = rounded
+            d_qkv_bias[:, columns] += jnp.sum(rounded.astype(f32), axis=0, keepdims=True)
+
+    forward(3, Q)
+    from_core(Q)
+
+    @pl.loop(0, 4)
+    def _(i):
+        @pl.when(i == 1)
+        def _():
+            forward_x(0)
+
+        @pl.when(i == 2)
+        def _():
+            forward_y(0)
+
+        @pl.when(i == 3)
+        def _():
+            far_halves(0)
+
+        project(near_first(i))
+
+        @pl.when(i == 0)
+        def _():
+            forward_out(2)
+            forward(1, U)
+
+        @pl.when(i == 2)
+        def _():
+            forward(1, N)
+
+    forward_out(3)
+    arrived(out_all.at[1 - core], out_recv.at[1 - core], at.other_core)
+
+    @pl.loop(0, 4)
+    def _(i):
+        @pl.when(i == 3)
+        def _():
+            far_halves(1)
+
+        attend(near_first(i))
+
+        @pl.when(i == 0)
+        def _():
+            forward_x(1)
+            forward_y(1)
+            forward(2, U)
+
+        @pl.when(i == 1)
+        def _():
+            forward(2, N)
+
+    def gradient(left, right, n):
+        low, high = SPANS[n]
+
+        @pl.loop(0, 8)
+        def _(f):
+            columns = pl.ds(pl.multiple_of(f * 128, 128), 128)
+            terms[f, :, low:high] = tn(flat(left[:, :, columns]), flat(right[...])).astype(bf16)
+
+    def to_core(n):
+        for other in range(4):
+            send(
+                piece(terms, 2 * other + 1 - core, n),
+                piece(core_in, other, n),
+                core_send.at[n, other],
+                core_recv.at[n, other],
+                at.other_core,
+            ).start()
+
+    def add_core(n):
+        low, high = SPANS[n]
+        for other in (3, 0, 2, 1):
+            arrived(piece(core_in, other, n), core_recv.at[n, other], at.other_core)
+            terms[2 * other + core, :, low:high] = (
+                terms[2 * other + core, :, low:high].astype(f32)
+                + core_in[other, :, low:high].astype(f32)
+            ).astype(bf16)
+
+    def pass_on(n, me, target):
+        low, high = SPANS[n]
+
+        @pl.when(z == me)
+        def _():
+            own = piece(terms, 2 * target + core, n)
+            if me not in (0, 3):
+                source = at.down if me < target else at.up
+                arrived(piece(line_in, target, n), line_recv.at[n, target], source)
+                terms[2 * target + core, :, low:high] = (
+                    terms[2 * target + core, :, low:high].astype(f32)
+                    + line_in[target, :, low:high].astype(f32)
+                ).astype(bf16)
+            slot = 4 if me == target + 1 else target
+            send(
+                own,
+                piece(line_in, slot, n),
+                line_send.at[n, target],
+                line_recv.at[n, slot],
+                at.up if me < target else at.down,
+            ).start()
+
+    def line_starts(n):
+        for target in (3, 2, 1):
+            pass_on(n, 0, target)
+        for target in (0, 1, 2):
+            pass_on(n, 3, target)
+
+    def line_step(n, step):
+        for me, target in (((1, 3), (2, 0)), ((1, 2), (2, 1)), ((2, 3), (1, 0)))[step]:
+            pass_on(n, me, target)
+
+    wholes = (qkv_all, up_all, down_all)
+
+    def line_ends(n):
+        low, high = SPANS[n]
+        total = 2 * z + core
+
+        def add(slot, source):
+            arrived(piece(line_in, slot, n), line_recv.at[n, slot], source)
+            terms[total, :, low:high] = (
+                terms[total, :, low:high].astype(f32) + line_in[slot, :, low:high].astype(f32)
+            ).astype(bf16)
+
+        @pl.when(z > 0)
+        def _():
+            add(z, at.down)
+
+        @pl.when(z < 3)
+        def _():
+            add(4, at.up)
+
+        own = piece(terms, total, n)
+        target = wholes[n].at[part]
+        send(own, target, all_send.at[n, 0], all_recv.at[n, 0], at.across_x).start()
+        send(own, target, all_send.at[n, 1], all_recv.at[n, 1], at.across_y).start()
+        pltpu.make_async_copy(own, target, keep_sem.at[n]).start()
+
+    def share(n):
+        whole = wholes[n]
+        arrived(whole.at[at.x_part], all_recv.at[n, 0], at.across_x)
+        block = whole.at[at.x_part, 0:64]
+        send(block, block, all_send.at[n, 2], all_recv.at[n, 2], at.across_y).start()
+        arrived(whole.at[at.y_part], all_recv.at[n, 1], at.across_y)
+        block = whole.at[at.y_part, 64:128]
+        send(block, block, all_send.at[n, 3], all_recv.at[n, 3], at.across_x).start()
+
+    def out_to_core():
+        send(
+            out_term.at[1 - core], out_core_in, rows_send.at[0], rows_recv.at[0], at.other_core
+        ).start()
+
+    def out_add(block):
+        out_line[...] = (out_line[...].astype(f32) + block.astype(f32)).astype(bf16)
+
+    def out_add_core():
+        arrived(out_core_in, rows_recv.at[0], at.other_core)
+        out_line[...] = out_term[core]
+        out_add(out_core_in[...])
+
+    def out_step(step):
+        @pl.when((z == step) & (z < part))
+        def _():
+            if step > 0:
+                arrived(out_line_in.at[0], rows_recv.at[1], at.down)
+                out_add(out_line_in[0])
+            send(out_line, out_line_in.at[0], rows_send.at[1], rows_recv.at[1], at.up).start()
+
+        @pl.when((z == 3 - step) & (z > part))
+        def _():
+            if step > 0:
+                arrived(out_line_in.at[1], rows_recv.at[2], at.up)
+                out_add(out_line_in[1])
+            send(out_line, out_line_in.at[1], rows_send.at[1], rows_recv.at[2], at.down).start()
+
+    def out_ends():
+        @pl.when(z == part)
+        def _():
+            @pl.when(z > 0)
+            def _():
+                arrived(out_line_in.at[0], rows_recv.at[1], at.down)
+                out_add(out_line_in[0])
+
+            @pl.when(z < 3)
+            def _():
+                arrived(out_line_in.at[1], rows_recv.at[2], at.up)
+                out_add(out_line_in[1])
+
+            for n, (peer, _) in enumerate(plane_peers):
+                send(out_line, out_grad, rows_send.at[2 + n], rows_recv.at[3], peer).start()
+            pltpu.make_async_copy(out_line, out_grad, keep_sem.at[3]).start()
+
+    gradient(normed_one, d_projected, Q)
+    to_core(Q)
+    for n in range(2):
+        out_term[n] = tn(flat(mixed[:, :, n * 128 : (n + 1) * 128]), flat(back[...])).astype(bf16)
+    out_to_core()
+    add_core(Q)
+    line_starts(Q)
+    out_add_core()
+    out_step(0)
+    forward(3, U)
+    forward(3, N)
+    from_core(U)
+    from_core(N)
+
+    halves = (slice(0, HALF), slice(HALF, 2 * HALF))
+    part_refs = (out_part, dx_part)
+    routes = (
+        (halves[0], at.across_x, at.x_part, at.across_y, at.y_part),
+        (halves[1], at.across_y, at.y_part, at.across_x, at.x_part),
+    )
+
+    def send_part(n, r, m):
+        half, peer, peer_part, _, _ = routes[r]
+        target = (at.far_part, peer_part)[m]
+        send(
+            part_refs[n].at[target, half],
+            plane_one.at[n, r, m],
+            part_send.at[n, r, m],
+            part_recv.at[n, r, m],
+            peer,
+        ).start()
+
+    def send_parts(n, i):
+        @pl.when(i == 0)
+        def _():
+            send_part(n, 0, 0)
+            send_part(n, 1, 0)
+
+        @pl.when(i == 1)
+        def _():
+            send_part(n, 0, 1)
+
+        @pl.when(i == 2)
+        def _():
+            send_part(n, 1, 1)
+
+    def turn_part(n, r):
+        half, peer, _, turn, turned = routes[r]
+        arrived(plane_one.at[n, r, 0], part_recv.at[n, r, 0], peer)
+        plane_turn[n, r] = (
+            part_refs[n][turned, half].astype(f32) + plane_one[n, r, 0].astype(f32)
+        ).astype(bf16)
+        send(
+            plane_turn.at[n, r],
+            plane_two.at[n, r],
+            part_send.at[n, r, 2],
+            part_recv.at[n, r, 2],
+            turn,
+        ).start()
+
+    def whole_part(n, r):
+        half, peer, _, turn, _ = routes[r]
+        arrived(plane_one.at[n, r, 1], part_recv.at[n, r, 1], peer)
+        arrived(plane_two.at[n, r], part_recv.at[n, r, 2], turn)
+        return (
+            part_refs[n][part, half].astype(f32)
+            + plane_one[n, r, 1].astype(f32)
+            + plane_two[n, r].astype(f32)
+        )
+
+    up_low, up_high = SPANS[U]
+    down_low, down_high = SPANS[N]
+
+    def feed(s):
+        value = nn(normed_two[s], flat(w_all[:, :, up_low:up_high])) + up_bias[...]
+        hidden[s] = value
+        low = (value * (0.5 * (1.0 + lax.erf(value * 2.0**-0.5)))).astype(bf16)
+        activated[s] = low
+        out_part[s] = (
+            nn(low, flat(w_all[:, :, down_low:down_high])) + nn(mixed[s], flat(out_all[...]))
+        ).astype(bf16)
+
+    def feed_back(s):
+        value = hidden[s]
+        slope = gelu_slope(value)
+        low = (nt(back[s], flat(w_all[:, :, down_low:down_high])) * slope).astype(bf16)
+        d_hidden[s] = low
+        d_up_bias[...] += jnp.sum(low.astype(f32), axis=0, keepdims=True)
+        d_two = nt(low, flat(w_all[:, :, up_low:up_high]))
+        d_one = nt(d_projected[s], flat(w_all[:, :, SPANS[Q][0] : SPANS[Q][1]]))
+        unit = (x_all[s].astype(f32) - stats[s][:, 0:1]) * stats[s][:, 1:2]
+        sums[0:1] += jnp.sum(d_one * unit, axis=0, keepdims=True)
+        sums[1:2] += jnp.sum(d_one, axis=0, keepdims=True)
+        sums[2:3] += jnp.sum(d_two * unit, axis=0, keepdims=True)
+        sums[3:4] += jnp.sum(d_two, axis=0, keepdims=True)
+        dx_part[s] = (d_one * vectors[0:1] + d_two * vectors[2:3]).astype(bf16)
+
+    @pl.loop(0, 4)
+    def _(i):
+        feed(far_first(i))
+        send_parts(0, i)
+
+        @pl.when(i == 1)
+        def _():
+            line_step(Q, 0)
+            out_step(1)
+
+        @pl.when(i == 3)
+        def _():
+            line_step(Q, 1)
+
+    gradient(activated, back, N)
+    to_core(N)
+    turn_part(0, 1)
+    turn_part(0, 0)
+    line_step(Q, 2)
+    out_step(2)
+    add_core(N)
+    line_starts(N)
+
+    @pl.loop(0, 4)
+    def _(i):
+        feed_back(far_first(i))
+        send_parts(1, i)
+
+        @pl.when(i == 1)
+        def _():
+            line_step(N, 0)
+            line_ends(Q)
+            out_ends()
+
+        @pl.when(i == 2)
+        def _():
+            line_step(N, 1)
+
+    gradient(normed_two, d_hidden, U)
+    to_core(U)
+    share(Q)
+    line_step(N, 2)
+    turn_part(1, 1)
+    turn_part(1, 0)
+    add_core(U)
+    line_starts(U)
+
+    small_part[...] = jnp.zeros_like(small_part)
+
+    def place(row, value):
+        small_part[row // 13, pl.ds(row % 13, 1)] = value
+
+    back_total = jnp.sum(back[part].astype(f32), axis=0, keepdims=True)
+    for n in range(8):
+        columns = slice(n * 128, (n + 1) * 128)
+        for number in range(4):
+            place(8 * number + n, sums[number : number + 1, columns])
+        place(56 + n, back_total[:, columns])
+        place(96 + n, back_total[:, columns])
+        place(64 + 4 * n + part, d_up_bias[:, columns])
+    for c in range(3):
+        for n in range(2):
+            columns = slice((2 * c + n) * 128, (2 * c + n + 1) * 128)
+            place(32 + 8 * c + 2 * part + n, d_qkv_bias[:, columns])
+    for k in range(1, 8):
+        send(
+            small_part.at[(shard + k) % 8],
+            small_in.at[k - 1],
+            total_send.at[k - 1],
+            total_recv.at[k - 1],
+            at.shard_after(k),
+        ).start()
+
+    line_step(U, 0)
+
+    for r in range(2):
+        half = halves[r]
+        live = live_rows(part)[half]
+        values = x_all[part, half].astype(f32)
+        summed = values + whole_part(0, r) + vectors[4:5] + vectors[5:6]
+        output[half] = jnp.where(live, summed, 0.0).astype(bf16)
+    line_ends(N)
+    line_step(U, 1)
+    total = small_part[shard]
+    for k in range(1, 8):
+        arrived(small_in.at[k - 1], total_recv.at[k - 1], at.shard_after(8 - k))
+        total = total + small_in[k - 1]
+    small_total[...] = total
+    for n, (peer, _) in enumerate(plane_peers):
+        send(
+            small_total, small_plane.at[part], total_send.at[7 + n], total_recv.at[7 + n], peer
+        ).start()
+    small_plane[part] = total
+    for r in range(2):
+        half = halves[r]
+        scaled = whole_part(1, r)
+        inverse = stats[part, half, 1:2]
+        unit = (x_all[part, half].astype(f32) - stats[part, half, 0:1]) * inverse
+        result = back[part, half].astype(f32) + inverse * (
+            scaled
+            - jnp.mean(scaled, axis=-1, keepdims=True)
+            - unit * jnp.mean(scaled * unit, axis=-1, keepdims=True)
+        )
+        input_grad[half] = result.astype(bf16)
+    line_step(U, 2)
+    share(N)
+    for n, (peer, other) in enumerate(plane_peers):
+        arrived(small_plane.at[other], total_recv.at[7 + n], peer)
+    small_sum[...] = (small_plane[0] + small_plane[1]) + (small_plane[2] + small_plane[3])
+    line_ends(U)
+    share(U)
+
+    @pl.when(z != part)
+    def _():
+        arrived(out_grad, rows_recv.at[3], at.across_x)
+        sent(out_line, rows_send.at[1], at.up)
+
+    @pl.when(z == part)
+    def _():
+        for n, (peer, _) in enumerate(plane_peers):
+            sent(out_line, rows_send.at[2 + n], peer)
+        pltpu.make_async_copy(out_line, out_grad, keep_sem.at[3]).wait()
+
+    sent(out_line, rows_send.at[0], at.other_core)
+    for n, (own, whole) in enumerate(activations):
+        sent(own, plane_send.at[n, 0], at.across_x)
+        sent(own, plane_send.at[n, 1], at.across_y)
+        sent(whole.at[part, 0:HALF], plane_send.at[n, 2], at.across_y)
+        sent(whole.at[part, 0:HALF], plane_send.at[n, 3], at.across_x)
+    for n, (peer, _) in enumerate(plane_peers):
+        sent(len_all.at[part], len_send.at[n], peer)
+        sent(small_total, total_send.at[7 + n], peer)
+    for k in range(1, 8):
+        sent(small_own, small_send.at[k - 1], at.shard_after(k))
+        sent(small_total, total_send.at[k - 1], at.shard_after(k))
+    for n in range(3):
+        for other in range(4):
+            block = piece(w_all, 2 * other + core, n)
+            sent(block, w_send.at[2, n, other], at.other_core)
+            sent(block, core_send.at[n, other], at.other_core)
+
+            @pl.when((other <= z) & (z < 3))
+            def _():
+                sent(block, w_send.at[0, n, other], at.up)
+
+            @pl.when((other >= z) & (z > 0))
+            def _():
+                sent(block, w_send.at[1, n, other], at.down)
+
+            @pl.when(z != other)
+            def _():
+                sent(block, line_send.at[n, other], at.up)
+
+    block = out_all.at[core]
+    sent(block, out_send.at[2], at.other_core)
+
+    @pl.when((z >= part) & (z < 3))
+    def _():
+        sent(block, out_send.at[0], at.up)
+
+    @pl.when((z <= part) & (z > 0))
+    def _():
+        sent(block, out_send.at[1], at.down)
+
+    for n in range(2):
+        for r in range(2):
+            for m in range(3):
+                sent(plane_turn.at[n, r], part_send.at[n, r, m], at.across_x)
+    for n, whole in enumerate(wholes):
+        arrived(whole.at[at.far_part, 0:64], all_recv.at[n, 2], at.across_y)
+        arrived(whole.at[at.far_part, 64:128], all_recv.at[n, 3], at.across_x)
+        own = piece(terms, shard, n)
+        sent(own, all_send.at[n, 0], at.across_x)
+        sent(own, all_send.at[n, 1], at.across_y)
+        sent(whole.at[part, 0:64], all_send.at[n, 2], at.across_y)
+        sent(whole.at[part, 64:128], all_send.at[n, 3], at.across_x)
+        pltpu.make_async_copy(own, whole.at[part], keep_sem.at[n]).wait()
+
+
+VMEM_SPEC = pl.BlockSpec(memory_space=pltpu.VMEM)
+HBM_SPEC = pl.BlockSpec(memory_space=pl.ANY)
+
+
+def whole_layer(lengths, x_own, cot_own, masters, tables):
+    shape = jax.ShapeDtypeStruct
+    vmem, dma = pltpu.VMEM, pltpu.SemaphoreType.DMA
+    bf16, f32 = jnp.bfloat16, jnp.float32
+    length = x_own.shape[0]
+    group = 4
+    head_cols, wide, rows = D // group, 2816, 128
+
+    def by_sequence(width, kind=bf16):
+        return vmem((group, length, width), kind)
+
+    return pl.pallas_call(
+        layer_kernel,
+        out_shape=(
+            shape(x_own.shape, bf16),
+            shape(x_own.shape, bf16),
+            shape((group, rows, 3 * head_cols), bf16),
+            shape((group, rows, FF // group), bf16),
+            shape((group, rows, D), bf16),
+            shape((rows, D), bf16),
+            shape((16, 128), f32),
+        ),
+        in_specs=[pl.BlockSpec(memory_space=pltpu.SMEM)]
+        + [HBM_SPEC] * 6
+        + [VMEM_SPEC, VMEM_SPEC],
+        out_specs=(VMEM_SPEC, VMEM_SPEC) + (HBM_SPEC,) * 4 + (VMEM_SPEC,),
+        scratch_shapes=[
+            by_sequence(D),
+            by_sequence(D),
+            vmem((group, 8, 128), f32),
+            vmem((8, rows, wide), bf16),
+            vmem((2, rows, D), bf16),
+            vmem((16, 128), f32),
+            vmem((8, 16, 128), f32),
+            vmem((8, D), f32),
+            vmem((1, 3 * head_cols), f32),
+            vmem((1, FF // group), f32),
+            by_sequence(128, f32),
+            by_sequence(D),
+            by_sequence(D),
+            by_sequence(D),
+            by_sequence(3 * head_cols),
+            by_sequence(head_cols),
+            by_sequence(3 * head_cols),
+            by_sequence(FF // group, f32),
+            by_sequence(FF // group),
+            by_sequence(D),
+            by_sequence(D),
+            vmem((8, rows, wide), bf16),
+            vmem((2, rows, D), bf16),
+            vmem((8, D), f32),
+            vmem((1, 3 * head_cols), f32),
+            vmem((1, FF // group), f32),
+            vmem((8, 16, 128), f32),
+            vmem((2, 2, 2, HALF, D), bf16),
+            vmem((2, 2, HALF, D), bf16),
+            vmem((2, 2, HALF, D), bf16),
+            vmem((4, rows, wide), bf16),
+            vmem((5, rows, wide), bf16),
+            vmem((rows, D), bf16),
+            vmem((rows, D), bf16),
+            vmem((2, rows, D), bf16),
+            vmem((7, 16, 128), f32),
+            vmem((16, 128), f32),
+            vmem((4, 16, 128), f32),
+            dma((15,)),
+            dma((2, 4)),
+            dma((2, 4)),
+            dma((3,)),
+            dma((3,)),
+            dma((3, 3, 4)),
+            dma((3, 8)),
+            dma((3,)),
+            dma((2,)),
+            dma((7,)),
+            dma((7,)),
+            dma((2, 2, 3)),
+            dma((2, 2, 3)),
+            dma((3, 4)),
+            dma((3, 4)),
+            dma((3, 4)),
+            dma((3, 5)),
+            dma((5,)),
+            dma((4,)),
+            dma((3, 4)),
+            dma((3, 4)),
+            dma((4,)),
+            dma((10,)),
+            dma((10,)),
+        ],
+        compiler_params=pltpu.CompilerParams(
+            collective_id=0, has_side_effects=True, vmem_limit_bytes=62 << 20
+        ),
+        name="layer",
+    )(lengths, x_own, cot_own, *masters, tables)
+
+
+def rope_tables(length, heads):
+    half = ROT // 2
+    angle = np.arange(length)[:, None] * ROPE_BASE ** (-2.0 * np.arange(half) / ROT)[None]
+    table = np.zeros((3, length, HD), np.float32)
+    table[0] = 1.0
+    table[0, :, :half] = table[0, :, half:ROT] = np.cos(angle)
+    table[1, :, :half] = -np.sin(angle)
+    table[2, :, half:ROT] = np.sin(angle)
+    return jnp.asarray(np.tile(table, (1, 1, heads)))
 
 
 def local_split(
@@ -229,16 +1245,29 @@
     parts, shards = lax.axis_size("dp"), lax.axis_size("fsdp")
     part, shard = lax.axis_index("dp"), lax.axis_index("fsdp")
     length = tokens_in.shape[1]
+    update = (masters, firsts, seconds)
+    if (parts, shards) == (4, 8):
+        tall = tuple(masters[:4]) + (small_master.reshape(-1, 128),)
+        output, input_grad, qkv_grad, up_grad, down_grad, out_grad, small_sum = whole_layer(
+            lengths, tokens_in[0], cotangent[0], tall, rope_tables(length, HEADS // parts)
+        )
+        grads = (qkv_grad, out_grad, up_grad, down_grad, small_sum[: tall[4].shape[0]])
+        return (output[None], input_grad[None]) + lamb_split(*update, grads)
+
     head_cols = D // parts
-    ff_cols = FF // parts
     ff_rows = down_master.shape[0] // parts
-
     qkv_own = sliced(qkv_master, part, parts, 3).astype(jnp.bfloat16)
     up_own = sliced(up_master, part, parts, shards).astype(jnp.bfloat16)
     down_own = lax.dynamic_slice_in_dim(down_master, part * ff_rows, ff_rows).astype(jnp.bfloat16)
     out_own = out_master.astype(jnp.bfloat16)
     small_own = small_master.astype(jnp.bfloat16)
 
+    def small_vectors(small_all):
+        vectors = split_small(small_all)
+        vectors[4] = sliced(vectors[4][None], part, parts, 3)[0]
+        vectors[6] = sliced(vectors[6][None], part, parts, shards)[0]
+        return vectors
+
     def over_shards(own):
         return lax.all_gather(own, "fsdp", axis=0, tiled=True)
 
@@ -247,12 +1276,9 @@
     lengths_all = lax.all_gather(lengths, "dp", axis=0, tiled=True)
     qkv_weight, up_weight, down_weight = (over_shards(w) for w in (qkv_own, up_own, down_own))
     out_weight = lax.dynamic_slice_in_dim(over_shards(out_own), part * head_cols, head_cols)
-    gain_one, shift_one, gain_two, shift_two, qkv_bias, out_bias, up_bias, down_bias = split_small(
-        over_shards(small_own).astype(jnp.float32)
-    )
-    qkv_bias = sliced(qkv_bias[None], part, parts, 3)[0]
-    up_bias = sliced(up_bias[None], part, parts, shards)[0]
-
+    gain_one, shift_one, gain_two, shift_two, qkv_bias, out_bias, up_bias, down_bias = (
+        small_vectors(over_shards(small_own).astype(jnp.float32))
+    )
     out_part, scaled_part, terms, sums = layer(
         x_all,
         cotangent_all,
@@ -261,6 +1287,7 @@
         (gain_one, shift_one, gain_two, shift_two, qkv_bias, up_bias),
         part,
     )
+    norm_sums, d_qkv_bias, d_up_bias = sums
     out_sum = lax.psum_scatter(out_part, "dp", scatter_dimension=0, tiled=True)
     scaled = lax.psum_scatter(scaled_part, "dp", scatter_dimension=0, tiled=True)
     out_sum, scaled = out_sum.astype(jnp.float32), scaled.astype(jnp.float32)
@@ -268,15 +1295,6 @@
     inputs = tokens_in[0].astype(jnp.float32)
     live = (jnp.arange(length) < lengths[0]).astype(jnp.float32)[:, None]
     back = cotangent[0].astype(jnp.float32) * live
-    unit_rows, inverse_rows = normalize(inputs)
-    output = ((inputs + out_sum + out_bias + down_bias) * live).astype(jnp.bfloat16)
-    input_grad = back + inverse_rows * (
-        scaled
-        - jnp.mean(scaled, axis=-1, keepdims=True)
-        - unit_rows * jnp.mean(scaled * unit_rows, axis=-1, keepdims=True)
-    )
-
-    norm_sums, d_qkv_bias, d_up_bias = sums
     back_total = jnp.sum(back, axis=0)
 
     def spread(values, pieces):
@@ -297,7 +1315,6 @@
     small_sum = lax.psum(small_grad, ("dp", "fsdp"))
     small_rows = small_master.shape[0]
     small_sum = lax.dynamic_slice_in_dim(small_sum, shard * small_rows, small_rows)
-
     qkv_term, out_term, up_term, down_term = terms
     out_wide = lax.dynamic_update_slice_in_dim(
         jnp.zeros((D, D), jnp.bfloat16), out_term, part * head_cols, axis=0
@@ -307,16 +1324,216 @@
         own = lax.psum_scatter(term, "fsdp", scatter_dimension=0, tiled=True)
         return lax.all_gather(own, "dp", axis=0, tiled=False).astype(jnp.float32)
 
-    qkv_sum = joined(to_owner(qkv_term), 3)
-    up_sum = joined(to_owner(up_term), shards)
-    down_sum = to_owner(down_term).reshape(down_master.shape)
-    out_sum_grad = lax.psum(
-        lax.psum_scatter(out_wide, "fsdp", scatter_dimension=0, tiled=True), "dp"
-    ).astype(jnp.float32)
-    reduced = (qkv_sum, out_sum_grad, up_sum, down_sum, small_sum)
-    return (output[None], input_grad.astype(jnp.bfloat16)[None]) + lamb(
-        masters, firsts, seconds, reduced
-    )
+    reduced = (
+        joined(to_owner(qkv_term), 3),
+        lax.psum(
+            lax.psum_scatter(out_wide, "fsdp", scatter_dimension=0, tiled=True), "dp"
+        ).astype(jnp.float32),
+        joined(to_owner(up_term), shards),
+        to_owner(down_term).reshape(down_master.shape),
+        small_sum,
+    )
+
+    unit_rows, inverse_rows = normalize(inputs)
+    output = ((inputs + out_sum + out_bias + down_bias) * live).astype(jnp.bfloat16)
+    input_grad = back + inverse_rows * (
+        scaled
+        - jnp.mean(scaled, axis=-1, keepdims=True)
+        - unit_rows * jnp.mean(scaled * unit_rows, axis=-1, keepdims=True)
+    )
+    return (output[None], input_grad.astype(jnp.bfloat16)[None]) + lamb(*update, reduced)
+
+
+def lamb_rows(first_old, second_old, master, grad):
+    first_new = BETA_ONE * first_old + (1.0 - BETA_ONE) * grad
+    second_new = BETA_TWO * second_old + (1.0 - BETA_TWO) * grad * grad
+    update = first_new / (jnp.sqrt(second_new) + ADAM_EPSILON) + DECAY * master
+    return first_new, second_new, update
+
+
+def lane_sums(values):
+    squares = jnp.sum(values * values, axis=0, keepdims=True)
+    total = squares[:, 0:128]
+    for n in range(1, squares.shape[1] // 128):
+        total = total + squares[:, n * 128 : (n + 1) * 128]
+    return total
+
+
+def moments_kernel(*refs):
+    qkv_grad, out_grad, up_grad, down_grad, small_grad = refs[0:5]
+    masters, firsts, seconds = refs[5:10], refs[10:15], refs[15:20]
+    first_news, second_news, updates = refs[20:25], refs[25:30], refs[30:35]
+    squares = refs[35]
+    step = pl.program_id(0)
+
+    @pl.when(step == 0)
+    def _():
+        squares[...] = jnp.zeros_like(squares)
+
+    def one(number, span, grad):
+        index = (slice(None), span)
+        first_new, second_new, update = lamb_rows(
+            firsts[number][index], seconds[number][index], masters[number][index], grad
+        )
+        first_news[number][index] = first_new
+        second_news[number][index] = second_new
+        updates[number][index] = update
+        return lane_sums(masters[number][index]), lane_sums(update)
+
+    def add(number, pairs):
+        weight, update = pairs[0]
+        for more_weight, more_update in pairs[1:]:
+            weight, update = weight + more_weight, update + more_update
+        squares[number : number + 1] += weight
+        squares[8 + number : 9 + number] += update
+
+    f32 = jnp.float32
+    parts = qkv_grad.shape[0]
+    width = qkv_grad.shape[2] // 3
+    add(
+        0,
+        [
+            one(
+                0,
+                slice((c * parts + d) * width, (c * parts + d + 1) * width),
+                qkv_grad[d, :, c * width : (c + 1) * width].astype(f32),
+            )
+            for c in range(3)
+            for d in range(parts)
+        ],
+    )
+    add(1, [one(1, slice(None), out_grad[...].astype(f32))])
+    pieces = up_grad.shape[2] // 128
+    add(
+        2,
+        [
+            one(
+                2,
+                slice((g * parts + d) * 128, (g * parts + d + 1) * 128),
+                up_grad[d, :, g * 128 : (g + 1) * 128].astype(f32),
+            )
+            for g in range(pieces)
+            for d in range(parts)
+        ],
+    )
+    add(3, [one(3, slice(None), down_grad[0].astype(f32))])
+
+    @pl.when(step == 0)
+    def _():
+        first_new, second_new, update = lamb_rows(
+            firsts[4][...], seconds[4][...], masters[4][...], small_grad[...]
+        )
+        first_news[4][...] = first_new
+        second_news[4][...] = second_new
+        updates[4][...] = update
+        squares[4:5] += lane_sums(masters[4][...])
+        squares[12:13] += lane_sums(update)
+
+
+def lamb_specs(masters, steps):
+    specs = [pl.BlockSpec((m.shape[0] // steps, m.shape[1]), lambda i: (i, 0)) for m in masters[:4]]
+    return specs + [pl.BlockSpec(masters[4].shape, lambda i: (0, 0))]
+
+
+def moments(grads, masters, firsts, seconds, steps=8):
+    qkv_grad, out_grad, up_grad, down_grad, small_grad = grads
+    shape = jax.ShapeDtypeStruct
+    each = lamb_specs(masters, steps)
+    rows = qkv_grad.shape[1]
+    halves = steps // qkv_grad.shape[0]
+    grad_specs = [
+        pl.BlockSpec((qkv_grad.shape[0], rows // steps, qkv_grad.shape[2]), lambda i: (0, i, 0)),
+        each[1],
+        pl.BlockSpec((up_grad.shape[0], rows // steps, up_grad.shape[2]), lambda i: (0, i, 0)),
+        pl.BlockSpec(
+            (1, rows // halves, down_grad.shape[2]), lambda i: (i // halves, i % halves, 0)
+        ),
+        each[4],
+    ]
+    out = [shape(m.shape, jnp.float32) for m in masters]
+    results = pl.pallas_call(
+        moments_kernel,
+        grid=(steps,),
+        in_specs=grad_specs + each * 3,
+        out_specs=each * 3 + [pl.BlockSpec((16, 128), lambda i: (0, 0))],
+        out_shape=out * 3 + [shape((16, 128), jnp.float32)],
+        compiler_params=pltpu.CompilerParams(vmem_limit_bytes=40 << 20),
+        name="moments",
+    )(*grads, *masters, *firsts, *seconds)
+    return results[0:5], results[5:10], results[10:15], results[15]
+
+
+def norms_kernel(squares, total, steps, everyone, send_sem, recv_sem):
+    shard, part = lax.axis_index("fsdp"), lax.axis_index("dp")
+    peers = [(part, (shard + k) % 8) for k in range(1, 8)]
+    barrier = pltpu.get_barrier_semaphore()
+    for peer in peers:
+        pl.semaphore_signal(barrier, inc=1, device_id=peer, device_id_type=MESH_ID)
+    pl.semaphore_wait(barrier, 7)
+    for k in range(1, 8):
+        send(
+            squares, everyone.at[shard], send_sem.at[k - 1], recv_sem.at[k - 1], peers[k - 1]
+        ).start()
+    everyone[shard] = squares[...]
+    for k in range(1, 8):
+        arrived(everyone.at[(shard + 8 - k) % 8], recv_sem.at[k - 1], peers[7 - k])
+    for k in range(1, 8):
+        sent(squares, send_sem.at[k - 1], peers[k - 1])
+    summed = everyone[0]
+    for k in range(1, 8):
+        summed = summed + everyone[k]
+    norms = jnp.sqrt(jnp.sum(summed, axis=1, keepdims=True))
+    total[...] = jnp.broadcast_to(norms, (16, 128))
+    steps[...] = jnp.broadcast_to(RATE * (norms[0:8] / norms[8:16]), (8, 128))
+
+
+def norms(squares):
+    shape = jax.ShapeDtypeStruct
+    dma = pltpu.SemaphoreType.DMA
+    return pl.pallas_call(
+        norms_kernel,
+        out_shape=(shape((16, 128), jnp.float32), shape((8, 128), jnp.float32)),
+        in_specs=[VMEM_SPEC],
+        out_specs=(VMEM_SPEC,) * 2,
+        scratch_shapes=[pltpu.VMEM((8, 16, 128), jnp.float32), dma((7,)), dma((7,))],
+        compiler_params=pltpu.CompilerParams(collective_id=2, has_side_effects=True),
+        name="norms",
+    )(squares)
+
+
+def step_kernel(*refs):
+    scales, masters, updates, news = refs[0], refs[1:6], refs[6:11], refs[11:16]
+    for number in range(5):
+        scale = scales[number : number + 1, 0:1]
+        news[number][...] = masters[number][...] - scale * updates[number][...]
+
+
+def step_masters(scales, masters, updates, steps=8):
+    each = lamb_specs(masters, steps)
+    return pl.pallas_call(
+        step_kernel,
+        grid=(steps,),
+        in_specs=[pl.BlockSpec((8, 128), lambda i: (0, 0))] + each * 2,
+        out_specs=each,
+        out_shape=[jax.ShapeDtypeStruct(m.shape, jnp.float32) for m in masters],
+        compiler_params=pltpu.CompilerParams(vmem_limit_bytes=40 << 20),
+        name="step_masters",
+    )(scales, *masters, *updates)
+
+
+def lamb_split(masters, firsts, seconds, grads):
+    def tall(arrays):
+        return tuple(arrays[:4]) + (arrays[4].reshape(-1, 128),)
+
+    def flat_small(arrays):
+        return tuple(arrays[:4]) + (arrays[4].reshape(-1),)
+
+    masters, firsts, seconds = tall(masters), tall(firsts), tall(seconds)
+    first_news, second_news, updates, squares = moments(grads, masters, firsts, seconds)
+    total, scales = norms(squares)
+    news = step_masters(scales, masters, updates)
+    lamb_norms = jnp.stack([total[0:5, 0], total[8:13, 0]])
+    return flat_small(news) + flat_small(first_news) + flat_small(second_news) + (lamb_norms,)
 
 
 def lamb(masters, firsts, seconds, reduced):

time: 638 us -> 207 us (0.32)
  waiting for transfers between devices: 298 us -> 0 us
  Pallas kernels: 0 us -> 178 us
  blocking collectives: 93.4 us -> 0 us
  matrix products: 78.1 us -> 0 us
  other arithmetic: 60.6 us -> 0.58 us
  local copies, waits for them, and re-layouts: 80.2 us -> 26.1 us
  between operations: 22 us -> 1.44 us
    pallas_call x0 -> x4, Pallas kernels: none -> 178 us  [the longest x1 152 us: whole_layer(): pl.pallas_call(layer_kernel, out_shape=(shape(x_own.shape, bf16), shape(x...]
    reduce_scatter x6 -> x0, waiting for transfers between devices: 170 us -> none  [the longest x3 95.4 us: to_owner(): own = lax.psum_scatter(term, 'fsdp', scatter_dimension=0, tiled=True)]
    all_gather x8 -> x0, waiting for transfers between devices: 94.8 us -> none  [the longest x4 90 us: over_shards(): return lax.all_gather(own, 'fsdp', axis=0, tiled=True)]
    dot_general x17 -> x0, matrix products: 72.9 us -> none  [the longest x4 20.2 us: against(): lax.dot_general(left, right, (((1,), (1,)), ((), ())), preferred_element_...]
    psum x2 -> x0, blocking collectives: 54.6 us -> none  [the longest x1 39.9 us: local_split(): small_sum = lax.psum(small_grad, ('dp', 'fsdp'))]
    psum x1 -> x0, waiting for transfers between devices: 32.2 us -> none  [local_split(): lax.psum(lax.psum_scatter(out_wide, 'fsdp', scatter_dimension=0, tiled=Tr...]
    all_gather x2 -> x0, blocking collectives: 30.8 us -> none  [the longest x1 15.7 us: over_shards(): return lax.all_gather(own, 'fsdp', axis=0, tiled=True)]
    reduce_sum x13 -> x0, other arithmetic: 29 us -> none  [the longest x6 21.3 us: local_squares(): return jnp.stack([jnp.sum(array_in * array_in) for array_in in arrays])]
  transfers between devices with their start and end apart: 15 -> 0, of which waited for: 13 -> 0; matrix products, arithmetic and copies ran while one was open for 29% -> 0% of each run, Pallas kernels for 0% -> 0%
where the time goes in v5:
time: 207 us; the launch traced here: 206 us
  Pallas kernels  178 us (86%)
  local copies, waits for them, and re-layouts  26.1 us (13%)
    pallas_call x1, Pallas kernels, whole_layer(): pl.pallas_call(layer_kernel, out_shape=(shape(x_own.shape, bf16), shape(x...  152 us
    unnamed x58, local copies, waits for them, and re-layouts  25.3 us
    pallas_call x1, Pallas kernels, moments(): pl.pallas_call(moments_kernel, grid=(steps,), in_specs=grad_specs + each...  14.2 us
    pallas_call x1, Pallas kernels, norms(): pl.pallas_call(norms_kernel, out_shape=(shape((16, 128), jnp.float32), sh...  6.98 us
    pallas_call x1, Pallas kernels, step_masters(): pl.pallas_call(step_kernel, grid=(steps,), in_specs=[pl.BlockSpec((8, 128...  4.25 us

profile of v5, /device:TPU:0, one launch (start us, length us, event | category | flops | bytes accessed | tf_op | source)
XLA Modules:
  0.0 205.6 jit_solution(17957203533279546555)
XLA Ops:
  1.4 152.1 %layer.1 = (bf16[256,1024]{1,0:T(8,128)(2,1)}, bf16[256,1024]{1,0:T(8,128)(2,1)}, bf16[4,128,768]{2,1,0:T(8,128)(2,1)}, bf16[4,128,1024]{2,1,0:T(8,128)(2,1)}, b...) custom-call(s32[1]{0:T(128)S(6)} %copy.39.length_own, bf16[256,1024]{1,0:T(8,128)(2,1)} %bitcast.19, ...), custom_call_target="tpu_custom_call" | custom-call | tf_op jit(solution)/shard_map/layer/pallas_call | solution.py:1125
  153.5 1.4 copy-done.2
  154.9 1.4 copy-done.10
  156.3 1.4 copy-done.11
  157.7 1.2 copy-done.12
  159.0 1.2 copy-done.13
  160.2 1.1 copy-done.14
  161.3 1.0 copy-done.16
  162.4 0.9 copy-done.19
  164.0 14.2 %moments.1 = (f32[128,3072]{1,0:T(8,128)}, f32[128,1024]{1,0:T(8,128)}, f32[128,4096]{1,0:T(8,128)}, f32[512,1024]{1,0:T(8,128)}, f32[13,128]{1,0:T(8,128)}, /*i...) custom-call(bf16[4,128,768]{2,1,0:T(8,128)(2,1)S(1)} %copy-done.14, ...), custom_call_target="tpu_custom_call" | custom-call | tf_op jit(solution)/shard_map/moments/pallas_call | solution.py:1454
  178.2 1.3 copy-done.5
  179.5 1.1 copy-done.8
  180.7 0.8 copy-done.17
  182.1 7.0 %norms.1 = (f32[16,128]{1,0:T(8,128)}, f32[8,128]{1,0:T(8,128)}) custom-call(f32[16,128]{1,0:T(8,128)} %copy-done.24), custom_call_target="tpu_custom_call" | custom-call | tf_op jit(solution)/shard_map/norms/pallas_call | solution.py:1493
  189.0 0.8 slice_reduce_fusion.1
  190.4 1.6 copy-done.1
  192.0 1.4 copy-done.3
  193.4 1.6 copy-done.6
  195.0 1.6 copy-done.7
  196.6 1.4 copy-done.9
  198.0 1.0 copy-done.18
  199.8 4.2 %step_masters.1 = (f32[128,3072]{1,0:T(8,128)}, f32[128,1024]{1,0:T(8,128)}, f32[128,4096]{1,0:T(8,128)}, f32[512,1024]{1,0:T(8,128)}, f32[13,128]{1,0:T(8,128)}) custom-call(f32[8,128]{1,0:T(8,128)S(1)} %copy-done.25, f32[128,3072]{1,0:T(8,128)S(1)} %copy-done.3, f32[128,1024]{1,0:T(8,128)S(1)} %copy-done.4, f32[128,4096]{1,0:T(8,128)S(1)} %copy-done, ...), custom_call_target="tpu_custom_call" | custom-call | tf_op jit(solution)/shard_map/step_masters/pallas_call | solution.py:1513
  204.0 0.8 copy.40
  204.8 0.8 copy.41
  (40 shorter events, 2.6 us)
Async XLA Ops:
  1.3 152.2 %copy-start.4 = (f32[128,1024]{1,0:T(8,128)S(1)}, f32[128,1024]{1,0:T(8,128)}, u32[]{:S(2)}) copy-start(f32[128,1024]{1,0:T(8,128)} %refs_2_.1) | copy-start | bytes 1572868
  1.3 152.2 %copy-start.15 = (f32[128,1024]{1,0:T(8,128)S(1)}, f32[128,1024]{1,0:T(8,128)}, u32[]{:S(2)}) copy-start(f32[128,1024]{1,0:T(8,128)} %refs_11_.1) | copy-start | bytes 1572868
  1.3 152.2 %copy-start.20 = (f32[1664]{0:T(1024)S(1)}, f32[1664]{0:T(1024)}, u32[]{:S(2)}) copy-start(f32[1664]{0:T(1024)} %param.26) | copy-start | bytes 19972
  1.3 152.2 %copy-start.21 = (f32[1664]{0:T(1024)S(1)}, f32[1664]{0:T(1024)}, u32[]{:S(2)}) copy-start(f32[1664]{0:T(1024)} %param.31) | copy-start | bytes 19972
  1.3 152.2 %copy-start.22 = (f32[1664]{0:T(1024)S(1)}, f32[1664]{0:T(1024)}, u32[]{:S(2)}) copy-start(f32[1664]{0:T(1024)} %param.36) | copy-start | bytes 19972
  153.5 1.4 copy-start.2
  154.9 1.4 copy-start.10
  156.3 1.4 copy-start.11
  157.7 1.2 copy-start.12
  159.0 1.2 copy-start.13
  160.2 1.1 copy-start.14
  161.3 1.0 copy-start.16
  162.4 0.9 copy-start.19
  164.0 26.4 %copy-start = (f32[128,4096]{1,0:T(8,128)S(1)}, f32[128,4096]{1,0:T(8,128)}, u32[]{:S(2)}) copy-start(f32[128,4096]{1,0:T(8,128)} %refs_3_.1) | copy-start | bytes 6291460
  178.2 1.3 copy-start.5
  179.5 1.1 copy-start.8
  190.4 1.6 copy-start.1
  192.0 1.4 copy-start.3
  193.4 1.6 copy-start.6
  195.0 1.6 copy-start.7
  196.6 1.4 copy-start.9
  198.0 1.0 copy-start.18
  199.8 4.3 %copy-start.27 = (bf16[256,1024]{1,0:T(8,128)(2,1)S(1)}, bf16[256,1024]{1,0:T(8,128)(2,1)}, u32[]{:S(2)}) copy-start(bf16[256,1024]{1,0:T(8,128)(2,1)} %get-tuple-element.48) | copy-start | bytes 1572868
  199.8 5.0 %copy-start.26 = (bf16[256,1024]{1,0:T(8,128)(2,1)S(1)}, bf16[256,1024]{1,0:T(8,128)(2,1)}, u32[]{:S(2)}) copy-start(bf16[256,1024]{1,0:T(8,128)(2,1)} %get-tuple-element.49) | copy-start | bytes 1572868
  (4 other events, 2.8 us)

commit v6 on v5

--- a/solution.py
+++ b/solution.py
@@ -1252,7 +1252,7 @@
             lengths, tokens_in[0], cotangent[0], tall, rope_tables(length, HEADS // parts)
         )
         grads = (qkv_grad, out_grad, up_grad, down_grad, small_sum[: tall[4].shape[0]])
-        return (output[None], input_grad[None]) + lamb_split(*update, grads)
+        return lamb_split(*update, grads, (output, input_grad))
 
     head_cols = D // parts
     ff_rows = down_master.shape[0] // parts
@@ -1362,8 +1362,8 @@
 def moments_kernel(*refs):
     qkv_grad, out_grad, up_grad, down_grad, small_grad = refs[0:5]
     masters, firsts, seconds = refs[5:10], refs[10:15], refs[15:20]
-    first_news, second_news, updates = refs[20:25], refs[25:30], refs[30:35]
-    squares = refs[35]
+    first_news, second_news, updates, kept = refs[20:25], refs[25:30], refs[30:35], refs[35:40]
+    squares = refs[40]
     step = pl.program_id(0)
 
     @pl.when(step == 0)
@@ -1372,13 +1372,17 @@
 
     def one(number, span, grad):
         index = (slice(None), span)
+        master = masters[number][index]
         first_new, second_new, update = lamb_rows(
-            firsts[number][index], seconds[number][index], masters[number][index], grad
+            firsts[number][index], seconds[number][index], master, grad
         )
         first_news[number][index] = first_new
         second_news[number][index] = second_new
-        updates[number][index] = update
-        return lane_sums(masters[number][index]), lane_sums(update)
+        rows = masters[number].shape[0]
+        place = (pl.ds(pl.multiple_of(step * rows, rows), rows), span)
+        updates[number][place] = update
+        kept[number][place] = master
+        return lane_sums(master), lane_sums(update)
 
     def add(number, pairs):
         weight, update = pairs[0]
@@ -1426,6 +1430,7 @@
         first_news[4][...] = first_new
         second_news[4][...] = second_new
         updates[4][...] = update
+        kept[4][...] = masters[4][...]
         squares[4:5] += lane_sums(masters[4][...])
         squares[12:13] += lane_sums(update)
 
@@ -1451,19 +1456,20 @@
         each[4],
     ]
     out = [shape(m.shape, jnp.float32) for m in masters]
+    near = [pltpu.VMEM(m.shape, jnp.float32) for m in masters]
     results = pl.pallas_call(
         moments_kernel,
         grid=(steps,),
         in_specs=grad_specs + each * 3,
-        out_specs=each * 3 + [pl.BlockSpec((16, 128), lambda i: (0, 0))],
-        out_shape=out * 3 + [shape((16, 128), jnp.float32)],
-        compiler_params=pltpu.CompilerParams(vmem_limit_bytes=40 << 20),
+        out_specs=each * 2 + [VMEM_SPEC] * 10 + [pl.BlockSpec((16, 128), lambda i: (0, 0))],
+        out_shape=out * 2 + near * 2 + [shape((16, 128), jnp.float32)],
+        compiler_params=pltpu.CompilerParams(vmem_limit_bytes=44 << 20),
         name="moments",
     )(*grads, *masters, *firsts, *seconds)
-    return results[0:5], results[5:10], results[10:15], results[15]
-
-
-def norms_kernel(squares, total, steps, everyone, send_sem, recv_sem):
+    return results[0:5], results[5:10], results[10:15], results[15:20], results[20]
+
+
+def norms_kernel(squares, total, everyone, send_sem, recv_sem):
     shard, part = lax.axis_index("fsdp"), lax.axis_index("dp")
     peers = [(part, (shard + k) % 8) for k in range(1, 8)]
     barrier = pltpu.get_barrier_semaphore()
@@ -1477,51 +1483,77 @@
     everyone[shard] = squares[...]
     for k in range(1, 8):
         arrived(everyone.at[(shard + 8 - k) % 8], recv_sem.at[k - 1], peers[7 - k])
-    for k in range(1, 8):
-        sent(squares, send_sem.at[k - 1], peers[k - 1])
     summed = everyone[0]
     for k in range(1, 8):
         summed = summed + everyone[k]
     norms = jnp.sqrt(jnp.sum(summed, axis=1, keepdims=True))
     total[...] = jnp.broadcast_to(norms, (16, 128))
-    steps[...] = jnp.broadcast_to(RATE * (norms[0:8] / norms[8:16]), (8, 128))
+    for k in range(1, 8):
+        sent(squares, send_sem.at[k - 1], peers[k - 1])
 
 
 def norms(squares):
-    shape = jax.ShapeDtypeStruct
     dma = pltpu.SemaphoreType.DMA
     return pl.pallas_call(
         norms_kernel,
-        out_shape=(shape((16, 128), jnp.float32), shape((8, 128), jnp.float32)),
+        out_shape=jax.ShapeDtypeStruct((16, 128), jnp.float32),
         in_specs=[VMEM_SPEC],
-        out_specs=(VMEM_SPEC,) * 2,
+        out_specs=VMEM_SPEC,
         scratch_shapes=[pltpu.VMEM((8, 16, 128), jnp.float32), dma((7,)), dma((7,))],
-        compiler_params=pltpu.CompilerParams(collective_id=2, has_side_effects=True),
+        compiler_params=pltpu.CompilerParams(
+            collective_id=1, has_side_effects=True, vmem_limit_bytes=2 << 20
+        ),
         name="norms",
     )(squares)
 
 
 def step_kernel(*refs):
-    scales, masters, updates, news = refs[0], refs[1:6], refs[6:11], refs[11:16]
+    total, masters, updates, layer_outs = refs[0], refs[1:6], refs[6:11], refs[11:13]
+    news, outs, lamb_norms = refs[13:18], refs[18:20], refs[20]
+    step = pl.program_id(0)
     for number in range(5):
-        scale = scales[number : number + 1, 0:1]
-        news[number][...] = masters[number][...] - scale * updates[number][...]
-
-
-def step_masters(scales, masters, updates, steps=8):
-    each = lamb_specs(masters, steps)
-    return pl.pallas_call(
+        weight_norm = total[number : number + 1, 0:1]
+        update_norm = total[8 + number : 9 + number, 0:1]
+        scale = RATE * (weight_norm / update_norm)
+        rows = news[number].shape[0]
+        place = slice(None)
+        if rows < masters[number].shape[0]:
+            place = pl.ds(pl.multiple_of(step * rows, rows), rows)
+        news[number][...] = masters[number][place] - scale * updates[number][place]
+    for source, target in zip(layer_outs, outs):
+        target[...] = source[...]
+
+    @pl.when(step == 0)
+    def _():
+        row = lax.broadcasted_iota(jnp.int32, (8, 128), 0)
+        lane = lax.broadcasted_iota(jnp.int32, (8, 128), 1)
+        for n in range(2):
+            half = jnp.where(row == lane, total[8 * n : 8 * n + 8], 0.0)
+            lamb_norms[n : n + 1] = jnp.sum(half, axis=0, keepdims=True)[:, 0:5]
+
+
+def step_masters(total, masters, updates, layer_outs, steps=4):
+    shape = jax.ShapeDtypeStruct
+    out_specs = [
+        pl.BlockSpec((o.shape[0] // steps, o.shape[1]), lambda i: (i, 0)) for o in layer_outs
+    ]
+    results = pl.pallas_call(
         step_kernel,
         grid=(steps,),
-        in_specs=[pl.BlockSpec((8, 128), lambda i: (0, 0))] + each * 2,
-        out_specs=each,
-        out_shape=[jax.ShapeDtypeStruct(m.shape, jnp.float32) for m in masters],
+        in_specs=[pl.BlockSpec((16, 128), lambda i: (0, 0))] + [VMEM_SPEC] * 10 + out_specs,
+        out_specs=lamb_specs(masters, steps)
+        + out_specs
+        + [pl.BlockSpec((2, 5), lambda i: (0, 0))],
+        out_shape=[shape(m.shape, jnp.float32) for m in masters]
+        + [shape(o.shape, o.dtype) for o in layer_outs]
+        + [shape((2, 5), jnp.float32)],
         compiler_params=pltpu.CompilerParams(vmem_limit_bytes=40 << 20),
         name="step_masters",
-    )(scales, *masters, *updates)
-
-
-def lamb_split(masters, firsts, seconds, grads):
+    )(total, *masters, *updates, *layer_outs)
+    return results[0:5], results[5:7], results[7]
+
+
+def lamb_split(masters, firsts, seconds, grads, layer_outs):
     def tall(arrays):
         return tuple(arrays[:4]) + (arrays[4].reshape(-1, 128),)
 
@@ -1529,11 +1561,15 @@
         return tuple(arrays[:4]) + (arrays[4].reshape(-1),)
 
     masters, firsts, seconds = tall(masters), tall(firsts), tall(seconds)
-    first_news, second_news, updates, squares = moments(grads, masters, firsts, seconds)
-    total, scales = norms(squares)
-    news = step_masters(scales, masters, updates)
-    lamb_norms = jnp.stack([total[0:5, 0], total[8:13, 0]])
-    return flat_small(news) + flat_small(first_news) + flat_small(second_news) + (lamb_norms,)
+    first_news, second_news, updates, kept, squares = moments(grads, masters, firsts, seconds)
+    news, outs, lamb_norms = step_masters(norms(squares), kept, updates, layer_outs)
+    return (
+        tuple(out[None] for out in outs)
+        + flat_small(news)
+        + flat_small(first_news)
+        + flat_small(second_news)
+        + (lamb_norms,)
+    )
 
 
 def lamb(masters, firsts, seconds, reduced):

time: 207 us -> 179 us (0.86)
  local copies, waits for them, and re-layouts: 26.1 us -> 0.7 us
    unnamed x58 -> x6, local copies, waits for them, and re-layouts: 25.3 us -> 0.7 us
where the time goes in v6:
time: 179 us
  Pallas kernels  177 us (99%)
    pallas_call x1, Pallas kernels, whole_layer(): pl.pallas_call(layer_kernel, out_shape=(shape(x_own.shape, bf16), shape(x...  152 us
    pallas_call x1, Pallas kernels, moments(): pl.pallas_call(moments_kernel, grid=(steps,), in_specs=grad_specs + each...  15.6 us
    pallas_call x1, Pallas kernels, norms(): pl.pallas_call(norms_kernel, out_shape=jax.ShapeDtypeStruct((16, 128), jn...  5.69 us
    pallas_call x1, Pallas kernels, step_masters(): pl.pallas_call(step_kernel, grid=(steps,), in_specs=[pl.BlockSpec((16, 12...  3.66 us

profile of v6, /device:TPU:0, one launch (start us, length us, event | category | flops | bytes accessed | tf_op | source)
XLA Modules:
  0.0 179.0 jit_solution(17957672984953848838)
XLA Ops:
  1.3 151.9 %layer.1 = (bf16[256,1024]{1,0:T(8,128)(2,1)}, bf16[256,1024]{1,0:T(8,128)(2,1)}, bf16[4,128,768]{2,1,0:T(8,128)(2,1)}, bf16[4,128,1024]{2,1,0:T(8,128)(2,1)}, b...) custom-call(s32[1]{0:T(128)S(6)} %copy.37.length_own, bf16[256,1024]{1,0:T(8,128)(2,1)} %bitcast.11, ...), custom_call_target="tpu_custom_call" | custom-call | tf_op jit(solution)/shard_map/layer/pallas_call | solution.py:1125
  153.2 0.0 copy-start
  153.2 0.0 copy-start.1
  153.2 15.6 %moments.1 = (f32[128,3072]{1,0:T(8,128)}, f32[128,1024]{1,0:T(8,128)}, f32[128,4096]{1,0:T(8,128)}, f32[512,1024]{1,0:T(8,128)}, f32[13,128]{1,0:T(8,128)}, /*i...) custom-call(bf16[4,128,768]{2,1,0:T(8,128)(2,1)} %get-tuple-element., ...), custom_call_target="tpu_custom_call" | custom-call | tf_op jit(solution)/shard_map/moments/pallas_call | solution.py:1460
  168.8 0.0 copy-start.2
  168.9 0.7 copy-done.2
  169.5 5.7 %norms.1.refs_0_ = f32[16,128]{1,0:T(8,128)S(1)} custom-call(f32[16,128]{1,0:T(8,128)S(1)} %copy-done.2), custom_call_target="tpu_custom_call" | custom-call | tf_op jit(solution)/shard_map/norms/pallas_call | solution.py:1497
  175.2 0.0 copy-done
  175.2 0.0 copy-done.1
  175.3 3.7 %step_masters.1 = (f32[128,3072]{1,0:T(8,128)}, f32[128,1024]{1,0:T(8,128)}, f32[128,4096]{1,0:T(8,128)}, f32[512,1024]{1,0:T(8,128)}, f32[13,128]{1,0:T(8,128)}...) custom-call(f32[16,128]{1,0:T(8,128)S(1)} %norms.1.refs_0_, ...), custom_call_target="tpu_custom_call" | custom-call | tf_op jit(solution)/shard_map/step_masters/pallas_call | solution.py:1540
Async XLA Ops:
  153.2 22.0 %copy-start = (bf16[256,1024]{1,0:T(8,128)(2,1)S(1)}, bf16[256,1024]{1,0:T(8,128)(2,1)}, u32[]{:S(2)}) copy-start(bf16[256,1024]{1,0:T(8,128)(2,1)} %get-tuple-element.70.refs_11_) | copy-start | bytes 1572868
  153.2 22.0 %copy-start.1 = (bf16[256,1024]{1,0:T(8,128)(2,1)S(1)}, bf16[256,1024]{1,0:T(8,128)(2,1)}, u32[]{:S(2)}) copy-start(bf16[256,1024]{1,0:T(8,128)(2,1)} %get-tuple-element.71.refs_12_) | copy-start | bytes 1572868
  168.8 0.7 copy-start.2

commit v7 on v6

--- a/solution.py
+++ b/solution.py
@@ -291,14 +291,17 @@
     up_master,
     down_master,
     small_master,
-    tables,
-    output,
-    input_grad,
+    tables_in,
+    output_out,
+    input_grad_out,
     qkv_all,
     up_all,
     down_all,
     out_grad,
     small_sum,
+    tables,
+    output,
+    input_grad,
     x_all,
     cot_all,
     len_all,
@@ -340,6 +343,8 @@
     load_sem,
     plane_send,
     plane_recv,
+    early_send,
+    early_recv,
     len_send,
     len_recv,
     w_send,
@@ -361,6 +366,7 @@
     keep_sem,
     total_send,
     total_recv,
+    store_sem,
 ):
     f32, bf16 = jnp.float32, jnp.bfloat16
     at = Place()
@@ -399,6 +405,7 @@
     loads.append((down_master.at[rows], stage[3]))
     loads.append((x_own, x_all.at[part]))
     loads.append((cot_own, cot_all.at[part]))
+    loads.append((tables_in, tables))
 
     def load(n):
         return pltpu.make_async_copy(loads[n][0], loads[n][1], load_sem.at[n])
@@ -411,10 +418,33 @@
     small_all[shard] = small_own[...]
     greet(at)
 
+    halves = (slice(0, HALF), slice(HALF, 2 * HALF))
     activations = ((x_own, x_all), (cot_own, cot_all))
-    for n, (own, whole) in enumerate(activations):
-        send(own, whole.at[part], plane_send.at[n, 0], plane_recv.at[n, 0], at.across_x).start()
-        send(own, whole.at[part], plane_send.at[n, 1], plane_recv.at[n, 1], at.across_y).start()
+    neighbours = ((at.across_x, at.x_part), (at.across_y, at.y_part))
+
+    def send_activations():
+        for r, (peer, _) in enumerate(neighbours):
+            send(
+                x_own, x_all.at[part], plane_send.at[0, r], plane_recv.at[0, r], peer
+            ).start()
+        for r, (peer, _) in enumerate(neighbours):
+            send(
+                cot_own.at[halves[0]],
+                cot_all.at[part, halves[0]],
+                early_send.at[r],
+                early_recv.at[r],
+                peer,
+            ).start()
+
+    def send_rest():
+        for r, (peer, _) in enumerate(neighbours):
+            send(
+                cot_own.at[halves[1]],
+                cot_all.at[part, halves[1]],
+                plane_send.at[1, r],
+                plane_recv.at[1, r],
+                peer,
+            ).start()
 
     def cast(n, first, last):
         for m in range(first, last):
@@ -423,6 +453,7 @@
         w_all[shard, :, low:high] = stage[(0, 2, 3)[n]][:, 0 : high - low].astype(bf16)
 
     def send_own(n):
+        cast(n, *((0, 3), (4, 12), (12, 13))[n])
         block = piece(w_all, shard, n)
 
         @pl.when(z < 3)
@@ -470,17 +501,25 @@
             arrived(piece(w_all, source, n), w_recv.at[n, source], at.other_core)
 
     def send_out_rows():
-        block = out_all.at[core]
-
-        @pl.when(z < 3)
-        def _():
-            send(block, block, out_send.at[0], out_recv.at[core], at.up).start()
-
-        @pl.when(z > 0)
-        def _():
-            send(block, block, out_send.at[1], out_recv.at[core], at.down).start()
-
-        send(block, block, out_send.at[2], out_recv.at[core], at.other_core).start()
+        load(3).wait()
+
+        @pl.when(z == part)
+        def _():
+            out_all[core] = stage[1][...].astype(bf16)
+            block = out_all.at[core]
+
+            @pl.when(z < 3)
+            def _():
+                send(block, block, out_send.at[0], out_recv.at[core], at.up).start()
+
+            @pl.when(z > 0)
+            def _():
+                send(block, block, out_send.at[1], out_recv.at[core], at.down).start()
+
+            send(block, block, out_send.at[2], out_recv.at[core], at.other_core).start()
+
+    def out_from_core():
+        arrived(out_all.at[1 - core], out_recv.at[1 - core], at.other_core)
 
     def forward_out(k):
         @pl.when((z - k == part) | (z + k == part))
@@ -498,69 +537,64 @@
 
             send(block, block, out_send.at[2], out_recv.at[core], at.other_core).start()
 
+    def forward_neighbour(n, r):
+        peer, source = neighbours[r]
+        whole = activations[n][1]
+        if n == 0:
+            arrived(whole.at[source], plane_recv.at[0, r], peer)
+        else:
+            arrived(whole.at[source, halves[0]], early_recv.at[r], peer)
+            arrived(whole.at[source, halves[1]], plane_recv.at[1, r], peer)
+        block = whole.at[source, halves[r]]
+        onward = neighbours[1 - r][0]
+        send(block, block, plane_send.at[n, 2 + r], plane_recv.at[n, 2 + r], onward).start()
+
     def forward_x(n):
-        whole = activations[n][1]
-        arrived(whole.at[at.x_part], plane_recv.at[n, 0], at.across_x)
-        block = whole.at[at.x_part, 0:HALF]
-        send(block, block, plane_send.at[n, 2], plane_recv.at[n, 2], at.across_y).start()
+        forward_neighbour(n, 0)
 
     def forward_y(n):
-        whole = activations[n][1]
-        arrived(whole.at[at.y_part], plane_recv.at[n, 1], at.across_y)
-        block = whole.at[at.y_part, HALF : 2 * HALF]
-        send(block, block, plane_send.at[n, 3], plane_recv.at[n, 3], at.across_x).start()
+        forward_neighbour(n, 1)
 
     def far_halves(n):
         whole = activations[n][1]
         arrived(whole.at[at.far_part, 0:HALF], plane_recv.at[n, 2], at.across_y)
         arrived(whole.at[at.far_part, HALF : 2 * HALF], plane_recv.at[n, 3], at.across_x)
 
-    cast(Q, 0, 3)
-    send_own(Q)
-    load(3).wait()
-
-    @pl.when(z == part)
-    def _():
-        out_all[core] = stage[1][...].astype(bf16)
-        send_out_rows()
-
-    for n, (peer, _) in enumerate(plane_peers):
-        send(len_all.at[part], len_all.at[part], len_send.at[n], len_recv.at[n], peer).start()
-    for k in range(1, 8):
-        send(
-            small_own,
-            small_all.at[shard],
-            small_send.at[k - 1],
-            small_recv.at[k - 1],
-            at.shard_after(k),
-        ).start()
-    cast(U, 4, 12)
-    cast(N, 12, 13)
-    load(13).wait()
-    load(14).wait()
-    forward(1, Q)
-    forward_out(1)
-    forward(2, Q)
-    send_own(U)
-    send_own(N)
-    for n, (peer, other) in enumerate(plane_peers):
-        arrived(len_all.at[other], len_recv.at[n], peer)
-    for k in range(1, 8):
-        arrived(small_all.at[(shard + 8 - k) % 8], small_recv.at[k - 1], at.shard_after(8 - k))
-    for number, row in enumerate((0, 8, 16, 24, 56, 96)):
-        for n in range(8):
-            source = row + n
-            vectors[number : number + 1, n * 128 : (n + 1) * 128] = small_all[
-                source // 13, source % 13 : source % 13 + 1
-            ]
-    for c in range(3):
-        for n in range(2):
-            source = 32 + 8 * c + 2 * part + n
-            columns = slice((2 * c + n) * 128, (2 * c + n + 1) * 128)
-            qkv_bias[:, columns] = small_all[source // 13, pl.ds(source % 13, 1)]
-    for g in range(8):
-        source = 64 + 4 * g + part
-        up_bias[:, g * 128 : (g + 1) * 128] = small_all[source // 13, pl.ds(source % 13, 1)]
+    def send_small():
+        for n, (peer, _) in enumerate(plane_peers):
+            send(len_all.at[part], len_all.at[part], len_send.at[n], len_recv.at[n], peer).start()
+        for k in range(1, 8):
+            send(
+                small_own,
+                small_all.at[shard],
+                small_send.at[k - 1],
+                small_recv.at[k - 1],
+                at.shard_after(k),
+            ).start()
+
+    def unpack_small():
+        for n in (13, 14, 15):
+            load(n).wait()
+        for n, (peer, other) in enumerate(plane_peers):
+            arrived(len_all.at[other], len_recv.at[n], peer)
+        for k in range(1, 8):
+            arrived(
+                small_all.at[(shard + 8 - k) % 8], small_recv.at[k - 1], at.shard_after(8 - k)
+            )
+        for number, row in enumerate((0, 8, 16, 24, 56, 96)):
+            for n in range(8):
+                source = row + n
+                vectors[number : number + 1, n * 128 : (n + 1) * 128] = small_all[
+                    source // 13, source % 13 : source % 13 + 1
+                ]
+        for c in range(3):
+            for n in range(2):
+                source = 32 + 8 * c + 2 * part + n
+                columns = slice((2 * c + n) * 128, (2 * c + n + 1) * 128)
+                qkv_bias[:, columns] = small_all[source // 13, pl.ds(source % 13, 1)]
+        for g in range(8):
+            source = 64 + 4 * g + part
+            up_bias[:, g * 128 : (g + 1) * 128] = small_all[source // 13, pl.ds(source % 13, 1)]
 
     sums[...] = jnp.zeros_like(sums)
     d_qkv_bias[...] = jnp.zeros_like(d_qkv_bias)
@@ -643,55 +677,6 @@
             d_projected[s, :, columns] = rounded
             d_qkv_bias[:, columns] += jnp.sum(rounded.astype(f32), axis=0, keepdims=True)
 
-    forward(3, Q)
-    from_core(Q)
-
-    @pl.loop(0, 4)
-    def _(i):
-        @pl.when(i == 1)
-        def _():
-            forward_x(0)
-
-        @pl.when(i == 2)
-        def _():
-            forward_y(0)
-
-        @pl.when(i == 3)
-        def _():
-            far_halves(0)
-
-        project(near_first(i))
-
-        @pl.when(i == 0)
-        def _():
-            forward_out(2)
-            forward(1, U)
-
-        @pl.when(i == 2)
-        def _():
-            forward(1, N)
-
-    forward_out(3)
-    arrived(out_all.at[1 - core], out_recv.at[1 - core], at.other_core)
-
-    @pl.loop(0, 4)
-    def _(i):
-        @pl.when(i == 3)
-        def _():
-            far_halves(1)
-
-        attend(near_first(i))
-
-        @pl.when(i == 0)
-        def _():
-            forward_x(1)
-            forward_y(1)
-            forward(2, U)
-
-        @pl.when(i == 1)
-        def _():
-            forward(2, N)
-
     def gradient(left, right, n):
         low, high = SPANS[n]
 
@@ -827,25 +812,25 @@
                 arrived(out_line_in.at[1], rows_recv.at[2], at.up)
                 out_add(out_line_in[1])
 
-            for n, (peer, _) in enumerate(plane_peers):
-                send(out_line, out_grad, rows_send.at[2 + n], rows_recv.at[3], peer).start()
+            for r, (peer, _) in enumerate(neighbours):
+                send(out_line, out_grad, rows_send.at[2 + r], rows_recv.at[3], peer).start()
             pltpu.make_async_copy(out_line, out_grad, keep_sem.at[3]).start()
 
-    gradient(normed_one, d_projected, Q)
-    to_core(Q)
-    for n in range(2):
-        out_term[n] = tn(flat(mixed[:, :, n * 128 : (n + 1) * 128]), flat(back[...])).astype(bf16)
-    out_to_core()
-    add_core(Q)
-    line_starts(Q)
-    out_add_core()
-    out_step(0)
-    forward(3, U)
-    forward(3, N)
-    from_core(U)
-    from_core(N)
-
-    halves = (slice(0, HALF), slice(HALF, 2 * HALF))
+    def out_share():
+        for r, (peer, source) in enumerate(neighbours):
+
+            @pl.when(z == source)
+            def _():
+                arrived(out_grad, rows_recv.at[3], peer)
+                block = out_grad.at[64 * r : 64 * r + 64]
+                onward = neighbours[1 - r][0]
+                send(block, block, rows_send.at[4], rows_recv.at[4 + r], onward).start()
+
+    def out_gradient():
+        for n in range(2):
+            columns = slice(n * 128, (n + 1) * 128)
+            out_term[n] = tn(flat(mixed[:, :, columns]), flat(back[...])).astype(bf16)
+
     part_refs = (out_part, dx_part)
     routes = (
         (halves[0], at.across_x, at.x_part, at.across_y, at.y_part),
@@ -862,20 +847,6 @@
             part_recv.at[n, r, m],
             peer,
         ).start()
-
-    def send_parts(n, i):
-        @pl.when(i == 0)
-        def _():
-            send_part(n, 0, 0)
-            send_part(n, 1, 0)
-
-        @pl.when(i == 1)
-        def _():
-            send_part(n, 0, 1)
-
-        @pl.when(i == 2)
-        def _():
-            send_part(n, 1, 1)
 
     def turn_part(n, r):
         half, peer, _, turn, turned = routes[r]
@@ -904,22 +875,25 @@
     up_low, up_high = SPANS[U]
     down_low, down_high = SPANS[N]
 
-    def feed(s):
+    def feed_in(s):
         value = nn(normed_two[s], flat(w_all[:, :, up_low:up_high])) + up_bias[...]
         hidden[s] = value
-        low = (value * (0.5 * (1.0 + lax.erf(value * 2.0**-0.5)))).astype(bf16)
-        activated[s] = low
+        activated[s] = (value * (0.5 * (1.0 + lax.erf(value * 2.0**-0.5)))).astype(bf16)
+
+    def feed_out(s):
         out_part[s] = (
-            nn(low, flat(w_all[:, :, down_low:down_high])) + nn(mixed[s], flat(out_all[...]))
+            nn(activated[s], flat(w_all[:, :, down_low:down_high]))
+            + nn(mixed[s], flat(out_all[...]))
         ).astype(bf16)
 
     def feed_back(s):
-        value = hidden[s]
-        slope = gelu_slope(value)
+        slope = gelu_slope(hidden[s])
         low = (nt(back[s], flat(w_all[:, :, down_low:down_high])) * slope).astype(bf16)
         d_hidden[s] = low
         d_up_bias[...] += jnp.sum(low.astype(f32), axis=0, keepdims=True)
-        d_two = nt(low, flat(w_all[:, :, up_low:up_high]))
+
+    def norm_back(s):
+        d_two = nt(d_hidden[s], flat(w_all[:, :, up_low:up_high]))
         d_one = nt(d_projected[s], flat(w_all[:, :, SPANS[Q][0] : SPANS[Q][1]]))
         unit = (x_all[s].astype(f32) - stats[s][:, 0:1]) * stats[s][:, 1:2]
         sums[0:1] += jnp.sum(d_one * unit, axis=0, keepdims=True)
@@ -928,100 +902,57 @@
         sums[3:4] += jnp.sum(d_two, axis=0, keepdims=True)
         dx_part[s] = (d_one * vectors[0:1] + d_two * vectors[2:3]).astype(bf16)
 
-    @pl.loop(0, 4)
-    def _(i):
-        feed(far_first(i))
-        send_parts(0, i)
-
-        @pl.when(i == 1)
-        def _():
-            line_step(Q, 0)
-            out_step(1)
-
-        @pl.when(i == 3)
-        def _():
-            line_step(Q, 1)
-
-    gradient(activated, back, N)
-    to_core(N)
-    turn_part(0, 1)
-    turn_part(0, 0)
-    line_step(Q, 2)
-    out_step(2)
-    add_core(N)
-    line_starts(N)
-
-    @pl.loop(0, 4)
-    def _(i):
-        feed_back(far_first(i))
-        send_parts(1, i)
-
-        @pl.when(i == 1)
-        def _():
-            line_step(N, 0)
-            line_ends(Q)
-            out_ends()
-
-        @pl.when(i == 2)
-        def _():
-            line_step(N, 1)
-
-    gradient(normed_two, d_hidden, U)
-    to_core(U)
-    share(Q)
-    line_step(N, 2)
-    turn_part(1, 1)
-    turn_part(1, 0)
-    add_core(U)
-    line_starts(U)
-
-    small_part[...] = jnp.zeros_like(small_part)
-
     def place(row, value):
         small_part[row // 13, pl.ds(row % 13, 1)] = value
 
-    back_total = jnp.sum(back[part].astype(f32), axis=0, keepdims=True)
-    for n in range(8):
-        columns = slice(n * 128, (n + 1) * 128)
-        for number in range(4):
-            place(8 * number + n, sums[number : number + 1, columns])
-        place(56 + n, back_total[:, columns])
-        place(96 + n, back_total[:, columns])
-        place(64 + 4 * n + part, d_up_bias[:, columns])
-    for c in range(3):
-        for n in range(2):
-            columns = slice((2 * c + n) * 128, (2 * c + n + 1) * 128)
-            place(32 + 8 * c + 2 * part + n, d_qkv_bias[:, columns])
-    for k in range(1, 8):
-        send(
-            small_part.at[(shard + k) % 8],
-            small_in.at[k - 1],
-            total_send.at[k - 1],
-            total_recv.at[k - 1],
-            at.shard_after(k),
-        ).start()
-
-    line_step(U, 0)
-
-    for r in range(2):
+    def small_start():
+        small_part[...] = jnp.zeros_like(small_part)
+        back_total = jnp.sum(back[part].astype(f32), axis=0, keepdims=True)
+        for n in range(8):
+            columns = slice(n * 128, (n + 1) * 128)
+            for number in range(4):
+                place(8 * number + n, sums[number : number + 1, columns])
+            place(56 + n, back_total[:, columns])
+            place(96 + n, back_total[:, columns])
+            place(64 + 4 * n + part, d_up_bias[:, columns])
+        for c in range(3):
+            for n in range(2):
+                columns = slice((2 * c + n) * 128, (2 * c + n + 1) * 128)
+                place(32 + 8 * c + 2 * part + n, d_qkv_bias[:, columns])
+        for k in range(1, 8):
+            send(
+                small_part.at[(shard + k) % 8],
+                small_in.at[k - 1],
+                total_send.at[k - 1],
+                total_recv.at[k - 1],
+                at.shard_after(k),
+            ).start()
+
+    def small_turn():
+        total = small_part[shard]
+        for k in range(1, 8):
+            arrived(small_in.at[k - 1], total_recv.at[k - 1], at.shard_after(8 - k))
+            total = total + small_in[k - 1]
+        small_total[...] = total
+        for n, (peer, _) in enumerate(plane_peers):
+            send(
+                small_total, small_plane.at[part], total_send.at[7 + n], total_recv.at[7 + n], peer
+            ).start()
+        small_plane[part] = total
+
+    def small_end():
+        for n, (peer, other) in enumerate(plane_peers):
+            arrived(small_plane.at[other], total_recv.at[7 + n], peer)
+        small_sum[...] = (small_plane[0] + small_plane[1]) + (small_plane[2] + small_plane[3])
+
+    def write_output(r):
         half = halves[r]
-        live = live_rows(part)[half]
         values = x_all[part, half].astype(f32)
         summed = values + whole_part(0, r) + vectors[4:5] + vectors[5:6]
-        output[half] = jnp.where(live, summed, 0.0).astype(bf16)
-    line_ends(N)
-    line_step(U, 1)
-    total = small_part[shard]
-    for k in range(1, 8):
-        arrived(small_in.at[k - 1], total_recv.at[k - 1], at.shard_after(8 - k))
-        total = total + small_in[k - 1]
-    small_total[...] = total
-    for n, (peer, _) in enumerate(plane_peers):
-        send(
-            small_total, small_plane.at[part], total_send.at[7 + n], total_recv.at[7 + n], peer
-        ).start()
-    small_plane[part] = total
-    for r in range(2):
+        output[half] = jnp.where(live_rows(part)[half], summed, 0.0).astype(bf16)
+        pltpu.make_async_copy(output.at[half], output_out.at[half], store_sem.at[0, r]).start()
+
+    def write_input_grad(r):
         half = halves[r]
         scaled = whole_part(1, r)
         inverse = stats[part, half, 1:2]
@@ -1032,31 +963,346 @@
             - unit * jnp.mean(scaled * unit, axis=-1, keepdims=True)
         )
         input_grad[half] = result.astype(bf16)
-    line_step(U, 2)
-    share(N)
-    for n, (peer, other) in enumerate(plane_peers):
-        arrived(small_plane.at[other], total_recv.at[7 + n], peer)
-    small_sum[...] = (small_plane[0] + small_plane[1]) + (small_plane[2] + small_plane[3])
-    line_ends(U)
-    share(U)
+        pltpu.make_async_copy(
+            input_grad.at[half], input_grad_out.at[half], store_sem.at[1, r]
+        ).start()
+
+    at_end = (z == 0) | (z == 3)
+    middle = (z == 1) | (z == 2)
+    send_activations()
+    send_own(Q)
+    send_out_rows()
+    send_small()
+
+    @pl.when(at_end)
+    def _():
+        send_rest()
+
+    @pl.when(middle)
+    def _():
+        forward(1, Q)
+        forward_out(1)
+        forward(2, Q)
+
+    send_own(U)
+    forward_x(0)
+
+    @pl.when(at_end)
+    def _():
+        forward_out(1)
+
+    @pl.when(middle)
+    def _():
+        forward_out(2)
+        from_core(Q)
+        send_own(N)
+        send_rest()
+
+    forward_y(0)
+
+    @pl.when(at_end)
+    def _():
+        forward(1, Q)
+        forward(2, Q)
+        forward(3, Q)
+        send_own(N)
+        from_core(Q)
+
+    unpack_small()
+
+    @pl.loop(0, 4)
+    def _(i):
+        project(near_first(i))
+
+        @pl.when((i == 0) & at_end)
+        def _():
+            forward_y(1)
+            forward_out(2)
+
+        @pl.when(i == 2)
+        def _():
+            forward_x(1)
+
+        @pl.when((i == 2) & at_end)
+        def _():
+            forward_out(3)
+
+        @pl.when((i == 2) & middle)
+        def _():
+            forward(1, U)
+            forward_y(1)
+
+        @pl.when(i == 2)
+        def _():
+            far_halves(0)
+
+        @pl.when((i == 2) & middle)
+        def _():
+            forward(1, N)
+
+    out_from_core()
+
+    @pl.loop(0, 4)
+    def _(i):
+        attend(near_first(i))
+
+        @pl.when((i == 0) & middle)
+        def _():
+            forward(2, U)
+
+        @pl.when((i == 1) & middle)
+        def _():
+            far_halves(1)
+
+        @pl.when((i == 2) & at_end)
+        def _():
+            forward(1, U)
+            far_halves(1)
+
+        @pl.when((i == 2) & middle)
+        def _():
+            forward(2, N)
+
+    gradient(normed_one, d_projected, Q)
+
+    @pl.when(at_end)
+    def _():
+        to_core(Q)
+
+    @pl.when(middle)
+    def _():
+        from_core(U)
+        from_core(N)
+
+    out_gradient()
+
+    @pl.when(at_end)
+    def _():
+        forward(2, U)
+        forward(3, U)
+        forward(1, N)
+        add_core(Q)
+        line_starts(Q)
+        from_core(U)
+
+    @pl.loop(0, 4)
+    def _(i):
+        feed_in(i)
+
+        @pl.when((i == 0) & at_end)
+        def _():
+            forward(2, N)
+
+        @pl.when((i == 0) & middle)
+        def _():
+            to_core(Q)
+
+    @pl.when(at_end)
+    def _():
+        forward(3, N)
+
+    gradient(activated, back, N)
+
+    @pl.when(at_end)
+    def _():
+        out_to_core()
+        from_core(N)
+
+    @pl.loop(0, 4)
+    def _(i):
+        feed_out(far_first(i))
+
+        @pl.when((i == 0) & middle)
+        def _():
+            add_core(Q)
+
+        @pl.when(i == 0)
+        def _():
+            send_part(0, 0, 0)
+            send_part(0, 1, 0)
+
+        @pl.when((i == 1) & at_end)
+        def _():
+            out_add_core()
+            out_step(0)
+            to_core(N)
+
+        @pl.when((i == 2) & middle)
+        def _():
+            send_part(0, 1, 1)
+
+    @pl.loop(0, 4)
+    def _(i):
+        feed_back(far_first(i))
+
+        @pl.when((i == 0) & middle)
+        def _():
+            out_to_core()
+            out_add_core()
+            line_step(Q, 0)
+            line_step(Q, 1)
+            send_part(0, 0, 1)
+            to_core(N)
+
+        @pl.when((i == 1) & at_end)
+        def _():
+            send_part(0, 1, 1)
+            add_core(N)
+            line_starts(N)
+            turn_part(0, 0)
+
+        @pl.when((i == 2) & at_end)
+        def _():
+            send_part(1, 0, 1)
+
+        @pl.when((i == 2) & middle)
+        def _():
+            out_step(1)
+
+        @pl.when((i == 3) & at_end)
+        def _():
+            send_part(0, 0, 1)
+
+        @pl.when((i == 3) & middle)
+        def _():
+            line_step(Q, 2)
+            send_part(1, 1, 1)
+
+        norm_back(far_first(i))
+
+        @pl.when((i == 0) & at_end)
+        def _():
+            send_part(1, 0, 0)
+            send_part(1, 1, 0)
+
+        @pl.when((i == 0) & middle)
+        def _():
+            add_core(N)
+
+        @pl.when((i == 1) & middle)
+        def _():
+            send_part(1, 0, 0)
+            send_part(1, 1, 0)
+            turn_part(0, 1)
+
+    @pl.when(middle)
+    def _():
+        turn_part(0, 0)
+        line_ends(Q)
+
+    gradient(normed_two, d_hidden, U)
+
+    @pl.when(middle)
+    def _():
+        to_core(U)
+        send_part(1, 0, 1)
+        line_step(N, 0)
+
+    turn_part(1, 1)
+
+    @pl.when(at_end)
+    def _():
+        to_core(U)
+        send_part(1, 1, 1)
+
+    @pl.when(middle)
+    def _():
+        turn_part(1, 0)
+
+    add_core(U)
+
+    @pl.when(at_end)
+    def _():
+        line_starts(U)
+        line_ends(Q)
+        turn_part(1, 0)
+
+    @pl.when(middle)
+    def _():
+        line_step(N, 1)
+        out_step(2)
+
+    small_start()
+
+    @pl.when(middle)
+    def _():
+        write_output(1)
+        line_step(N, 2)
+        line_step(U, 0)
+        write_output(0)
+        line_ends(N)
+        share(Q)
+
+    out_ends()
+
+    @pl.when(at_end)
+    def _():
+        turn_part(0, 1)
+        write_output(0)
+        share(Q)
+        line_ends(N)
+
+    @pl.when(middle)
+    def _():
+        line_step(U, 1)
+        line_step(U, 2)
+        share(N)
+        write_input_grad(0)
+        line_ends(U)
+        out_share()
+
+    small_turn()
+
+    @pl.when(at_end)
+    def _():
+        out_share()
+        line_ends(U)
+
+    @pl.when(middle)
+    def _():
+        share(U)
+
+    write_input_grad(1)
+    small_end()
+
+    @pl.when(at_end)
+    def _():
+        write_output(1)
+        share(N)
+        share(U)
+        write_input_grad(0)
+
+    for r, half in enumerate(halves):
+        pltpu.make_async_copy(output.at[half], output_out.at[half], store_sem.at[0, r]).wait()
+        pltpu.make_async_copy(
+            input_grad.at[half], input_grad_out.at[half], store_sem.at[1, r]
+        ).wait()
+    @pl.when(z == at.far_part)
+    def _():
+        for r, (peer, _) in enumerate(neighbours):
+            arrived(out_grad.at[64 * r : 64 * r + 64], rows_recv.at[4 + r], neighbours[1 - r][0])
 
     @pl.when(z != part)
     def _():
-        arrived(out_grad, rows_recv.at[3], at.across_x)
         sent(out_line, rows_send.at[1], at.up)
 
+    @pl.when((z == at.x_part) | (z == at.y_part))
+    def _():
+        sent(out_line.at[0:64], rows_send.at[4], at.across_x)
+
     @pl.when(z == part)
     def _():
-        for n, (peer, _) in enumerate(plane_peers):
-            sent(out_line, rows_send.at[2 + n], peer)
+        for r, (peer, _) in enumerate(neighbours):
+            sent(out_line, rows_send.at[2 + r], peer)
         pltpu.make_async_copy(out_line, out_grad, keep_sem.at[3]).wait()
 
     sent(out_line, rows_send.at[0], at.other_core)
-    for n, (own, whole) in enumerate(activations):
-        sent(own, plane_send.at[n, 0], at.across_x)
-        sent(own, plane_send.at[n, 1], at.across_y)
-        sent(whole.at[part, 0:HALF], plane_send.at[n, 2], at.across_y)
-        sent(whole.at[part, 0:HALF], plane_send.at[n, 3], at.across_x)
+    for r, (peer, _) in enumerate(neighbours):
+        sent(x_own, plane_send.at[0, r], peer)
+        sent(cot_own.at[halves[0]], early_send.at[r], peer)
+        sent(cot_own.at[halves[1]], plane_send.at[1, r], peer)
+        for n in range(2):
+            sent(x_all.at[part, halves[0]], plane_send.at[n, 2 + r], peer)
     for n, (peer, _) in enumerate(plane_peers):
         sent(len_all.at[part], len_send.at[n], peer)
         sent(small_total, total_send.at[7 + n], peer)
@@ -1135,9 +1381,12 @@
         ),
         in_specs=[pl.BlockSpec(memory_space=pltpu.SMEM)]
         + [HBM_SPEC] * 6
-        + [VMEM_SPEC, VMEM_SPEC],
-        out_specs=(VMEM_SPEC, VMEM_SPEC) + (HBM_SPEC,) * 4 + (VMEM_SPEC,),
+        + [VMEM_SPEC, HBM_SPEC],
+        out_specs=(HBM_SPEC,) * 6 + (VMEM_SPEC,),
         scratch_shapes=[
+            vmem(tables.shape, f32),
+            vmem(x_own.shape, bf16),
+            vmem(x_own.shape, bf16),
             by_sequence(D),
             by_sequence(D),
             vmem((group, 8, 128), f32),
@@ -1176,9 +1425,11 @@
             vmem((7, 16, 128), f32),
             vmem((16, 128), f32),
             vmem((4, 16, 128), f32),
-            dma((15,)),
+            dma((16,)),
             dma((2, 4)),
             dma((2, 4)),
+            dma((2,)),
+            dma((2,)),
             dma((3,)),
             dma((3,)),
             dma((3, 3, 4)),
@@ -1194,12 +1445,13 @@
             dma((3, 4)),
             dma((3, 5)),
             dma((5,)),
-            dma((4,)),
+            dma((6,)),
             dma((3, 4)),
             dma((3, 4)),
             dma((4,)),
             dma((10,)),
             dma((10,)),
+            dma((2, 2)),
         ],
         compiler_params=pltpu.CompilerParams(
             collective_id=0, has_side_effects=True, vmem_limit_bytes=62 << 20

time: 179 us -> 160 us (0.89)
  Pallas kernels: 177 us -> 157 us
    pallas_call x1, Pallas kernels: 152 us -> 132 us  [whole_layer(): pl.pallas_call(layer_kernel, out_shape=(shape(x_own.shape, bf16), shape(x...]
where the time goes in v7:
time: 160 us; the launch traced here: 159 us
  Pallas kernels  157 us (98%)
    pallas_call x1, Pallas kernels, whole_layer(): pl.pallas_call(layer_kernel, out_shape=(shape(x_own.shape, bf16), shape(x...  132 us
    pallas_call x1, Pallas kernels, moments(): pl.pallas_call(moments_kernel, grid=(steps,), in_specs=grad_specs + each...  15.6 us
    pallas_call x1, Pallas kernels, norms(): pl.pallas_call(norms_kernel, out_shape=jax.ShapeDtypeStruct((16, 128), jn...  6.25 us
    pallas_call x1, Pallas kernels, step_masters(): pl.pallas_call(step_kernel, grid=(steps,), in_specs=[pl.BlockSpec((16, 12...  3.66 us

profile of v7, /device:TPU:0, one launch (start us, length us, event | category | flops | bytes accessed | tf_op | source)
XLA Modules:
  0.0 159.4 jit_solution(6012867649478281057)
XLA Ops:
  1.3 131.7 %layer.1 = (bf16[256,1024]{1,0:T(8,128)(2,1)}, bf16[256,1024]{1,0:T(8,128)(2,1)}, bf16[4,128,768]{2,1,0:T(8,128)(2,1)}, bf16[4,128,1024]{2,1,0:T(8,128)(2,1)}, b...) custom-call(s32[1]{0:T(128)S(6)} %copy.37.length_own, bf16[256,1024]{1,0:T(8,128)(2,1)} %bitcast.11, ...), custom_call_target="tpu_custom_call" | custom-call | tf_op jit(solution)/shard_map/layer/pallas_call | solution.py:1371
  133.0 0.0 copy-start
  133.0 0.0 copy-start.1
  133.0 15.6 %moments.1 = (f32[128,3072]{1,0:T(8,128)}, f32[128,1024]{1,0:T(8,128)}, f32[128,4096]{1,0:T(8,128)}, f32[512,1024]{1,0:T(8,128)}, f32[13,128]{1,0:T(8,128)}, /*i...) custom-call(bf16[4,128,768]{2,1,0:T(8,128)(2,1)} %get-tuple-element., ...), custom_call_target="tpu_custom_call" | custom-call | tf_op jit(solution)/shard_map/moments/pallas_call | solution.py:1712
  148.6 0.0 copy-start.2
  148.6 0.7 copy-done.2
  149.3 6.3 %norms.1.refs_0_ = f32[16,128]{1,0:T(8,128)S(1)} custom-call(f32[16,128]{1,0:T(8,128)S(1)} %copy-done.2), custom_call_target="tpu_custom_call" | custom-call | tf_op jit(solution)/shard_map/norms/pallas_call | solution.py:1749
  155.6 0.0 copy-done
  155.6 0.0 copy-done.1
  155.6 3.7 %step_masters.1 = (f32[128,3072]{1,0:T(8,128)}, f32[128,1024]{1,0:T(8,128)}, f32[128,4096]{1,0:T(8,128)}, f32[512,1024]{1,0:T(8,128)}, f32[13,128]{1,0:T(8,128)}...) custom-call(f32[16,128]{1,0:T(8,128)S(1)} %norms.1.refs_0_, ...), custom_call_target="tpu_custom_call" | custom-call | tf_op jit(solution)/shard_map/step_masters/pallas_call | solution.py:1792
Async XLA Ops:
  133.0 22.6 %copy-start = (bf16[256,1024]{1,0:T(8,128)(2,1)S(1)}, bf16[256,1024]{1,0:T(8,128)(2,1)}, u32[]{:S(2)}) copy-start(bf16[256,1024]{1,0:T(8,128)(2,1)} %get-tuple-element.70.refs_11_) | copy-start | bytes 1572868
  133.0 22.6 %copy-start.1 = (bf16[256,1024]{1,0:T(8,128)(2,1)S(1)}, bf16[256,1024]{1,0:T(8,128)(2,1)}, u32[]{:S(2)}) copy-start(bf16[256,1024]{1,0:T(8,128)(2,1)} %get-tuple-element.71.refs_12_) | copy-start | bytes 1572868
  148.6 0.7 copy-start.2

commit v8 on v7

--- a/solution.py
+++ b/solution.py
@@ -1454,7 +1454,7 @@
             dma((2, 2)),
         ],
         compiler_params=pltpu.CompilerParams(
-            collective_id=0, has_side_effects=True, vmem_limit_bytes=62 << 20
+            collective_id=0, has_side_effects=True, vmem_limit_bytes=56 << 20
         ),
         name="layer",
     )(lengths, x_own, cot_own, *masters, tables)
@@ -1614,8 +1614,7 @@
 def moments_kernel(*refs):
     qkv_grad, out_grad, up_grad, down_grad, small_grad = refs[0:5]
     masters, firsts, seconds = refs[5:10], refs[10:15], refs[15:20]
-    first_news, second_news, updates, kept = refs[20:25], refs[25:30], refs[30:35], refs[35:40]
-    squares = refs[40]
+    first_news, second_news, updates, squares = refs[20:25], refs[25:30], refs[30:35], refs[35]
     step = pl.program_id(0)
 
     @pl.when(step == 0)
@@ -1624,16 +1623,15 @@
 
     def one(number, span, grad):
         index = (slice(None), span)
-        master = masters[number][index]
+        rows = firsts[number].shape[0]
+        place = (pl.ds(pl.multiple_of(step * rows, rows), rows), span)
+        master = masters[number][place]
         first_new, second_new, update = lamb_rows(
             firsts[number][index], seconds[number][index], master, grad
         )
         first_news[number][index] = first_new
         second_news[number][index] = second_new
-        rows = masters[number].shape[0]
-        place = (pl.ds(pl.multiple_of(step * rows, rows), rows), span)
         updates[number][place] = update
-        kept[number][place] = master
         return lane_sums(master), lane_sums(update)
 
     def add(number, pairs):
@@ -1682,7 +1680,6 @@
         first_news[4][...] = first_new
         second_news[4][...] = second_new
         updates[4][...] = update
-        kept[4][...] = masters[4][...]
         squares[4:5] += lane_sums(masters[4][...])
         squares[12:13] += lane_sums(update)
 
@@ -1712,13 +1709,13 @@
     results = pl.pallas_call(
         moments_kernel,
         grid=(steps,),
-        in_specs=grad_specs + each * 3,
-        out_specs=each * 2 + [VMEM_SPEC] * 10 + [pl.BlockSpec((16, 128), lambda i: (0, 0))],
-        out_shape=out * 2 + near * 2 + [shape((16, 128), jnp.float32)],
-        compiler_params=pltpu.CompilerParams(vmem_limit_bytes=44 << 20),
+        in_specs=grad_specs + [VMEM_SPEC] * 5 + each * 2,
+        out_specs=each * 2 + [VMEM_SPEC] * 5 + [pl.BlockSpec((16, 128), lambda i: (0, 0))],
+        out_shape=out * 2 + near + [shape((16, 128), jnp.float32)],
+        compiler_params=pltpu.CompilerParams(vmem_limit_bytes=12 << 20),
         name="moments",
     )(*grads, *masters, *firsts, *seconds)
-    return results[0:5], results[5:10], results[10:15], results[15:20], results[20]
+    return results[0:5], results[5:10], results[10:15], results[15]
 
 
 def norms_kernel(squares, total, everyone, send_sem, recv_sem):
@@ -1799,7 +1796,7 @@
         out_shape=[shape(m.shape, jnp.float32) for m in masters]
         + [shape(o.shape, o.dtype) for o in layer_outs]
         + [shape((2, 5), jnp.float32)],
-        compiler_params=pltpu.CompilerParams(vmem_limit_bytes=40 << 20),
+        compiler_params=pltpu.CompilerParams(vmem_limit_bytes=12 << 20),
         name="step_masters",
     )(total, *masters, *updates, *layer_outs)
     return results[0:5], results[5:7], results[7]
@@ -1812,9 +1809,15 @@
     def flat_small(arrays):
         return tuple(arrays[:4]) + (arrays[4].reshape(-1),)
 
-    masters, firsts, seconds = tall(masters), tall(firsts), tall(seconds)
-    first_news, second_news, updates, kept, squares = moments(grads, masters, firsts, seconds)
-    news, outs, lamb_norms = step_masters(norms(squares), kept, updates, layer_outs)
+    def placed(arrays, space):
+        return tuple(pltpu.with_memory_space_constraint(a, space) for a in arrays)
+
+    masters = placed(tall(masters), pltpu.VMEM)
+    firsts, seconds = placed(tall(firsts), pltpu.HBM), placed(tall(seconds), pltpu.HBM)
+    grads = placed(grads[:4], pltpu.HBM) + (grads[4],)
+    layer_outs = placed(layer_outs, pltpu.HBM)
+    first_news, second_news, updates, squares = moments(grads, masters, firsts, seconds)
+    news, outs, lamb_norms = step_masters(norms(squares), masters, updates, layer_outs)
     return (
         tuple(out[None] for out in outs)
         + flat_small(news)

time: 160 us -> 160 us (level)
  no operation moved by 1% of the time
where the time goes in v8:
time: 160 us
  Pallas kernels  158 us (99%)
    pallas_call x1, Pallas kernels, whole_layer(): pl.pallas_call(layer_kernel, out_shape=(shape(x_own.shape, bf16), shape(x...  132 us
    pallas_call x1, Pallas kernels, moments(): pl.pallas_call(moments_kernel, grid=(steps,), in_specs=grad_specs + [VMEM...  14.5 us
    pallas_call x1, Pallas kernels, norms(): pl.pallas_call(norms_kernel, out_shape=jax.ShapeDtypeStruct((16, 128), jn...  6.33 us
    pallas_call x1, Pallas kernels, step_masters(): pl.pallas_call(step_kernel, grid=(steps,), in_specs=[pl.BlockSpec((16, 12...  5.15 us

profile of v8, /device:TPU:0, one launch (start us, length us, event | category | flops | bytes accessed | tf_op | source)
XLA Modules:
  0.0 160.0 jit_solution(245678374833660893)
XLA Ops:
  1.3 0.0 copy-start
  1.3 0.0 copy-start.1
  1.3 0.0 copy-start.2
  1.3 0.0 copy-start.3
  1.3 0.0 copy-start.4
  1.4 131.8 %layer.1 = (bf16[256,1024]{1,0:T(8,128)(2,1)}, bf16[256,1024]{1,0:T(8,128)(2,1)}, bf16[4,128,768]{2,1,0:T(8,128)(2,1)}, bf16[4,128,1024]{2,1,0:T(8,128)(2,1)}, b...) custom-call(s32[1]{0:T(128)S(6)} %copy.37.length_own, bf16[256,1024]{1,0:T(8,128)(2,1)} %bitcast.15, ...), custom_call_target="tpu_custom_call" | custom-call | tf_op jit(solution)/shard_map/layer/pallas_call | solution.py:1371
  133.2 0.0 copy-done
  133.2 0.0 copy-done.1
  133.2 0.0 copy-done.2
  133.2 0.0 copy-done.3
  133.2 0.0 copy-done.4
  133.2 0.0 copy-start.5
  133.2 0.7 copy-done.5
  133.9 14.5 %moments.1 = (f32[128,3072]{1,0:T(8,128)}, f32[128,1024]{1,0:T(8,128)}, f32[128,4096]{1,0:T(8,128)}, f32[512,1024]{1,0:T(8,128)}, f32[13,128]{1,0:T(8,128)}, /*i...) custom-call(bf16[4,128,768]{2,1,0:T(8,128)(2,1)} %get-tuple-element., ...), custom_call_target="tpu_custom_call" | custom-call | tf_op jit(solution)/shard_map/moments/pallas_call | solution.py:1709
  148.4 6.3 %norms.1.refs_0_ = f32[16,128]{1,0:T(8,128)S(1)} custom-call(f32[16,128]{1,0:T(8,128)S(1)} %get-tuple-element.54.squares), custom_call_target="tpu_custom_call" | custom-call | tf_op jit(solution)/shard_map/norms/pallas_call | solution.py:1746
  154.7 5.2 %step_masters.1 = (f32[128,3072]{1,0:T(8,128)}, f32[128,1024]{1,0:T(8,128)}, f32[128,4096]{1,0:T(8,128)}, f32[512,1024]{1,0:T(8,128)}, f32[13,128]{1,0:T(8,128)}...) custom-call(f32[16,128]{1,0:T(8,128)S(1)} %norms.1.refs_0_, f32[128,3072]{1,0:T(8,128)S(1)} %copy-done.2, ...), custom_call_target="tpu_custom_call" | custom-call | tf_op jit(solution)/shard_map/step_masters/pallas_call | solution.py:1789
Async XLA Ops:
  1.3 131.9 %copy-start = (f32[128,4096]{1,0:T(8,128)S(1)}, f32[128,4096]{1,0:T(8,128)}, u32[]{:S(2)}) copy-start(f32[128,4096]{1,0:T(8,128)} %refs_3_.1) | copy-start | bytes 6291460
  1.3 131.9 %copy-start.1 = (f32[512,1024]{1,0:T(8,128)S(1)}, f32[512,1024]{1,0:T(8,128)}, u32[]{:S(2)}) copy-start(f32[512,1024]{1,0:T(8,128)} %refs_4_.1) | copy-start | bytes 6291460
  1.3 131.9 %copy-start.2 = (f32[128,3072]{1,0:T(8,128)S(1)}, f32[128,3072]{1,0:T(8,128)}, u32[]{:S(2)}) copy-start(f32[128,3072]{1,0:T(8,128)} %refs_1_.1) | copy-start | bytes 4718596
  1.3 131.9 %copy-start.3 = (f32[128,1024]{1,0:T(8,128)S(1)}, f32[128,1024]{1,0:T(8,128)}, u32[]{:S(2)}) copy-start(f32[128,1024]{1,0:T(8,128)} %refs_2_.1) | copy-start | bytes 1572868
  1.3 131.9 %copy-start.4 = (f32[1664]{0:T(1024)S(1)}, f32[1664]{0:T(1024)}, u32[]{:S(2)}) copy-start(f32[1664]{0:T(1024)} %param.26) | copy-start | bytes 19972
  133.2 0.7 copy-start.5

commit v9 on v8

--- a/solution.py
+++ b/solution.py
@@ -1599,7 +1599,8 @@
 def lamb_rows(first_old, second_old, master, grad):
     first_new = BETA_ONE * first_old + (1.0 - BETA_ONE) * grad
     second_new = BETA_TWO * second_old + (1.0 - BETA_TWO) * grad * grad
-    update = first_new / (jnp.sqrt(second_new) + ADAM_EPSILON) + DECAY * master
+    root = second_new * lax.rsqrt(second_new)
+    update = first_new / (root + ADAM_EPSILON) + DECAY * master
     return first_new, second_new, update
 
 
@@ -1689,7 +1690,7 @@
     return specs + [pl.BlockSpec(masters[4].shape, lambda i: (0, 0))]
 
 
-def moments(grads, masters, firsts, seconds, steps=8):
+def moments(grads, masters, firsts, seconds, steps=4):
     qkv_grad, out_grad, up_grad, down_grad, small_grad = grads
     shape = jax.ShapeDtypeStruct
     each = lamb_specs(masters, steps)
@@ -1712,7 +1713,7 @@
         in_specs=grad_specs + [VMEM_SPEC] * 5 + each * 2,
         out_specs=each * 2 + [VMEM_SPEC] * 5 + [pl.BlockSpec((16, 128), lambda i: (0, 0))],
         out_shape=out * 2 + near + [shape((16, 128), jnp.float32)],
-        compiler_params=pltpu.CompilerParams(vmem_limit_bytes=12 << 20),
+        compiler_params=pltpu.CompilerParams(vmem_limit_bytes=24 << 20),
         name="moments",
     )(*grads, *masters, *firsts, *seconds)
     return results[0:5], results[5:10], results[10:15], results[15]
@@ -1815,7 +1816,6 @@
     masters = placed(tall(masters), pltpu.VMEM)
     firsts, seconds = placed(tall(firsts), pltpu.HBM), placed(tall(seconds), pltpu.HBM)
     grads = placed(grads[:4], pltpu.HBM) + (grads[4],)
-    layer_outs = placed(layer_outs, pltpu.HBM)
     first_news, second_news, updates, squares = moments(grads, masters, firsts, seconds)
     news, outs, lamb_norms = step_masters(norms(squares), masters, updates, layer_outs)
     return (

time: 160 us -> 156 us (0.975)
  Pallas kernels: 158 us -> 153 us
    pallas_call x1, Pallas kernels: 14.5 us -> 11.5 us  [moments(): pl.pallas_call(moments_kernel, grid=(steps,), in_specs=grad_specs + [VMEM...]
where the time goes in v9:
time: 156 us
  Pallas kernels  153 us (98%)
    pallas_call x1, Pallas kernels, whole_layer(): pl.pallas_call(layer_kernel, out_shape=(shape(x_own.shape, bf16), shape(x...  132 us
    pallas_call x1, Pallas kernels, moments(): pl.pallas_call(moments_kernel, grid=(steps,), in_specs=grad_specs + [VMEM...  11.5 us
    pallas_call x1, Pallas kernels, norms(): pl.pallas_call(norms_kernel, out_shape=jax.ShapeDtypeStruct((16, 128), jn...  6.33 us
    pallas_call x1, Pallas kernels, step_masters(): pl.pallas_call(step_kernel, grid=(steps,), in_specs=[pl.BlockSpec((16, 12...  3.62 us

profile of v9, /device:TPU:0, one launch (start us, length us, event | category | flops | bytes accessed | tf_op | source)
XLA Modules:
  0.0 155.5 jit_solution(9973016582850840405)
XLA Ops:
  1.3 0.0 copy-start
  1.3 0.0 copy-start.1
  1.3 0.0 copy-start.2
  1.3 0.0 copy-start.3
  1.3 0.0 copy-start.6
  1.4 131.8 %layer.1 = (bf16[256,1024]{1,0:T(8,128)(2,1)}, bf16[256,1024]{1,0:T(8,128)(2,1)}, bf16[4,128,768]{2,1,0:T(8,128)(2,1)}, bf16[4,128,1024]{2,1,0:T(8,128)(2,1)}, b...) custom-call(s32[1]{0:T(128)S(6)} %copy.37.length_own, bf16[256,1024]{1,0:T(8,128)(2,1)} %bitcast.15, ...), custom_call_target="tpu_custom_call" | custom-call | tf_op jit(solution)/shard_map/layer/pallas_call | solution.py:1371
  133.2 0.0 copy-done
  133.2 0.0 copy-done.1
  133.2 0.0 copy-done.2
  133.2 0.0 copy-done.3
  133.2 0.0 copy-done.6
  133.2 0.0 copy-start.7
  133.2 0.7 copy-done.7
  133.9 0.0 copy-start.4
  133.9 0.0 copy-start.5
  133.9 11.5 %moments.1 = (f32[128,3072]{1,0:T(8,128)}, f32[128,1024]{1,0:T(8,128)}, f32[128,4096]{1,0:T(8,128)}, f32[512,1024]{1,0:T(8,128)}, f32[13,128]{1,0:T(8,128)}, /*i...) custom-call(bf16[4,128,768]{2,1,0:T(8,128)(2,1)} %get-tuple-element., ...), custom_call_target="tpu_custom_call" | custom-call | tf_op jit(solution)/shard_map/moments/pallas_call | solution.py:1710
  145.4 6.3 %norms.1.refs_0_ = f32[16,128]{1,0:T(8,128)S(1)} custom-call(f32[16,128]{1,0:T(8,128)S(1)} %get-tuple-element.54.squares), custom_call_target="tpu_custom_call" | custom-call | tf_op jit(solution)/shard_map/norms/pallas_call | solution.py:1747
  151.7 0.0 copy-done.4
  151.8 0.0 copy-done.5
  151.8 3.6 %step_masters.1 = (f32[128,3072]{1,0:T(8,128)}, f32[128,1024]{1,0:T(8,128)}, f32[128,4096]{1,0:T(8,128)}, f32[512,1024]{1,0:T(8,128)}, f32[13,128]{1,0:T(8,128)}...) custom-call(f32[16,128]{1,0:T(8,128)S(1)} %norms.1.refs_0_, f32[128,3072]{1,0:T(8,128)S(1)} %copy-done.2, ...), custom_call_target="tpu_custom_call" | custom-call | tf_op jit(solution)/shard_map/step_masters/pallas_call | solution.py:1790
Async XLA Ops:
  1.3 131.9 %copy-start = (f32[128,4096]{1,0:T(8,128)S(1)}, f32[128,4096]{1,0:T(8,128)}, u32[]{:S(2)}) copy-start(f32[128,4096]{1,0:T(8,128)} %refs_3_.1) | copy-start | bytes 6291460
  1.3 131.9 %copy-start.1 = (f32[512,1024]{1,0:T(8,128)S(1)}, f32[512,1024]{1,0:T(8,128)}, u32[]{:S(2)}) copy-start(f32[512,1024]{1,0:T(8,128)} %refs_4_.1) | copy-start | bytes 6291460
  1.3 131.9 %copy-start.2 = (f32[128,3072]{1,0:T(8,128)S(1)}, f32[128,3072]{1,0:T(8,128)}, u32[]{:S(2)}) copy-start(f32[128,3072]{1,0:T(8,128)} %refs_1_.1) | copy-start | bytes 4718596
  1.3 131.9 %copy-start.3 = (f32[128,1024]{1,0:T(8,128)S(1)}, f32[128,1024]{1,0:T(8,128)}, u32[]{:S(2)}) copy-start(f32[128,1024]{1,0:T(8,128)} %refs_2_.1) | copy-start | bytes 1572868
  1.3 131.9 %copy-start.6 = (f32[1664]{0:T(1024)S(1)}, f32[1664]{0:T(1024)}, u32[]{:S(2)}) copy-start(f32[1664]{0:T(1024)} %param.26) | copy-start | bytes 19972
  133.2 0.7 copy-start.7
  133.9 17.8 %copy-start.4 = (bf16[256,1024]{1,0:T(8,128)(2,1)S(1)}, bf16[256,1024]{1,0:T(8,128)(2,1)}, u32[]{:S(2)}) copy-start(bf16[256,1024]{1,0:T(8,128)(2,1)} %get-tuple-element.60.refs_11_) | copy-start | bytes 1572868
  133.9 17.8 %copy-start.5 = (bf16[256,1024]{1,0:T(8,128)(2,1)S(1)}, bf16[256,1024]{1,0:T(8,128)(2,1)}, u32[]{:S(2)}) copy-start(bf16[256,1024]{1,0:T(8,128)(2,1)} %get-tuple-element.61.refs_12_) | copy-start | bytes 1572868

commit v10 on v9

--- a/solution.py
+++ b/solution.py
@@ -255,7 +255,7 @@
     peers = [at.across_x, at.across_y, at.across_far] + [at.shard_after(k) for k in range(1, 8)]
     for peer in peers:
         pl.semaphore_signal(barrier, inc=1, device_id=peer, device_id_type=MESH_ID)
-    pl.semaphore_wait(barrier, len(peers))
+    return lambda: pl.semaphore_wait(barrier, len(peers))
 
 
 SPANS = ((0, 768), (768, 1792), (1792, 2816))
@@ -371,6 +371,7 @@
     f32, bf16 = jnp.float32, jnp.bfloat16
     at = Place()
     z, core, part, shard = at.z, at.core, at.part, at.shard
+    all_are_in = greet(at)
     length = x_own.shape[0]
     head_cols = mixed.shape[2]
     activated = normed_one
@@ -416,9 +417,10 @@
     small_own[...] = jnp.zeros_like(small_own)
     small_own[0:13] = small_master[...].astype(bf16).astype(f32)
     small_all[shard] = small_own[...]
-    greet(at)
+    all_are_in()
 
     halves = (slice(0, HALF), slice(HALF, 2 * HALF))
+    quarters = (slice(0, HALF // 2), slice(HALF // 2, HALF))
     activations = ((x_own, x_all), (cot_own, cot_all))
     neighbours = ((at.across_x, at.x_part), (at.across_y, at.y_part))
 
@@ -813,7 +815,13 @@
                 out_add(out_line_in[1])
 
             for r, (peer, _) in enumerate(neighbours):
-                send(out_line, out_grad, rows_send.at[2 + r], rows_recv.at[3], peer).start()
+                send(
+                    out_line.at[quarters[r]],
+                    out_grad.at[quarters[r]],
+                    rows_send.at[2 + r],
+                    rows_recv.at[3],
+                    peer,
+                ).start()
             pltpu.make_async_copy(out_line, out_grad, keep_sem.at[3]).start()
 
     def out_share():
@@ -821,10 +829,18 @@
 
             @pl.when(z == source)
             def _():
-                arrived(out_grad, rows_recv.at[3], peer)
-                block = out_grad.at[64 * r : 64 * r + 64]
+                block = out_grad.at[quarters[r]]
+                arrived(block, rows_recv.at[3], peer)
                 onward = neighbours[1 - r][0]
                 send(block, block, rows_send.at[4], rows_recv.at[4 + r], onward).start()
+
+    def out_far():
+        @pl.when(z == at.far_part)
+        def _():
+            for r, (peer, _) in enumerate(neighbours):
+                block = out_grad.at[quarters[r]]
+                arrived(block, rows_recv.at[4 + r], neighbours[1 - r][0])
+                send(block, block, rows_send.at[2 + r], rows_recv.at[4 + r], peer).start()
 
     def out_gradient():
         for n in range(2):
@@ -974,38 +990,39 @@
     send_out_rows()
     send_small()
 
-    @pl.when(at_end)
+    @pl.when(middle)
     def _():
         send_rest()
-
-    @pl.when(middle)
-    def _():
         forward(1, Q)
         forward_out(1)
         forward(2, Q)
+        forward_y(0)
 
     send_own(U)
-    forward_x(0)
 
     @pl.when(at_end)
     def _():
-        forward_out(1)
-
-    @pl.when(middle)
-    def _():
-        forward_out(2)
-        from_core(Q)
-        send_own(N)
-        send_rest()
-
-    forward_y(0)
-
-    @pl.when(at_end)
-    def _():
+        forward_y(0)
         forward(1, Q)
         forward(2, Q)
+
+    @pl.when(middle)
+    def _():
+        forward_out(2)
+        forward(1, U)
+
+    forward_x(0)
+
+    @pl.when(middle)
+    def _():
+        from_core(Q)
+
+    send_own(N)
+
+    @pl.when(at_end)
+    def _():
+        send_rest()
         forward(3, Q)
-        send_own(N)
         from_core(Q)
 
     unpack_small()
@@ -1016,52 +1033,61 @@
 
         @pl.when((i == 0) & at_end)
         def _():
-            forward_y(1)
+            forward_out(1)
+            far_halves(0)
+
+        @pl.when((i == 1) & at_end)
+        def _():
             forward_out(2)
 
-        @pl.when(i == 2)
-        def _():
+        @pl.when((i == 2) & at_end)
+        def _():
+            forward_out(3)
+
+        @pl.when((i == 2) & middle)
+        def _():
+            far_halves(0)
             forward_x(1)
-
-        @pl.when((i == 2) & at_end)
-        def _():
-            forward_out(3)
-
-        @pl.when((i == 2) & middle)
-        def _():
-            forward(1, U)
-            forward_y(1)
-
-        @pl.when(i == 2)
-        def _():
-            far_halves(0)
-
-        @pl.when((i == 2) & middle)
-        def _():
-            forward(1, N)
-
-    out_from_core()
+            forward(2, U)
+            out_from_core()
+
+    @pl.when(at_end)
+    def _():
+        out_from_core()
+
+    forward_y(1)
+
+    @pl.when(at_end)
+    def _():
+        forward_x(1)
+
+    @pl.when(middle)
+    def _():
+        forward(1, N)
 
     @pl.loop(0, 4)
     def _(i):
         attend(near_first(i))
 
-        @pl.when((i == 0) & middle)
-        def _():
-            forward(2, U)
-
-        @pl.when((i == 1) & middle)
+        @pl.when((i == 2) & middle)
+        def _():
+            forward(2, N)
+
+        @pl.when(i == 2)
         def _():
             far_halves(1)
 
         @pl.when((i == 2) & at_end)
         def _():
             forward(1, U)
-            far_halves(1)
-
-        @pl.when((i == 2) & middle)
-        def _():
-            forward(2, N)
+
+    @pl.when(at_end)
+    def _():
+        forward(2, U)
+
+    @pl.when(middle)
+    def _():
+        from_core(N)
 
     gradient(normed_one, d_projected, Q)
 
@@ -1072,64 +1098,67 @@
     @pl.when(middle)
     def _():
         from_core(U)
-        from_core(N)
 
     out_gradient()
 
     @pl.when(at_end)
     def _():
-        forward(2, U)
         forward(3, U)
+        add_core(Q)
+        out_to_core()
+        line_starts(Q)
         forward(1, N)
-        add_core(Q)
-        line_starts(Q)
         from_core(U)
+
+    @pl.when(middle)
+    def _():
+        to_core(Q)
 
     @pl.loop(0, 4)
     def _(i):
         feed_in(i)
 
-        @pl.when((i == 0) & at_end)
+        @pl.when((i == 2) & at_end)
         def _():
             forward(2, N)
 
-        @pl.when((i == 0) & middle)
-        def _():
-            to_core(Q)
-
     @pl.when(at_end)
     def _():
+        out_add_core()
+
+    gradient(activated, back, N)
+
+    @pl.when(at_end)
+    def _():
+        out_step(0)
         forward(3, N)
-
-    gradient(activated, back, N)
-
-    @pl.when(at_end)
-    def _():
-        out_to_core()
         from_core(N)
 
     @pl.loop(0, 4)
     def _(i):
         feed_out(far_first(i))
 
-        @pl.when((i == 0) & middle)
-        def _():
-            add_core(Q)
-
         @pl.when(i == 0)
         def _():
             send_part(0, 0, 0)
             send_part(0, 1, 0)
 
+        @pl.when((i == 0) & at_end)
+        def _():
+            to_core(N)
+
         @pl.when((i == 1) & at_end)
         def _():
-            out_add_core()
-            out_step(0)
-            to_core(N)
-
-        @pl.when((i == 2) & middle)
+            send_part(0, 0, 1)
+            add_core(N)
+
+        @pl.when((i == 2) & at_end)
         def _():
             send_part(0, 1, 1)
+
+    @pl.when(middle)
+    def _():
+        out_to_core()
 
     @pl.loop(0, 4)
     def _(i):
@@ -1137,163 +1166,164 @@
 
         @pl.when((i == 0) & middle)
         def _():
-            out_to_core()
+            send_part(0, 1, 1)
+            add_core(Q)
+
+        @pl.when((i == 1) & middle)
+        def _():
             out_add_core()
-            line_step(Q, 0)
-            line_step(Q, 1)
-            send_part(0, 0, 1)
-            to_core(N)
-
-        @pl.when((i == 1) & at_end)
-        def _():
-            send_part(0, 1, 1)
-            add_core(N)
-            line_starts(N)
-            turn_part(0, 0)
-
-        @pl.when((i == 2) & at_end)
-        def _():
-            send_part(1, 0, 1)
-
-        @pl.when((i == 2) & middle)
-        def _():
-            out_step(1)
-
-        @pl.when((i == 3) & at_end)
-        def _():
-            send_part(0, 0, 1)
-
-        @pl.when((i == 3) & middle)
-        def _():
-            line_step(Q, 2)
-            send_part(1, 1, 1)
-
-        norm_back(far_first(i))
-
-        @pl.when((i == 0) & at_end)
+
+        @pl.when(i == 2)
         def _():
             send_part(1, 0, 0)
             send_part(1, 1, 0)
 
+        @pl.when((i == 2) & middle)
+        def _():
+            turn_part(0, 0)
+            turn_part(0, 1)
+            line_step(Q, 1)
+            out_step(1)
+            add_core(N)
+
+        @pl.when((i == 3) & middle)
+        def _():
+            send_part(1, 1, 1)
+            line_step(N, 0)
+
+        norm_back(far_first(i))
+
+        @pl.when((i == 0) & at_end)
+        def _():
+            line_starts(N)
+
         @pl.when((i == 0) & middle)
         def _():
-            add_core(N)
+            send_part(0, 0, 1)
+            line_step(Q, 0)
 
         @pl.when((i == 1) & middle)
         def _():
-            send_part(1, 0, 0)
-            send_part(1, 1, 0)
-            turn_part(0, 1)
+            to_core(N)
+
+        @pl.when((i == 2) & at_end)
+        def _():
+            turn_part(0, 0)
+            send_part(1, 1, 1)
+
+        @pl.when((i == 2) & middle)
+        def _():
+            line_step(Q, 2)
+
+    @pl.when(at_end)
+    def _():
+        turn_part(0, 1)
 
     @pl.when(middle)
     def _():
-        turn_part(0, 0)
-        line_ends(Q)
+        send_part(1, 0, 1)
 
     gradient(normed_two, d_hidden, U)
 
+    @pl.when(at_end)
+    def _():
+        send_part(1, 0, 1)
+
     @pl.when(middle)
     def _():
-        to_core(U)
-        send_part(1, 0, 1)
-        line_step(N, 0)
-
-    turn_part(1, 1)
+        small_start()
+
+    to_core(U)
 
     @pl.when(at_end)
     def _():
-        to_core(U)
-        send_part(1, 1, 1)
+        small_start()
+
+    line_ends(Q)
 
     @pl.when(middle)
     def _():
-        turn_part(1, 0)
+        line_step(N, 1)
+        line_step(N, 2)
 
     add_core(U)
 
+    @pl.when(middle)
+    def _():
+        out_step(2)
+        out_ends()
+        line_ends(N)
+        turn_part(1, 1)
+        line_step(U, 0)
+        small_turn()
+        out_share()
+
+    turn_part(1, 0)
+
     @pl.when(at_end)
     def _():
         line_starts(U)
-        line_ends(Q)
-        turn_part(1, 0)
-
-    @pl.when(middle)
-    def _():
-        line_step(N, 1)
-        out_step(2)
-
-    small_start()
-
-    @pl.when(middle)
-    def _():
-        write_output(1)
-        line_step(N, 2)
-        line_step(U, 0)
-        write_output(0)
+        turn_part(1, 1)
         line_ends(N)
-        share(Q)
-
-    out_ends()
-
-    @pl.when(at_end)
-    def _():
-        turn_part(0, 1)
-        write_output(0)
-        share(Q)
-        line_ends(N)
+        out_ends()
+
+    share(Q)
 
     @pl.when(middle)
     def _():
         line_step(U, 1)
         line_step(U, 2)
+        write_input_grad(1)
+        line_ends(U)
+        write_output(0)
         share(N)
-        write_input_grad(0)
+
+    write_output(1)
+
+    @pl.when(at_end)
+    def _():
+        write_output(0)
+        out_share()
+        write_input_grad(1)
+        share(N)
         line_ends(U)
-        out_share()
-
-    small_turn()
-
-    @pl.when(at_end)
-    def _():
-        out_share()
-        line_ends(U)
 
     @pl.when(middle)
     def _():
-        share(U)
-
-    write_input_grad(1)
-    small_end()
-
-    @pl.when(at_end)
-    def _():
-        write_output(1)
-        share(N)
         share(U)
         write_input_grad(0)
 
+    out_far()
+
+    @pl.when(at_end)
+    def _():
+        small_turn()
+        write_input_grad(0)
+        share(U)
+
+    small_end()
     for r, half in enumerate(halves):
         pltpu.make_async_copy(output.at[half], output_out.at[half], store_sem.at[0, r]).wait()
         pltpu.make_async_copy(
             input_grad.at[half], input_grad_out.at[half], store_sem.at[1, r]
         ).wait()
-    @pl.when(z == at.far_part)
-    def _():
-        for r, (peer, _) in enumerate(neighbours):
-            arrived(out_grad.at[64 * r : 64 * r + 64], rows_recv.at[4 + r], neighbours[1 - r][0])
+    for r, (peer, source) in enumerate(neighbours):
+
+        @pl.when(z == source)
+        def _():
+            arrived(out_grad.at[quarters[1 - r]], rows_recv.at[5 - r], neighbours[1 - r][0])
+            sent(out_grad.at[quarters[r]], rows_send.at[4], neighbours[1 - r][0])
+
+        @pl.when((z == part) | (z == at.far_part))
+        def _():
+            sent(out_grad.at[quarters[r]], rows_send.at[2 + r], peer)
 
     @pl.when(z != part)
     def _():
         sent(out_line, rows_send.at[1], at.up)
 
-    @pl.when((z == at.x_part) | (z == at.y_part))
-    def _():
-        sent(out_line.at[0:64], rows_send.at[4], at.across_x)
-
     @pl.when(z == part)
     def _():
-        for r, (peer, _) in enumerate(neighbours):
-            sent(out_line, rows_send.at[2 + r], peer)
         pltpu.make_async_copy(out_line, out_grad, keep_sem.at[3]).wait()
 
     sent(out_line, rows_send.at[0], at.other_core)
@@ -1815,7 +1845,7 @@
 
     masters = placed(tall(masters), pltpu.VMEM)
     firsts, seconds = placed(tall(firsts), pltpu.HBM), placed(tall(seconds), pltpu.HBM)
-    grads = placed(grads[:4], pltpu.HBM) + (grads[4],)
+    grads = placed(grads, pltpu.HBM)
     first_news, second_news, updates, squares = moments(grads, masters, firsts, seconds)
     news, outs, lamb_norms = step_masters(norms(squares), masters, updates, layer_outs)
     return (

time: 156 us -> 155 us (level)
  no operation moved by 1% of the time
where the time goes in v10:
time: 155 us
  Pallas kernels  153 us (99%)
  between operations  1.55 us (1%)
    pallas_call x1, Pallas kernels, whole_layer(): pl.pallas_call(layer_kernel, out_shape=(shape(x_own.shape, bf16), shape(x...  130 us
    pallas_call x1, Pallas kernels, moments(): pl.pallas_call(moments_kernel, grid=(steps,), in_specs=grad_specs + [VMEM...  11.6 us
    pallas_call x1, Pallas kernels, norms(): pl.pallas_call(norms_kernel, out_shape=jax.ShapeDtypeStruct((16, 128), jn...  7.88 us
    pallas_call x1, Pallas kernels, step_masters(): pl.pallas_call(step_kernel, grid=(steps,), in_specs=[pl.BlockSpec((16, 12...  3.63 us

profile of v10, /device:TPU:0, one launch (start us, length us, event | category | flops | bytes accessed | tf_op | source)
XLA Modules:
  0.0 155.0 jit_solution(7985021393634163448)
XLA Ops:
  1.3 0.0 copy-start
  1.3 0.0 copy-start.1
  1.3 0.0 copy-start.2
  1.3 0.0 copy-start.3
  1.3 0.0 copy-start.6
  1.4 130.3 %layer.1 = (bf16[256,1024]{1,0:T(8,128)(2,1)}, bf16[256,1024]{1,0:T(8,128)(2,1)}, bf16[4,128,768]{2,1,0:T(8,128)(2,1)}, bf16[4,128,1024]{2,1,0:T(8,128)(2,1)}, b...) custom-call(s32[1]{0:T(128)S(6)} %copy.37.length_own, bf16[256,1024]{1,0:T(8,128)(2,1)} %bitcast.14, ...), custom_call_target="tpu_custom_call" | custom-call | tf_op jit(solution)/shard_map/layer/pallas_call | solution.py:1401
  131.6 0.0 copy-done
  131.7 0.0 copy-done.1
  131.7 0.0 copy-done.2
  131.7 0.0 copy-done.3
  131.7 0.0 copy-done.6
  131.7 0.0 copy-start.4
  131.7 0.0 copy-start.5
  131.7 11.6 %moments.1 = (f32[128,3072]{1,0:T(8,128)}, f32[128,1024]{1,0:T(8,128)}, f32[128,4096]{1,0:T(8,128)}, f32[512,1024]{1,0:T(8,128)}, f32[13,128]{1,0:T(8,128)}, /*i...) custom-call(bf16[4,128,768]{2,1,0:T(8,128)(2,1)} %get-tuple-element., ...), custom_call_target="tpu_custom_call" | custom-call | tf_op jit(solution)/shard_map/moments/pallas_call | solution.py:1740
  143.3 7.9 %norms.1.refs_0_ = f32[16,128]{1,0:T(8,128)S(1)} custom-call(f32[16,128]{1,0:T(8,128)S(1)} %get-tuple-element.54.squares), custom_call_target="tpu_custom_call" | custom-call | tf_op jit(solution)/shard_map/norms/pallas_call | solution.py:1777
  151.2 0.0 copy-done.4
  151.2 0.0 copy-done.5
  151.2 3.6 %step_masters.1 = (f32[128,3072]{1,0:T(8,128)}, f32[128,1024]{1,0:T(8,128)}, f32[128,4096]{1,0:T(8,128)}, f32[512,1024]{1,0:T(8,128)}, f32[13,128]{1,0:T(8,128)}...) custom-call(f32[16,128]{1,0:T(8,128)S(1)} %norms.1.refs_0_, f32[128,3072]{1,0:T(8,128)S(1)} %copy-done.2, ...), custom_call_target="tpu_custom_call" | custom-call | tf_op jit(solution)/shard_map/step_masters/pallas_call | solution.py:1820
Async XLA Ops:
  1.3 130.3 %copy-start = (f32[128,4096]{1,0:T(8,128)S(1)}, f32[128,4096]{1,0:T(8,128)}, u32[]{:S(2)}) copy-start(f32[128,4096]{1,0:T(8,128)} %refs_3_.1) | copy-start | bytes 6291460
  1.3 130.3 %copy-start.1 = (f32[512,1024]{1,0:T(8,128)S(1)}, f32[512,1024]{1,0:T(8,128)}, u32[]{:S(2)}) copy-start(f32[512,1024]{1,0:T(8,128)} %refs_4_.1) | copy-start | bytes 6291460
  1.3 130.3 %copy-start.2 = (f32[128,3072]{1,0:T(8,128)S(1)}, f32[128,3072]{1,0:T(8,128)}, u32[]{:S(2)}) copy-start(f32[128,3072]{1,0:T(8,128)} %refs_1_.1) | copy-start | bytes 4718596
  1.3 130.3 %copy-start.3 = (f32[128,1024]{1,0:T(8,128)S(1)}, f32[128,1024]{1,0:T(8,128)}, u32[]{:S(2)}) copy-start(f32[128,1024]{1,0:T(8,128)} %refs_2_.1) | copy-start | bytes 1572868
  1.3 130.3 %copy-start.6 = (f32[1664]{0:T(1024)S(1)}, f32[1664]{0:T(1024)}, u32[]{:S(2)}) copy-start(f32[1664]{0:T(1024)} %param.26) | copy-start | bytes 19972
  131.7 19.5 %copy-start.4 = (bf16[256,1024]{1,0:T(8,128)(2,1)S(1)}, bf16[256,1024]{1,0:T(8,128)(2,1)}, u32[]{:S(2)}) copy-start(bf16[256,1024]{1,0:T(8,128)(2,1)} %get-tuple-element.60.refs_11_) | copy-start | bytes 1572868
  131.7 19.5 %copy-start.5 = (bf16[256,1024]{1,0:T(8,128)(2,1)S(1)}, bf16[256,1024]{1,0:T(8,128)(2,1)}, u32[]{:S(2)}) copy-start(bf16[256,1024]{1,0:T(8,128)(2,1)} %get-tuple-element.61.refs_12_) | copy-start | bytes 1572868

commit v11 on v10

--- a/solution.py
+++ b/solution.py
@@ -300,8 +300,6 @@
     out_grad,
     small_sum,
     tables,
-    output,
-    input_grad,
     x_all,
     cot_all,
     len_all,
@@ -331,7 +329,6 @@
     small_part,
     plane_one,
     plane_two,
-    plane_turn,
     core_in,
     line_in,
     out_core_in,
@@ -867,11 +864,11 @@
     def turn_part(n, r):
         half, peer, _, turn, turned = routes[r]
         arrived(plane_one.at[n, r, 0], part_recv.at[n, r, 0], peer)
-        plane_turn[n, r] = (
+        part_refs[n][turned, half] = (
             part_refs[n][turned, half].astype(f32) + plane_one[n, r, 0].astype(f32)
         ).astype(bf16)
         send(
-            plane_turn.at[n, r],
+            part_refs[n].at[turned, half],
             plane_two.at[n, r],
             part_send.at[n, r, 2],
             part_recv.at[n, r, 2],
@@ -965,6 +962,7 @@
         half = halves[r]
         values = x_all[part, half].astype(f32)
         summed = values + whole_part(0, r) + vectors[4:5] + vectors[5:6]
+        output = out_part.at[part]
         output[half] = jnp.where(live_rows(part)[half], summed, 0.0).astype(bf16)
         pltpu.make_async_copy(output.at[half], output_out.at[half], store_sem.at[0, r]).start()
 
@@ -978,6 +976,7 @@
             - jnp.mean(scaled, axis=-1, keepdims=True)
             - unit * jnp.mean(scaled * unit, axis=-1, keepdims=True)
         )
+        input_grad = dx_part.at[part]
         input_grad[half] = result.astype(bf16)
         pltpu.make_async_copy(
             input_grad.at[half], input_grad_out.at[half], store_sem.at[1, r]
@@ -1302,6 +1301,7 @@
         share(U)
 
     small_end()
+    output, input_grad = out_part.at[part], dx_part.at[part]
     for r, half in enumerate(halves):
         pltpu.make_async_copy(output.at[half], output_out.at[half], store_sem.at[0, r]).wait()
         pltpu.make_async_copy(
@@ -1371,7 +1371,7 @@
     for n in range(2):
         for r in range(2):
             for m in range(3):
-                sent(plane_turn.at[n, r], part_send.at[n, r, m], at.across_x)
+                sent(plane_two.at[n, r], part_send.at[n, r, m], at.across_x)
     for n, whole in enumerate(wholes):
         arrived(whole.at[at.far_part, 0:64], all_recv.at[n, 2], at.across_y)
         arrived(whole.at[at.far_part, 64:128], all_recv.at[n, 3], at.across_x)
@@ -1415,8 +1415,6 @@
         out_specs=(HBM_SPEC,) * 6 + (VMEM_SPEC,),
         scratch_shapes=[
             vmem(tables.shape, f32),
-            vmem(x_own.shape, bf16),
-            vmem(x_own.shape, bf16),
             by_sequence(D),
             by_sequence(D),
             vmem((group, 8, 128), f32),
@@ -1445,7 +1443,6 @@
             vmem((1, FF // group), f32),
             vmem((8, 16, 128), f32),
             vmem((2, 2, 2, HALF, D), bf16),
-            vmem((2, 2, HALF, D), bf16),
             vmem((2, 2, HALF, D), bf16),
             vmem((4, rows, wide), bf16),
             vmem((5, rows, wide), bf16),
@@ -1484,7 +1481,7 @@
             dma((2, 2)),
         ],
         compiler_params=pltpu.CompilerParams(
-            collective_id=0, has_side_effects=True, vmem_limit_bytes=56 << 20
+            collective_id=0, has_side_effects=True, vmem_limit_bytes=54 << 20
         ),
         name="layer",
     )(lengths, x_own, cot_own, *masters, tables)
@@ -1844,7 +1841,9 @@
         return tuple(pltpu.with_memory_space_constraint(a, space) for a in arrays)
 
     masters = placed(tall(masters), pltpu.VMEM)
-    firsts, seconds = placed(tall(firsts), pltpu.HBM), placed(tall(seconds), pltpu.HBM)
+    firsts, seconds = tall(firsts), tall(seconds)
+    firsts = placed(firsts[:1], pltpu.VMEM) + placed(firsts[1:], pltpu.HBM)
+    seconds = placed(seconds, pltpu.HBM)
     grads = placed(grads, pltpu.HBM)
     first_news, second_news, updates, squares = moments(grads, masters, firsts, seconds)
     news, outs, lamb_norms = step_masters(norms(squares), masters, updates, layer_outs)

time: 155 us -> 155 us (level)
  no operation moved by 1% of the time
where the time goes in v11:
time: 155 us
  Pallas kernels  153 us (99%)
  between operations  1.57 us (1%)
    pallas_call x1, Pallas kernels, whole_layer(): pl.pallas_call(layer_kernel, out_shape=(shape(x_own.shape, bf16), shape(x...  130 us
    pallas_call x1, Pallas kernels, moments(): pl.pallas_call(moments_kernel, grid=(steps,), in_specs=grad_specs + [VMEM...  11.3 us
    pallas_call x1, Pallas kernels, norms(): pl.pallas_call(norms_kernel, out_shape=jax.ShapeDtypeStruct((16, 128), jn...  7.9 us
    pallas_call x1, Pallas kernels, step_masters(): pl.pallas_call(step_kernel, grid=(steps,), in_specs=[pl.BlockSpec((16, 12...  3.63 us

profile of v11, /device:TPU:0, one launch (start us, length us, event | category | flops | bytes accessed | tf_op | source)
XLA Modules:
  0.0 154.7 jit_solution(7397476788724659605)
XLA Ops:
  1.3 0.0 copy-start
  1.3 0.0 copy-start.1
  1.3 0.0 copy-start.2
  1.3 0.0 copy-start.3
  1.3 0.0 copy-start.4
  1.4 0.0 copy-start.7
  1.4 130.3 %layer.1 = (bf16[256,1024]{1,0:T(8,128)(2,1)}, bf16[256,1024]{1,0:T(8,128)(2,1)}, bf16[4,128,768]{2,1,0:T(8,128)(2,1)}, bf16[4,128,1024]{2,1,0:T(8,128)(2,1)}, b...) custom-call(s32[1]{0:T(128)S(6)} %copy.37.length_own, bf16[256,1024]{1,0:T(8,128)(2,1)} %bitcast.14, ...), custom_call_target="tpu_custom_call" | custom-call | tf_op jit(solution)/shard_map/layer/pallas_call | solution.py:1401
  131.6 0.0 copy-done
  131.6 0.0 copy-done.1
  131.7 0.0 copy-done.2
  131.7 0.0 copy-done.3
  131.7 0.0 copy-done.4
  131.7 0.0 copy-done.7
  131.7 0.0 copy-start.5
  131.7 0.0 copy-start.6
  131.7 11.3 %moments.1 = (f32[128,3072]{1,0:T(8,128)}, f32[128,1024]{1,0:T(8,128)}, f32[128,4096]{1,0:T(8,128)}, f32[512,1024]{1,0:T(8,128)}, f32[13,128]{1,0:T(8,128)}, /*i...) custom-call(bf16[4,128,768]{2,1,0:T(8,128)(2,1)} %get-tuple-element., ...), custom_call_target="tpu_custom_call" | custom-call | tf_op jit(solution)/shard_map/moments/pallas_call | solution.py:1737
  143.0 7.9 %norms.1.refs_0_ = f32[16,128]{1,0:T(8,128)S(1)} custom-call(f32[16,128]{1,0:T(8,128)S(1)} %get-tuple-element.54.squares), custom_call_target="tpu_custom_call" | custom-call | tf_op jit(solution)/shard_map/norms/pallas_call | solution.py:1774
  150.9 0.0 copy-done.5
  150.9 0.0 copy-done.6
  150.9 3.6 %step_masters.1 = (f32[128,3072]{1,0:T(8,128)}, f32[128,1024]{1,0:T(8,128)}, f32[128,4096]{1,0:T(8,128)}, f32[512,1024]{1,0:T(8,128)}, f32[13,128]{1,0:T(8,128)}...) custom-call(f32[16,128]{1,0:T(8,128)S(1)} %norms.1.refs_0_, f32[128,3072]{1,0:T(8,128)S(1)} %copy-done.2, ...), custom_call_target="tpu_custom_call" | custom-call | tf_op jit(solution)/shard_map/step_masters/pallas_call | solution.py:1817
Async XLA Ops:
  1.3 130.3 %copy-start = (f32[128,4096]{1,0:T(8,128)S(1)}, f32[128,4096]{1,0:T(8,128)}, u32[]{:S(2)}) copy-start(f32[128,4096]{1,0:T(8,128)} %refs_3_.1) | copy-start | bytes 6291460
  1.3 130.3 %copy-start.1 = (f32[512,1024]{1,0:T(8,128)S(1)}, f32[512,1024]{1,0:T(8,128)}, u32[]{:S(2)}) copy-start(f32[512,1024]{1,0:T(8,128)} %refs_4_.1) | copy-start | bytes 6291460
  1.3 130.3 %copy-start.2 = (f32[128,3072]{1,0:T(8,128)S(1)}, f32[128,3072]{1,0:T(8,128)}, u32[]{:S(2)}) copy-start(f32[128,3072]{1,0:T(8,128)} %refs_1_.1) | copy-start | bytes 4718596
  1.3 130.3 %copy-start.3 = (f32[128,1024]{1,0:T(8,128)S(1)}, f32[128,1024]{1,0:T(8,128)}, u32[]{:S(2)}) copy-start(f32[128,1024]{1,0:T(8,128)} %refs_2_.1) | copy-start | bytes 1572868
  1.3 130.3 %copy-start.4 = (f32[128,3072]{1,0:T(8,128)S(1)}, f32[128,3072]{1,0:T(8,128)}, u32[]{:S(2)}) copy-start(f32[128,3072]{1,0:T(8,128)} %refs_10_.1) | copy-start | bytes 4718596
  1.4 130.3 %copy-start.7 = (f32[1664]{0:T(1024)S(1)}, f32[1664]{0:T(1024)}, u32[]{:S(2)}) copy-start(f32[1664]{0:T(1024)} %param.26) | copy-start | bytes 19972
  131.7 19.2 %copy-start.5 = (bf16[256,1024]{1,0:T(8,128)(2,1)S(1)}, bf16[256,1024]{1,0:T(8,128)(2,1)}, u32[]{:S(2)}) copy-start(bf16[256,1024]{1,0:T(8,128)(2,1)} %get-tuple-element.60.refs_11_) | copy-start | bytes 1572868
  131.7 19.2 %copy-start.6 = (bf16[256,1024]{1,0:T(8,128)(2,1)S(1)}, bf16[256,1024]{1,0:T(8,128)(2,1)}, u32[]{:S(2)}) copy-start(bf16[256,1024]{1,0:T(8,128)(2,1)} %get-tuple-element.61.refs_12_) | copy-start | bytes 1572868
